TPU v7x, 32 devices: a whole 2x2x4 slice. The times are simulated.
32 devices in a mesh: dp: 8 (over y, x, core), mp: 4 (over z).
Axes of the slice: x: 2, y: 2, z: 4, core: 2. Of those that a mesh axis runs over, the one named last changes fastest.
Arguments:
- layer_in: bfloat16 [8, 1024, 1472], P('dp', 'mp'), may hold values from -6 to 6
- segment_ids: int32 [8, 1024], P('dp'), may hold values from 0 to 7, never falling along the last dimension, each value on 1 to 512 neighbouring positions
- bucket_table: int32 [2047], replicated, may hold values from 0 to 31
- attn_gain: float32 [1472], replicated, may hold values from 0.25 to 1.75
- query_weight: float32 [1472, 512], P(None, 'mp'), may hold values from -0.01953125 to 0.01953125
- key_weight: float32 [1472, 512], P(None, 'mp'), may hold values from -0.15625 to 0.15625
- value_weight: float32 [1472, 512], P(None, 'mp'), may hold values from -0.15625 to 0.15625
- out_weight: float32 [512, 1472], P('mp'), may hold values from -1 to 1
- rel_bias: float32 [32, 8], P(None, 'mp'), may hold values from -4 to 4
- ff_gain: float32 [1472], replicated, may hold values from 0.25 to 1.75
- gate_weight: float32 [1472, 3584], P(None, 'mp'), may hold values from -0.15625 to 0.15625
- up_weight: float32 [1472, 3584], P(None, 'mp'), may hold values from -0.15625 to 0.15625
- down_weight: float32 [3584, 1472], P('mp'), may hold values from -0.09375 to 0.09375
- cotangent: bfloat16 [8, 1024, 1472], P('dp', 'mp'), may hold values from -6 to 6
Outputs:
- layer_out: bfloat16 [8, 1024, 1472], P('dp', 'mp')
- input_grad: bfloat16 [8, 1024, 1472], P('dp', 'mp')
- new_attn_gain: float32 [1472], replicated
- attn_gain_moment: float32 [1472], replicated
- new_query_weight: float32 [1472, 512], P(None, 'mp')
- query_row_moment: float32 [1472], replicated
- query_col_moment: float32 [512], P('mp')
- new_key_weight: float32 [1472, 512], P(None, 'mp')
- key_row_moment: float32 [1472], replicated
- key_col_moment: float32 [512], P('mp')
- new_value_weight: float32 [1472, 512], P(None, 'mp')
- value_row_moment: float32 [1472], replicated
- value_col_moment: float32 [512], P('mp')
- new_out_weight: float32 [512, 1472], P('mp')
- out_row_moment: float32 [512], P('mp')
- out_col_moment: float32 [1472], replicated
- new_rel_bias: float32 [32, 8], P(None, 'mp')
- rel_row_moment: float32 [32], replicated
- rel_col_moment: float32 [8], P('mp')
- new_ff_gain: float32 [1472], replicated
- ff_gain_moment: float32 [1472], replicated
- new_gate_weight: float32 [1472, 3584], P(None, 'mp')
- gate_row_moment: float32 [1472], replicated
- gate_col_moment: float32 [3584], P('mp')
- new_up_weight: float32 [1472, 3584], P(None, 'mp')
- up_row_moment: float32 [1472], replicated
- up_col_moment: float32 [3584], P('mp')
- new_down_weight: float32 [3584, 1472], P('mp')
- down_row_moment: float32 [3584], P('mp')
- down_col_moment: float32 [1472], replicated
Inputs may be any that keep to these rules, and one draw needn't show every extreme that they name: `segment_ids`: along each row the numbers never fall; a document holds 1 to 512 bytes.
All inputs are finite; a program needn't handle non-finite values.
Results may differ from a plain program's by a relative error of at most 0.029.
Values may be sent and summed in bfloat16 or wider, within the bound.
A program may use at most 256 MiB of HBM per device.

v0:
```python
import jax
import jax.numpy as jnp
from jax import lax
from jax.sharding import PartitionSpec as P

HD = 64
BUCKETS = 32


highest = lax.Precision.HIGHEST
step_scale = 0.3


def rms_norm(values, gain):
    return values * lax.rsqrt(jnp.mean(values * values, axis=-1, keepdims=True) + 1e-06) * gain


def gated_gelu(gate_act, up_act):
    return jax.nn.gelu(gate_act, approximate=True) * up_act


def product(left_side, right_side):
    return jnp.dot(left_side, right_side, preferred_element_type=jnp.float32)


def left_inner(left_side, right_side):
    return lax.dot_general(
        left_side, right_side, (((0,), (0,)), ((), ())), preferred_element_type=jnp.float32
    )


def right_inner(left_side, right_side):
    return lax.dot_general(
        left_side, right_side, (((1,), (1,)), ((), ())), preferred_element_type=jnp.float32
    )


def toeplitz(vector, seq_len):
    slot_count = vector.shape[0]
    span = vector.shape[1]
    rolled = jnp.concatenate([vector[:, seq_len - 1 :], vector[:, : seq_len - 1]], axis=1)
    tiled = jnp.tile(rolled, (1, seq_len))[:, : seq_len * (span - 1)]
    return tiled.reshape(slot_count, seq_len, span - 1)[:, :, :seq_len]


def diagonal_sums(matrix):
    slot_count = matrix.shape[0]
    seq_len = matrix.shape[1]
    padded = jnp.pad(matrix, ((0, 0), (0, 0), (seq_len - 1, seq_len)))
    span = 3 * seq_len - 1
    flat = jnp.pad(padded.reshape(slot_count, seq_len * span), ((0, 0), (0, seq_len)))
    skewed = flat.reshape(slot_count, seq_len, span + 1)
    return jnp.sum(skewed[:, :, : 2 * seq_len - 1], axis=1)


def take_piece(source, split_dim, block_index, block_count):
    length = source.shape[split_dim] // block_count
    return lax.dynamic_slice_in_dim(source, block_index * length, length, split_dim)


def place_block(part_sums, block_index, block_count):
    length = part_sums.shape[0]
    full_vector = jnp.zeros((length * block_count,), jnp.float32)
    return lax.dynamic_update_slice_in_dim(full_vector, part_sums, block_index * length, 0)


def local(
    layer_in,
    segment_ids,
    bucket_table,
    attn_gain,
    query_weight,
    key_weight,
    value_weight,
    out_weight,
    rel_bias,
    ff_gain,
    gate_weight,
    up_weight,
    down_weight,
    cotangent,
):
    batch_rows, local_len, model_width = layer_in.shape
    seq_len = segment_ids.shape[1]
    lane_width = query_weight.shape[1]
    slots_here = lane_width // HD
    ff_width = gate_weight.shape[1]
    tensor_index = lax.axis_index("mp")
    tensor_count = lax.axis_size("mp")
    data_index = lax.axis_index("dp")
    data_count = lax.axis_size("dp")
    slot_ids = tensor_index * slots_here + jnp.arange(slots_here)
    slot_valid = ((slot_ids < 5) | (slot_ids == 6)).astype(jnp.float32)
    lane_mask = jnp.repeat(slot_valid, HD)
    qkv_low = (
        jnp.concatenate([query_weight, key_weight, value_weight], axis=1) * jnp.tile(lane_mask, 3)
    ).astype(jnp.bfloat16)
    proj_low = (out_weight * lane_mask[:, None]).astype(jnp.bfloat16)
    gate_up_low = jnp.concatenate([gate_weight, up_weight], axis=1).astype(jnp.bfloat16)
    down_low = down_weight.astype(jnp.bfloat16)
    onehot = (bucket_table[:, None] == jnp.arange(BUCKETS)[None, :]).astype(jnp.float32)
    vector = lax.dot_general(
        rel_bias,
        onehot,
        (((0,), (1,)), ((), ())),
        precision=highest,
        preferred_element_type=jnp.float32,
    )
    bias_table = toeplitz(vector, seq_len)
    residual_in = layer_in.astype(jnp.float32)
    normed_local = rms_norm(residual_in, attn_gain).astype(jnp.bfloat16)
    normed = lax.all_gather(normed_local, "mp", axis=1, tiled=True)
    flat_norm = normed.reshape(batch_rows * seq_len, model_width)
    qkv_rows = (
        product(flat_norm, qkv_low)
        .astype(jnp.bfloat16)
        .reshape(batch_rows, seq_len, 3, slots_here, HD)
    )
    queries = qkv_rows[:, :, 0]
    key_rows = qkv_rows[:, :, 1]
    value_rows = qkv_rows[:, :, 2]

    def row_scores(row_query, row_keys, row_segments):
        raw_scores = (
            jnp.einsum("ihd,jhd->hij", row_query, row_keys, preferred_element_type=jnp.float32)
            + bias_table
        )
        same_doc = row_segments[:, None] == row_segments[None, :]
        return jnp.where(same_doc[None], raw_scores, -1e30)

    def attend_row(row_item):
        row_query, row_keys, row_values, row_segments = row_item
        scores = row_scores(row_query, row_keys, row_segments)
        row_peak = jnp.max(scores, axis=-1, keepdims=True)
        log_total = row_peak + jnp.log(jnp.sum(jnp.exp(scores - row_peak), axis=-1, keepdims=True))
        soft_probs = jnp.exp(scores - log_total).astype(jnp.bfloat16)
        mixed_row = jnp.einsum(
            "hij,jhd->ihd", soft_probs, row_values, preferred_element_type=jnp.float32
        )
        return (mixed_row.astype(jnp.bfloat16).reshape(seq_len, lane_width), log_total[:, :, 0])

    attended, log_totals = lax.map(attend_row, (queries, key_rows, value_rows, segment_ids))
    flat_attended = attended.reshape(batch_rows * seq_len, lane_width)
    attn_terms = product(flat_attended, proj_low).reshape(batch_rows, seq_len, model_width)
    attn_branch = lax.psum_scatter(attn_terms, "mp", scatter_dimension=1, tiled=True)
    middle = residual_in + attn_branch
    normed_ff_local = rms_norm(middle, ff_gain).astype(jnp.bfloat16)
    normed_ff = lax.all_gather(normed_ff_local, "mp", axis=1, tiled=True)
    flat_ff = normed_ff.reshape(batch_rows * seq_len, model_width)
    gate_up = product(flat_ff, gate_up_low)
    gate_act = gate_up[:, :ff_width]
    up_act = gate_up[:, ff_width:]
    hidden = gated_gelu(gate_act, up_act).astype(jnp.bfloat16)
    ff_terms = product(hidden, down_low).reshape(batch_rows, seq_len, model_width)
    ff_branch = lax.psum_scatter(
        ff_terms.astype(jnp.bfloat16), "mp", scatter_dimension=1, tiled=True
    ).astype(jnp.float32)
    layer_out = (middle + ff_branch).astype(jnp.bfloat16)
    cot_full = lax.all_gather(cotangent, "mp", axis=1, tiled=True)
    flat_cot = cot_full.reshape(batch_rows * seq_len, model_width)
    d_hidden = right_inner(flat_cot, down_low)
    gate_pull = jax.vjp(gated_gelu, gate_act, up_act)[1]
    d_gate, d_up = gate_pull(d_hidden)
    d_gate_up = jnp.concatenate([d_gate, d_up], axis=1).astype(jnp.bfloat16)
    d_down_w = left_inner(hidden, flat_cot)
    d_gate_up_w = left_inner(flat_ff, d_gate_up)
    d_gate_w = d_gate_up_w[:, :ff_width]
    d_up_w = d_gate_up_w[:, ff_width:]
    dn_ff_terms = right_inner(d_gate_up, gate_up_low).reshape(batch_rows, seq_len, model_width)
    dn_ff = lax.psum_scatter(
        dn_ff_terms.astype(jnp.bfloat16), "mp", scatter_dimension=1, tiled=True
    ).astype(jnp.float32)
    ff_norm_pull = jax.vjp(rms_norm, middle, ff_gain)[1]
    d_middle_norm, d_ff_gain = ff_norm_pull(dn_ff)
    d_middle = cotangent.astype(jnp.float32) + d_middle_norm
    d_attn_local = d_middle.astype(jnp.bfloat16)
    d_attn_full = lax.all_gather(d_attn_local, "mp", axis=1, tiled=True)
    flat_d_attn = d_attn_full.reshape(batch_rows * seq_len, model_width)
    d_out_w = left_inner(flat_attended, flat_d_attn)
    d_attended = (
        right_inner(flat_d_attn, proj_low)
        .astype(jnp.bfloat16)
        .reshape(batch_rows, seq_len, slots_here, HD)
    )

    def attend_back(bias_sum, row_item):
        row_query, row_keys, row_values, row_segments, row_lse, row_grad = row_item
        scores = row_scores(row_query, row_keys, row_segments)
        soft_probs = jnp.exp(scores - row_lse[:, :, None])
        d_values = jnp.einsum(
            "hij,ihd->jhd",
            soft_probs.astype(jnp.bfloat16),
            row_grad,
            preferred_element_type=jnp.float32,
        ).astype(jnp.bfloat16)
        d_probs = jnp.einsum(
            "ihd,jhd->hij", row_grad, row_values, preferred_element_type=jnp.float32
        )
        row_delta = jnp.sum(soft_probs * d_probs, axis=-1, keepdims=True)
        d_scores = (soft_probs * (d_probs - row_delta)).astype(jnp.bfloat16)
        d_query = jnp.einsum(
            "hij,jhd->ihd", d_scores, row_keys, preferred_element_type=jnp.float32
        ).astype(jnp.bfloat16)
        d_keys = jnp.einsum(
            "hij,ihd->jhd", d_scores, row_query, preferred_element_type=jnp.float32
        ).astype(jnp.bfloat16)
        stacked = jnp.stack([d_query, d_keys, d_values], axis=1).reshape(seq_len, 3 * lane_width)
        return (bias_sum + d_scores.astype(jnp.float32), stacked)

    bias_start = jnp.zeros((slots_here, seq_len, seq_len), jnp.float32)
    bias_grad, d_qkv = lax.scan(
        attend_back,
        bias_start,
        (queries, key_rows, value_rows, segment_ids, log_totals, d_attended),
    )
    flat_d_qkv = d_qkv.reshape(batch_rows * seq_len, 3 * lane_width)
    dn_attn_terms = right_inner(flat_d_qkv, qkv_low).reshape(batch_rows, seq_len, model_width)
    dn_attn = lax.psum_scatter(
        dn_attn_terms.astype(jnp.bfloat16), "mp", scatter_dimension=1, tiled=True
    ).astype(jnp.float32)
    attn_norm_pull = jax.vjp(rms_norm, residual_in, attn_gain)[1]
    d_input_norm, d_attn_gain = attn_norm_pull(dn_attn)
    input_grad = (d_middle + d_input_norm).astype(jnp.bfloat16)
    d_qkv_w = left_inner(flat_norm, flat_d_qkv)
    d_query_w = d_qkv_w[:, :lane_width]
    d_key_w = d_qkv_w[:, lane_width : 2 * lane_width]
    d_value_w = d_qkv_w[:, 2 * lane_width :]
    d_vector = diagonal_sums(bias_grad)
    d_rel = lax.dot_general(
        onehot,
        d_vector,
        (((0,), (1,)), ((), ())),
        precision=highest,
        preferred_element_type=jnp.float32,
    )
    matrix_params = (
        query_weight,
        key_weight,
        value_weight,
        out_weight,
        rel_bias,
        gate_weight,
        up_weight,
        down_weight,
    )
    free_dims = (0, 0, 0, 1, 0, 0, 0, 1)
    summed = (
        lax.psum(d_attn_gain.astype(jnp.bfloat16), "dp").astype(jnp.float32),
        lax.psum(d_query_w.astype(jnp.bfloat16), "dp").astype(jnp.float32),
        lax.psum(d_key_w.astype(jnp.bfloat16), "dp").astype(jnp.float32),
        lax.psum(d_value_w.astype(jnp.bfloat16), "dp").astype(jnp.float32),
        lax.psum(d_out_w.astype(jnp.bfloat16), "dp").astype(jnp.float32),
        lax.psum(d_rel.astype(jnp.bfloat16), "dp").astype(jnp.float32),
        lax.psum(d_ff_gain.astype(jnp.bfloat16), "dp").astype(jnp.float32),
        lax.psum(d_gate_w.astype(jnp.bfloat16), "dp").astype(jnp.float32),
        lax.psum(d_up_w.astype(jnp.bfloat16), "dp").astype(jnp.float32),
        lax.psum(d_down_w.astype(jnp.bfloat16), "dp").astype(jnp.float32),
    )
    gain_pieces = (
        take_piece(summed[0], 0, data_index, data_count),
        take_piece(summed[6], 0, data_index, data_count),
    )
    matrix_grads = (
        summed[1],
        summed[2],
        summed[3],
        summed[4],
        summed[5],
        summed[7],
        summed[8],
        summed[9],
    )
    row_parts = []
    col_parts = []
    weight_squares = []
    for grad_region, free_dim, weight in zip(matrix_grads, free_dims, matrix_params):
        grad_piece = take_piece(grad_region, free_dim, data_index, data_count)
        squares = grad_piece * grad_piece + 1e-30
        weight_piece = take_piece(weight, free_dim, data_index, data_count)
        weight_squares.append(jnp.sum(weight_piece * weight_piece))
        if free_dim == 0:
            row_parts.append(place_block(jnp.sum(squares, axis=1), data_index, data_count))
            col_parts.append(place_block(jnp.sum(squares, axis=0), tensor_index, tensor_count))
        else:
            row_parts.append(place_block(jnp.sum(squares, axis=1), tensor_index, tensor_count))
            col_parts.append(place_block(jnp.sum(squares, axis=0), data_index, data_count))
    gain_parts = [place_block(gain_piece, data_index, data_count) for gain_piece in gain_pieces]
    vector_parts = row_parts + col_parts + gain_parts + [jnp.stack(weight_squares)]
    vector_stats = jnp.concatenate(vector_parts)
    vector_sums = lax.psum(vector_stats, ("dp", "mp"))
    split_sums = []
    offset = 0
    for part in vector_parts:
        split_sums.append(vector_sums[offset : offset + part.shape[0]])
        offset = offset + part.shape[0]
    matrix_count = len(matrix_params)
    weight_totals = split_sums[2 * matrix_count + 2]
    new_regions = []
    row_outputs = []
    col_outputs = []
    for position in range(matrix_count):
        free_dim = free_dims[position]
        row_total = split_sums[position]
        col_total = split_sums[matrix_count + position]
        full_rows = row_total.shape[0]
        full_cols = col_total.shape[0]
        row_moment = row_total / full_cols
        col_moment = col_total / full_rows
        row_level = jnp.sum(row_moment) / full_rows
        grad_region = matrix_grads[position]
        rows_here = grad_region.shape[0]
        cols_here = grad_region.shape[1]
        if free_dim == 0:
            row_start = 0
            col_start = tensor_index * cols_here
            row_outputs.append(row_moment)
            col_outputs.append(
                lax.dynamic_slice_in_dim(col_moment, tensor_index * cols_here, cols_here, 0)
            )
        else:
            row_start = tensor_index * rows_here
            col_start = 0
            row_outputs.append(
                lax.dynamic_slice_in_dim(row_moment, tensor_index * rows_here, rows_here, 0)
            )
            col_outputs.append(col_moment)
        row_factor = lax.rsqrt(
            lax.dynamic_slice_in_dim(row_moment, row_start, rows_here, 0) / row_level
        )
        col_factor = lax.rsqrt(lax.dynamic_slice_in_dim(col_moment, col_start, cols_here, 0))
        update = grad_region * row_factor[:, None] * col_factor[None, :]
        step_rate = step_scale * jnp.sqrt(weight_totals[position] / (full_rows * full_cols))
        weight = matrix_params[position]
        new_regions.append(weight - step_rate * update)
    new_weights = tuple(new_regions)
    attn_gain_grad = split_sums[2 * matrix_count]
    ff_gain_grad = split_sums[2 * matrix_count + 1]
    attn_gain_moment = attn_gain_grad * attn_gain_grad + 1e-30
    ff_gain_moment = ff_gain_grad * ff_gain_grad + 1e-30
    new_attn_gain = attn_gain - step_scale * jnp.sqrt(
        jnp.mean(attn_gain * attn_gain)
    ) * attn_gain_grad * lax.rsqrt(jnp.mean(attn_gain_moment))
    new_ff_gain = ff_gain - step_scale * jnp.sqrt(
        jnp.mean(ff_gain * ff_gain)
    ) * ff_gain_grad * lax.rsqrt(jnp.mean(ff_gain_moment))
    return (
        layer_out,
        input_grad,
        new_attn_gain,
        attn_gain_moment,
        new_weights[0],
        row_outputs[0],
        col_outputs[0],
        new_weights[1],
        row_outputs[1],
        col_outputs[1],
        new_weights[2],
        row_outputs[2],
        col_outputs[2],
        new_weights[3],
        row_outputs[3],
        col_outputs[3],
        new_weights[4],
        row_outputs[4],
        col_outputs[4],
        new_ff_gain,
        ff_gain_moment,
        new_weights[5],
        row_outputs[5],
        col_outputs[5],
        new_weights[6],
        row_outputs[6],
        col_outputs[6],
        new_weights[7],
        row_outputs[7],
        col_outputs[7],
    )


def solution(mesh):
    return jax.shard_map(
        local,
        mesh=mesh,
        in_specs=(
            P("dp", "mp", None),
            P("dp", None),
            P(),
            P(),
            P(None, "mp"),
            P(None, "mp"),
            P(None, "mp"),
            P("mp", None),
            P(None, "mp"),
            P(),
            P(None, "mp"),
            P(None, "mp"),
            P("mp", None),
            P("dp", "mp", None),
        ),
        out_specs=(
            P("dp", "mp", None),
            P("dp", "mp", None),
            P(),
            P(),
            P(None, "mp"),
            P(),
            P("mp"),
            P(None, "mp"),
            P(),
            P("mp"),
            P(None, "mp"),
            P(),
            P("mp"),
            P("mp", None),
            P("mp"),
            P(),
            P(None, "mp"),
            P(),
            P("mp"),
            P(),
            P(),
            P(None, "mp"),
            P(),
            P("mp"),
            P(None, "mp"),
            P(),
            P("mp"),
            P("mp", None),
            P("mp"),
            P(),
        ),
        check_vma=False,
    )
```

profile of v0, /device:TPU:0, one launch (start us, length us, event | category | flops | bytes accessed | tf_op | source)
XLA Modules:
  0.0 1012.3 jit_solution(939090028204672081)
XLA Ops:
  13.6 7.9 tile.18
  21.5 23.8 %reshape.309 = f32[4192256]{0:T(1024)} reshape(f32[2,1024,2047]{2,1,0:T(8,128)} %tile.18) | data formatting | bytes 33538048
  45.3 24.4 %tile.19 = f32[2,2096128]{1,0:T(2,128)} reshape(f32[4192256]{0:T(1024)} %reshape.309) | data formatting | bytes 33538048 | tf_op jit(solution)/shard_map/tile | solution.py:42
  69.7 12.1 %slice.187 = f32[2,2095104]{1,0:T(2,128)} slice(f32[2,2096128]{1,0:T(2,128)} %tile.19), slice={[0:2], [0:2095104]} | slice | bytes 33521664 | tf_op jit(solution)/shard_map/slice | solution.py:42
  81.8 37.8 %reshape.311 = f32[4190208]{0:T(1024)} reshape(f32[2,2095104]{1,0:T(2,128)} %slice.187) | data formatting | bytes 33521664
  119.6 16.7 %reshape.300 = f32[2,1024,2046]{2,1,0:T(8,128)} reshape(f32[4190208]{0:T(1024)} %reshape.311) | data formatting | bytes 33521664 | tf_op jit(solution)/shard_map/reshape | solution.py:43
  136.3 8.4 slice.188
  144.7 9.0 copy.63
  154.6 3.6 fusion.45
  165.8 3.5 convolution_bitcast_fusion
  169.4 109.4 %reduce-scatter.5.cloned.1.call-done = f32[1,256,1472]{1,2,0:T(8,128)} async-done(((f32[1,1024,1472]{1,2,0:T(8,128)}), f32[1,256,1472]{1,2,0:T(8,128)}) %reduce-scatter.5.cloned.1.call-update) | async-done | bytes 1507344 | tf_op jit(solution)/shard_map/reduce_scatter | solution.py:145
  282.3 4.3 convert.29
  286.5 4.4 convert.28
  290.9 52.7 %all-gather.7.cloned.1.call-done = bf16[1,1024,1472]{1,2,0:T(8,128)(2,1)} async-done(((bf16[1,256,1472]{1,2,0:T(8,128)(2,1)}), bf16[1,1024,1472]{1,2,0:T(8,128)(2,1)}) %all-gather.7.cloned.1.call-update) | async-done | bytes 3014672 | tf_op jit(solution)/shard_map/all_gather | solution.py:148
  343.6 11.4 %fusion.8 = f32[1024,1792]{1,0:T(8,128)} fusion(bf16[1472,896]{1,0:T(8,128)(2,1)} %convert.29, bf16[1472,896]{1,0:T(8,128)(2,1)} %convert.28, bf16[1,1024,1472]{1,2,0:T(8,128)(2,1)} %all-gather.7.cloned.1.call-done), kind=kOutput, calls=%fused_computation.31 | convolution fusion | flops 5412814848 | bytes 15630336 | tf_op jit(solution)/shard_map/dot_general | solution.py:23
  355.0 49.5 %all-gather.9.cloned.1.call-done = bf16[1,1024,1472]{1,2,0:T(8,128)(2,1)} async-done(((bf16[1,256,1472]{1,2,0:T(8,128)(2,1)}), bf16[1,1024,1472]{1,2,0:T(8,128)(2,1)}) %all-gather.9.cloned.1.call-update) | async-done | bytes 3014672 | tf_op jit(solution)/shard_map/all_gather | solution.py:159
  404.5 13.1 %fusion.7 = (bf16[1024,896]{1,0:T(8,128)(2,1)S(1)}, bf16[1024,896]{1,0:T(8,128)(2,1)S(1)}, bf16[1024,896]{1,0:T(8,128)(2,1)}) fusion(f32[1024,1792]{1,0:T(8,128)} %fusion.8, f32[896,1472]{0,1:T(8,128)} %param.26, bf16[1,1024,1472]{1,2,0:T(8,128)(2,1)} %all-gather.9.cloned.1.call-done), kind=kOutput, calls=%fused_computation.25 | convolution fusion | flops 2726305792 | bytes 21135360 | tf_op jit(solution)/shard_map/dot_general | solution.py:33
  419.5 7.0 fusion.11
  426.5 56.5 %reduce-scatter.9.cloned.1.call-done = bf16[1,256,1472]{1,2,0:T(8,128)(2,1)} async-done(((bf16[1,1024,1472]{1,2,0:T(8,128)(2,1)}), bf16[1,256,1472]{1,2,0:T(8,128)(2,1)}) %reduce-scatter.9.cloned.1.call-update) | async-done | bytes 753680 | tf_op jit(solution)/shard_map/reduce_scatter | solution.py:170
  484.9 2.7 fusion.67
  487.7 7.4 convolution_convert_fusion.4
  495.1 6.0 convolution_convert_fusion
  501.1 2.8 fusion.107
  503.9 45.1 %all-gather.11.cloned.1.call-done = bf16[1,1024,1472]{1,2,0:T(8,128)(2,1)} async-done(((bf16[1,256,1472]{1,2,0:T(8,128)(2,1)}), bf16[1,1024,1472]{1,2,0:T(8,128)(2,1)}) %all-gather.11.cloned.1.call-update) | async-done | bytes 3014672 | tf_op jit(solution)/shard_map/all_gather | solution.py:177
  549.0 2.5 fusion.50
  551.5 4.9 fusion.55
  556.5 4.5 multiply_reduce_fusion
  561.1 2.5 multiply_convert_fusion
  571.5 5.1 fusion.10
  577.1 8.0 fusion.9
  599.3 6.2 copy.64
  605.5 8.9 pad.10.clone
  614.5 30.3 %reshape.313 = bf16[6289408]{0:T(1024)(128)(2,1)} reshape(bf16[2,1024,3071]{2,1,0:T(8,128)(2,1)} %pad.10.clone) | data formatting | bytes 25157632
  644.8 16.6 %reshape.307 = bf16[2,3144704]{1,0:T(2,128)(2,1)} reshape(bf16[6289408]{0:T(1024)(128)(2,1)} %reshape.313) | data formatting | bytes 25157632 | tf_op jit(solution)/shard_map/reshape | solution.py:51
  661.4 11.5 %pad.11 = bf16[2,3145728]{1,0:T(2,128)(2,1)S(1)} pad(bf16[2,3144704]{1,0:T(2,128)(2,1)} %reshape.307, bf16[]{:T(256)} %constant.178.clone.1), padding=0_0x0_1024 | pad | bytes 25161730 | tf_op jit(solution)/shard_map/jit(_pad)/pad | solution.py:51
  672.9 10.5 %copy.67 = bf16[1,2,1024,3072]{3,2,1,0:T(8,128)(2,1)S(1)} copy(bf16[1,2,1024,3072]{3,1,2,0:T(2,128)(2,1)S(1)} %bitcast.113) | data formatting | bytes 25165824
  686.3 23.6 %all-reduce.9.cloned.1.call-done = (bf16[1472,128]{1,0:T(8,128)(2,1)}, bf16[1472,128]{1,0:T(8,128)(2,1)}, bf16[1472,128]{1,0:T(8,128)(2,1)}, bf16[128,1472]{0,1:...) async-done(((bf16[1472,128]{1,0:T(8,128)(2,1)}, bf16[1472,128]{1,0:T(8,128)(2,1)}, bf16[1472,128]{1,0:T(8,128)(2,1)}, ...) | async-done | bytes 9420816 | tf_op jit(solution)/shard_map/psum | solution.py:249
  716.9 2.7 convert_element_type.206
  719.8 2.7 convert_element_type.207
  722.6 2.7 convert_element_type.209
  736.3 34.4 %reduce-scatter.11.cloned.1.call-done = bf16[1,256,1472]{1,2,0:T(8,128)(2,1)} async-done(((bf16[1,1024,1472]{1,2,0:T(8,128)(2,1)}), bf16[1,256,1472]{1,2,0:T(8,128)(2,1)}) %reduce-scatter.11.cloned.1.call-update) | async-done | bytes 753680 | tf_op jit(solution)/shard_map/reduce_scatter | solution.py:218
  772.7 14.0 %all-reduce.2 = (bf16[32,2]{0,1:T(2,128)(2,1)S(1)}, bf16[1472]{0:T(1024)(128)(2,1)S(1)}, bf16[1472]{0:T(1024)(128)(2,1)S(1)}) all-reduce(bf16[32,2]{0,1:T(2,128)(2,1)S(1)} %convolution_convert_fusion.9, bf16[1472]{0:T(1024)(128)(2,1)S(1)} %get-tuple-element.92, ...), channel_id=1, replica_groups=mesh['dp'=8,'mp'=4] {'dp'}, use_global_device_ids=true, to_apply=%region_21.22 | all-reduce | flops 3008 | bytes 12032 | tf_op jit(solution)/shard_map/psum | solution.py:253
  787.7 5.9 concatenate.21
  793.6 37.7 %reduce-scatter.7.cloned.1.call-done = bf16[1,256,1472]{1,2,0:T(8,128)(2,1)} async-done(((bf16[1,1024,1472]{1,2,0:T(8,128)(2,1)}), bf16[1,256,1472]{1,2,0:T(8,128)(2,1)}) %reduce-scatter.7.cloned.1.call-update) | async-done | bytes 753680 | tf_op jit(solution)/shard_map/reduce_scatter | solution.py:155
  831.3 3.4 fusion.42
  834.7 124.0 %all-reduce.7.cloned.1.call-done = f32[26096]{0:T(1024)} async-done(((f32[26096]{0:T(1024)}), f32[26096]{0:T(1024)}) %all-reduce.7.cloned.1.call-update) | async-done | bytes 104400 | tf_op jit(solution)/shard_map/psum | solution.py:290
  988.3 7.0 multiply_subtract_fusion
  998.7 5.0 multiply_subtract_fusion.1
  (238 shorter events, 89.3 us)
Async XLA Ops:
  7.2 147.3 %all-gather.5.cloned.1.call-start = ((), (), s32[]{:S(2)}) async-start(), calls=%async_computation.4 | async-start | bytes 3768320 | tf_op jit(solution)/shard_map/all_gather | solution.py:112
  12.0 266.8 %reduce-scatter.5.cloned.1.call-start = ((), (), s32[]{:S(2)}) async-start(), calls=%async_computation.5 | async-start | bytes 7536640 | tf_op jit(solution)/shard_map/reduce_scatter | solution.py:145
  144.7 9.2 copy-start.30
  144.7 9.9 copy-start.18
  144.7 9.9 copy-start.20
  154.6 4.5 copy-start.2
  158.2 4.1 copy-start.11
  161.1 3.3 copy-start
  169.3 109.5 %copy-start.3 = (bf16[1,256,1472]{1,2,0:T(8,128)(2,1)S(1)}, bf16[1,256,1472]{1,2,0:T(8,128)(2,1)}, u32[]{:S(2)}) copy-start(bf16[1,256,1472]{1,2,0:T(8,128)(2,1)} %param.14) | copy-start | bytes 2260996
  169.3 111.1 %copy-start.23 = (f32[1472]{0:T(1024)S(1)}, f32[1472]{0:T(1024)}, u32[]{:S(2)}) copy-start(f32[1472]{0:T(1024)} %param.23) | copy-start | bytes 17668
  169.4 174.2 %all-gather.7.cloned.1.call-start = ((), (), s32[]{:S(2)}) async-start(), calls=%async_computation.6 | async-start | bytes 3768320 | tf_op jit(solution)/shard_map/all_gather | solution.py:148
  281.6 122.9 %all-gather.9.cloned.1.call-start = ((), (), s32[]{:S(2)}) async-start(), calls=%async_computation.8 | async-start | bytes 3768320 | tf_op jit(solution)/shard_map/all_gather | solution.py:159
  282.2 200.8 %reduce-scatter.9.cloned.1.call-start = ((), (), s32[]{:S(2)}) async-start(), calls=%async_computation.9 | async-start | bytes 3768320 | tf_op jit(solution)/shard_map/reduce_scatter | solution.py:170
  404.5 15.0 %copy-start.13 = (bf16[1472,896]{1,0:T(8,128)(2,1)S(1)}, bf16[1472,896]{1,0:T(8,128)(2,1)}, u32[]{:S(2)}) copy-start(bf16[1472,896]{1,0:T(8,128)(2,1)} %convert.29) | copy-start | bytes 7913476
  404.5 15.0 %copy-start.14 = (bf16[1472,896]{1,0:T(8,128)(2,1)S(1)}, bf16[1472,896]{1,0:T(8,128)(2,1)}, u32[]{:S(2)}) copy-start(bf16[1472,896]{1,0:T(8,128)(2,1)} %convert.28) | copy-start | bytes 7913476
  426.5 122.5 %all-gather.11.cloned.1.call-start = ((), (), s32[]{:S(2)}) async-start(), calls=%async_computation.10 | async-start | bytes 3768320 | tf_op jit(solution)/shard_map/all_gather | solution.py:177
  487.6 222.3 %all-reduce.9.cloned.1.call-start = ((), (), s32[]{:S(2)}) async-start(), calls=%async_computation.13 | async-start | bytes 18841600 | tf_op jit(solution)/shard_map/psum | solution.py:249
  487.7 7.4 copy-start.37
  487.7 7.4 copy-start.41
  487.7 7.4 copy-start.43
  551.5 5.0 copy-start.12
  551.5 9.5 slice-start
  556.5 4.6 slice-start.1
  571.4 199.3 %reduce-scatter.11.cloned.1.call-start = ((), (), s32[]{:S(2)}) async-start(), calls=%async_computation.11 | async-start | bytes 3768320 | tf_op jit(solution)/shard_map/reduce_scatter | solution.py:218
  576.6 9.9 copy-start.24
  576.6 11.2 %copy-start.35 = (f32[32,2]{0,1:T(2,128)S(1)}, f32[32,2]{0,1:T(2,128)}, u32[]{:S(2)}) copy-start(f32[32,2]{0,1:T(2,128)} %param.22) | copy-start | bytes 772
  576.6 254.7 %reduce-scatter.7.cloned.1.call-start = ((), (), s32[]{:S(2)}) async-start(), calls=%async_computation.7 | async-start | bytes 3768320 | tf_op jit(solution)/shard_map/reduce_scatter | solution.py:155
  585.2 373.6 %all-reduce.7.cloned.1.call-start = ((), (), s32[]{:S(2)}) async-start(), calls=%async_computation.12 | async-start | bytes 212992 | tf_op jit(solution)/shard_map/psum | solution.py:290
  709.9 6.9 copy-start.6
  722.6 48.1 %copy-start.32 = (f32[256]{0:T(256)S(1)}, f32[256]{0:T(256)}, u32[]{:S(2)}) copy-start(f32[256]{0:T(256)} %copy-done.31) | copy-start | bytes 3076
  725.3 68.3 %copy-start.34 = (f32[256]{0:T(256)S(1)}, f32[256]{0:T(256)}, u32[]{:S(2)}) copy-start(f32[256]{0:T(256)} %copy-done.33) | copy-start | bytes 3076
  793.6 192.9 %copy-start.15 = (bf16[128,1472]{0,1:T(8,128)(2,1)S(1)}, bf16[128,1472]{0,1:T(8,128)(2,1)}, u32[]{:S(2)}) copy-start(bf16[128,1472]{0,1:T(8,128)(2,1)} %get-tuple-element.110) | copy-start | bytes 1130500
  960.9 34.4 %copy-start.25 = (f32[1472]{0:T(1024)}, f32[1472]{0:T(1024)S(1)}, u32[]{:S(2)}) copy-start(f32[1472]{0:T(1024)S(1)} %get-tuple-element.179) | copy-start | bytes 17668
  960.9 34.4 %copy-start.26 = (f32[1472]{0:T(1024)}, f32[1472]{0:T(1024)S(1)}, u32[]{:S(2)}) copy-start(f32[1472]{0:T(1024)S(1)} %get-tuple-element.181) | copy-start | bytes 17668
  960.9 34.5 %copy-start.27 = (f32[1472]{0:T(1024)}, f32[1472]{0:T(1024)S(1)}, u32[]{:S(2)}) copy-start(f32[1472]{0:T(1024)S(1)} %get-tuple-element.185) | copy-start | bytes 17668
  960.9 34.5 %copy-start.28 = (f32[1472]{0:T(1024)}, f32[1472]{0:T(1024)S(1)}, u32[]{:S(2)}) copy-start(f32[1472]{0:T(1024)S(1)} %get-tuple-element.187) | copy-start | bytes 17668
  960.9 34.5 %copy-start.29 = (f32[1472]{0:T(1024)}, f32[1472]{0:T(1024)S(1)}, u32[]{:S(2)}) copy-start(f32[1472]{0:T(1024)S(1)} %get-tuple-element.189) | copy-start | bytes 17668
  981.5 13.9 %copy-start.39 = (f32[32]{0:T(128)}, f32[32]{0:T(128)S(1)}, u32[]{:S(2)}) copy-start(f32[32]{0:T(128)S(1)} %get-tuple-element.129) | copy-start | bytes 388
  986.5 8.9 copy-start.16
  986.5 8.9 copy-start.17
  986.5 8.9 copy-start.19
  986.5 8.9 copy-start.21
  988.3 8.7 slice-start.2
  988.3 8.7 slice-start.4
  988.3 8.7 slice-start.3
  988.3 8.7 slice-start.5
  988.3 9.6 copy-start.9
  995.4 3.3 copy-start.7
  (12 other events, 23.3 us)
Sparse Core Ops, SparseCore 0:
  12.1 63.9 all-gather.4
  169.5 109.2 reduce-scatter.4
  281.8 61.7 all-gather.6
  345.0 59.4 all-gather.8
  426.6 56.4 reduce-scatter.8
  487.7 61.1 all-gather.10
  571.5 138.3 all-reduce.8
  712.4 58.2 reduce-scatter.10
  773.1 58.1 reduce-scatter.6
  838.3 120.4 all-reduce.6
where the time goes:
time: 1020 us; the launch traced here: 1010 us
  waiting for transfers between devices  534 us (52%)
  local copies, waits for them, and re-layouts  251 us (25%)
  other arithmetic  96 us (9%)
  matrix products  88.3 us (9%)
  between operations  28.7 us (3%)
  blocking collectives  14 us (1%)
    unnamed x106, local copies, waits for them, and re-layouts  127 us
    psum x1, waiting for transfers between devices, local(): vector_sums = lax.psum(vector_stats, ('dp', 'mp'))  124 us
    reduce_scatter x1, waiting for transfers between devices, local(): lax.psum_scatter(attn_terms, 'mp', scatter_dimension=1, tiled=True)  109 us
    reduce_scatter x1, waiting for transfers between devices, local(): lax.psum_scatter(dn_ff_terms.astype(jnp.bfloat16), 'mp', scatter_dimensio...  56.5 us
    all_gather x1, waiting for transfers between devices, local(): normed_ff = lax.all_gather(normed_ff_local, 'mp', axis=1, tiled=True)  52.7 us
    all_gather x1, waiting for transfers between devices, local(): cot_full = lax.all_gather(cotangent, 'mp', axis=1, tiled=True)  49.5 us
    all_gather x1, waiting for transfers between devices, local(): d_attn_full = lax.all_gather(d_attn_local, 'mp', axis=1, tiled=True)  45.1 us
    reduce_scatter x1, waiting for transfers between devices, local(): lax.psum_scatter(ff_terms.astype(jnp.bfloat16), 'mp', scatter_dimension=1...  37.7 us
  transfers between devices with their start and end apart: 10, of which 9 were waited for; matrix products, arithmetic and copies ran while one was open for 33% of the time, Pallas kernels for 0%

commit v1 on v0

v1 whole, which is shorter than its diff:
```python
import functools

import jax
import jax.numpy as jnp
from jax import lax
from jax.experimental import pallas as pl
from jax.experimental.pallas import tpu as pltpu
from jax.sharding import PartitionSpec as P

HD = 64
BUCKETS = 32
BLOCK = 128


highest = lax.Precision.HIGHEST
step_scale = 0.3


def rms_norm(values, gain):
    return values * lax.rsqrt(jnp.mean(values * values, axis=-1, keepdims=True) + 1e-06) * gain


def gated_gelu(gate_act, up_act):
    return jax.nn.gelu(gate_act, approximate=True) * up_act


def product(left_side, right_side):
    return jnp.dot(left_side, right_side, preferred_element_type=jnp.float32)


def left_inner(left_side, right_side):
    return lax.dot_general(
        left_side, right_side, (((0,), (0,)), ((), ())), preferred_element_type=jnp.float32
    )


def right_inner(left_side, right_side):
    return lax.dot_general(
        left_side, right_side, (((1,), (1,)), ((), ())), preferred_element_type=jnp.float32
    )


def slot_lanes(values, slot):
    lane = lax.broadcasted_iota(jnp.int32, values.shape, 1)
    return jnp.where((lane >= slot * HD) & (lane < (slot + 1) * HD), values, jnp.zeros_like(values))


def attend_kernel(seq_len, slots, qkv_ref, seg_col_ref, seg_row_ref, vec_ref, out_ref, probs_ref, tilt_ref):
    step = pl.program_id(0)
    steps = seq_len // BLOCK
    lanes = slots * HD

    @pl.when(step == 0)
    def _():
        for slot in range(slots):
            spread = jnp.broadcast_to(vec_ref[slot : slot + 1, :], (BLOCK, 2 * seq_len))
            tilt_ref[slot] = pltpu.roll(
                spread, 2 * seq_len - BLOCK + 1, 1, stride=1, stride_axis=0
            )

    same_doc = seg_col_ref[...] == seg_row_ref[...]
    rows = pl.ds(pl.multiple_of(step * BLOCK, BLOCK), BLOCK)
    window = pl.ds(pl.multiple_of((steps - 1 - step) * BLOCK, BLOCK), seq_len)
    queries = qkv_ref[rows, 0:lanes]
    keys = qkv_ref[:, lanes : 2 * lanes]
    values = qkv_ref[:, 2 * lanes : 3 * lanes]
    mixed = jnp.zeros((BLOCK, lanes), jnp.float32)
    for slot in range(slots):
        scores = right_inner(slot_lanes(queries, slot), keys) + tilt_ref[slot, :, window]
        scores = jnp.where(same_doc, scores, -1e30)
        peak = jnp.max(scores, axis=-1, keepdims=True)
        raised = jnp.exp(scores - peak)
        probs = raised * (1.0 / jnp.sum(raised, axis=-1, keepdims=True))
        probs_ref[slot] = probs
        mixed = mixed + slot_lanes(product(probs.astype(jnp.bfloat16), values), slot)
    out_ref[...] = mixed.astype(jnp.bfloat16)


def attend(qkv, seg_col, seg_row, vector):
    seq_len = qkv.shape[0]
    slots = vector.shape[0]
    lanes = slots * HD
    return pl.pallas_call(
        functools.partial(attend_kernel, seq_len, slots),
        grid=(seq_len // BLOCK,),
        in_specs=[
            pl.BlockSpec((seq_len, 3 * lanes), lambda i: (0, 0)),
            pl.BlockSpec((BLOCK, 1), lambda i: (i, 0)),
            pl.BlockSpec((1, seq_len), lambda i: (0, 0)),
            pl.BlockSpec((slots, 2 * seq_len), lambda i: (0, 0)),
        ],
        out_specs=[
            pl.BlockSpec((BLOCK, lanes), lambda i: (i, 0)),
            pl.BlockSpec((slots, BLOCK, seq_len), lambda i: (0, i, 0)),
        ],
        out_shape=[
            jax.ShapeDtypeStruct((seq_len, lanes), jnp.bfloat16),
            jax.ShapeDtypeStruct((slots, seq_len, seq_len), jnp.float32),
        ],
        scratch_shapes=[pltpu.VMEM((slots, BLOCK, 2 * seq_len), jnp.float32)],
        compiler_params=pltpu.CompilerParams(vmem_limit_bytes=32 << 20),
        cost_estimate=pl.CostEstimate(
            flops=8 * slots * seq_len * seq_len * HD,
            bytes_accessed=4 * slots * seq_len * seq_len,
            transcendentals=slots * seq_len * seq_len,
        ),
        name="attend",
    )(qkv, seg_col, seg_row, vector)


def attend_back_kernel(
    seq_len, slots, qkv_ref, grad_ref, probs_ref, dqkv_ref, dvec_ref, diag_ref, dk_ref, dv_ref
):
    step = pl.program_id(0)
    steps = seq_len // BLOCK
    lanes = slots * HD

    @pl.when(step == 0)
    def _():
        diag_ref[...] = jnp.zeros_like(diag_ref)
        dk_ref[...] = jnp.zeros_like(dk_ref)
        dv_ref[...] = jnp.zeros_like(dv_ref)

    rows = pl.ds(pl.multiple_of(step * BLOCK, BLOCK), BLOCK)
    window = pl.ds(pl.multiple_of((steps - 1 - step) * BLOCK, BLOCK), seq_len)
    queries = qkv_ref[rows, 0:lanes]
    keys = qkv_ref[:, lanes : 2 * lanes]
    values = qkv_ref[:, 2 * lanes : 3 * lanes]
    grad = grad_ref[...]
    d_query = jnp.zeros((BLOCK, lanes), jnp.float32)
    for slot in range(slots):
        probs = probs_ref[slot]
        slot_grad = slot_lanes(grad, slot)
        d_probs = right_inner(slot_grad, values)
        delta = jnp.sum(probs * d_probs, axis=-1, keepdims=True)
        d_scores = (probs * (d_probs - delta)).astype(jnp.bfloat16)
        d_query = d_query + slot_lanes(product(d_scores, keys), slot)
        dk_ref[...] += left_inner(slot_lanes(queries, slot), d_scores)
        dv_ref[...] += left_inner(slot_grad, probs.astype(jnp.bfloat16))
        diag_ref[slot, :, window] += d_scores.astype(jnp.float32)
    dqkv_ref[rows, 0:lanes] = d_query.astype(jnp.bfloat16)

    @pl.when(step == steps - 1)
    def _():
        dqkv_ref[:, lanes : 2 * lanes] = dk_ref[...].T.astype(jnp.bfloat16)
        dqkv_ref[:, 2 * lanes : 3 * lanes] = dv_ref[...].T.astype(jnp.bfloat16)
        for slot in range(slots):
            level = diag_ref[slot]
            half = BLOCK // 2
            while half >= 1:
                level = pltpu.roll(level[:half], half, 1) + level[half:]
                half //= 2
            dvec_ref[slot : slot + 1, :] = level


def attend_back(qkv, grad, probs):
    seq_len = qkv.shape[0]
    slots = probs.shape[0]
    lanes = slots * HD
    return pl.pallas_call(
        functools.partial(attend_back_kernel, seq_len, slots),
        grid=(seq_len // BLOCK,),
        in_specs=[
            pl.BlockSpec((seq_len, 3 * lanes), lambda i: (0, 0)),
            pl.BlockSpec((BLOCK, lanes), lambda i: (i, 0)),
            pl.BlockSpec((slots, BLOCK, seq_len), lambda i: (0, i, 0)),
        ],
        out_specs=[
            pl.BlockSpec((seq_len, 3 * lanes), lambda i: (0, 0)),
            pl.BlockSpec((slots, 2 * seq_len), lambda i: (0, 0)),
        ],
        out_shape=[
            jax.ShapeDtypeStruct((seq_len, 3 * lanes), jnp.bfloat16),
            jax.ShapeDtypeStruct((slots, 2 * seq_len), jnp.float32),
        ],
        scratch_shapes=[
            pltpu.VMEM((slots, BLOCK, 2 * seq_len), jnp.float32),
            pltpu.VMEM((lanes, seq_len), jnp.float32),
            pltpu.VMEM((lanes, seq_len), jnp.float32),
        ],
        compiler_params=pltpu.CompilerParams(vmem_limit_bytes=32 << 20),
        cost_estimate=pl.CostEstimate(
            flops=16 * slots * seq_len * seq_len * HD,
            bytes_accessed=4 * slots * seq_len * seq_len,
            transcendentals=0,
        ),
        name="attend_back",
    )(qkv, grad, probs)


def to_owners(rows_of_slots):
    count = lax.axis_size("mp")
    seq_len, lanes = rows_of_slots.shape
    pieces = rows_of_slots.reshape(count, seq_len // count, lanes)
    pieces = lax.all_to_all(pieces, "mp", split_axis=0, concat_axis=0)
    return pieces.transpose(1, 0, 2).reshape(seq_len // count, count * lanes)


def to_slots(own_rows):
    count = lax.axis_size("mp")
    local_len, width = own_rows.shape
    pieces = own_rows.reshape(local_len, count, width // count).transpose(1, 0, 2)
    pieces = lax.all_to_all(pieces, "mp", split_axis=0, concat_axis=0)
    return pieces.reshape(count * local_len, width // count)


def local(
    layer_in,
    segment_ids,
    bucket_table,
    attn_gain,
    query_weight,
    key_weight,
    value_weight,
    out_weight,
    rel_bias,
    ff_gain,
    gate_weight,
    up_weight,
    down_weight,
    cotangent,
):
    _, local_len, model_width = layer_in.shape
    seq_len = segment_ids.shape[1]
    lane_width = query_weight.shape[1]
    slots_here = lane_width // HD
    ff_width = gate_weight.shape[1]
    tensor_index = lax.axis_index("mp")
    tensor_count = lax.axis_size("mp")
    data_index = lax.axis_index("dp")
    data_count = lax.axis_size("dp")
    layer_in = layer_in[0]
    cotangent = cotangent[0]
    slot_ids = tensor_index * slots_here + jnp.arange(slots_here)
    slot_valid = ((slot_ids < 5) | (slot_ids == 6)).astype(jnp.float32)
    lane_mask = jnp.repeat(slot_valid, HD)
    qkv_low = (
        jnp.concatenate([query_weight, key_weight, value_weight], axis=1) * jnp.tile(lane_mask, 3)
    ).astype(jnp.bfloat16)
    proj_low = (out_weight * lane_mask[:, None]).astype(jnp.bfloat16)
    gate_up_low = jnp.concatenate([gate_weight, up_weight], axis=1).astype(jnp.bfloat16)
    down_low = down_weight.astype(jnp.bfloat16)
    onehot = (bucket_table[:, None] == jnp.arange(BUCKETS)[None, :]).astype(jnp.float32)
    onehot = jnp.pad(onehot, ((0, 1), (0, 0)))
    vector = lax.dot_general(
        rel_bias,
        onehot,
        (((0,), (1,)), ((), ())),
        precision=highest,
        preferred_element_type=jnp.float32,
    )
    residual_in = layer_in.astype(jnp.float32)
    normed_local = rms_norm(residual_in, attn_gain).astype(jnp.bfloat16)
    flat_norm = lax.all_gather(normed_local, "mp", axis=0, tiled=True)
    proj_all = gather_proj(proj_low)
    qkv = product(flat_norm, qkv_low).astype(jnp.bfloat16)
    attended, probs = attend(qkv, segment_ids.reshape(seq_len, 1), segment_ids, vector)
    own_attended = to_owners(attended)
    middle = residual_in + product(own_attended, proj_all)
    normed_ff_local = rms_norm(middle, ff_gain).astype(jnp.bfloat16)
    flat_ff = lax.all_gather(normed_ff_local, "mp", axis=0, tiled=True)
    flat_cot = lax.all_gather(cotangent, "mp", axis=0, tiled=True)
    gate_up = product(flat_ff, gate_up_low)
    gate_act = gate_up[:, :ff_width]
    up_act = gate_up[:, ff_width:]
    hidden = gated_gelu(gate_act, up_act).astype(jnp.bfloat16)
    ff_terms = product(hidden, down_low)
    ff_branch = lax.psum_scatter(
        ff_terms.astype(jnp.bfloat16), "mp", scatter_dimension=0, tiled=True
    ).astype(jnp.float32)
    layer_out = (middle + ff_branch).astype(jnp.bfloat16)
    d_hidden = right_inner(flat_cot, down_low)
    gate_pull = jax.vjp(gated_gelu, gate_act, up_act)[1]
    d_gate, d_up = gate_pull(d_hidden)
    d_gate_up = jnp.concatenate([d_gate, d_up], axis=1).astype(jnp.bfloat16)
    d_down_w = left_inner(hidden, flat_cot)
    d_gate_up_w = left_inner(flat_ff, d_gate_up)
    dn_ff_terms = right_inner(d_gate_up, gate_up_low)
    dn_ff = lax.psum_scatter(
        dn_ff_terms.astype(jnp.bfloat16), "mp", scatter_dimension=0, tiled=True
    ).astype(jnp.float32)
    d_gate_w = lax.psum(d_gate_up_w[:, :ff_width].astype(jnp.bfloat16), "dp").astype(jnp.float32)
    d_up_w = lax.psum(d_gate_up_w[:, ff_width:].astype(jnp.bfloat16), "dp").astype(jnp.float32)
    d_down_w = lax.psum(d_down_w.astype(jnp.bfloat16), "dp").astype(jnp.float32)
    ff_norm_pull = jax.vjp(rms_norm, middle, ff_gain)[1]
    d_middle_norm, d_ff_gain = ff_norm_pull(dn_ff)
    d_middle = cotangent.astype(jnp.float32) + d_middle_norm
    d_attn_local = d_middle.astype(jnp.bfloat16)
    d_attended = to_slots(right_inner(d_attn_local, proj_all).astype(jnp.bfloat16))
    d_out_w = left_inner(own_attended, d_attn_local).astype(jnp.bfloat16)
    d_out_w = lax.psum_scatter(d_out_w, "mp", scatter_dimension=0, tiled=True)
    flat_d_qkv, d_vector = attend_back(qkv, d_attended, probs)
    dn_attn_terms = right_inner(flat_d_qkv, qkv_low)
    dn_attn = lax.psum_scatter(
        dn_attn_terms.astype(jnp.bfloat16), "mp", scatter_dimension=0, tiled=True
    ).astype(jnp.float32)
    attn_norm_pull = jax.vjp(rms_norm, residual_in, attn_gain)[1]
    d_input_norm, d_attn_gain = attn_norm_pull(dn_attn)
    input_grad = (d_middle + d_input_norm).astype(jnp.bfloat16)
    d_qkv_w = left_inner(flat_norm, flat_d_qkv).astype(jnp.bfloat16)
    d_rel = lax.dot_general(
        onehot,
        d_vector,
        (((0,), (1,)), ((), ())),
        precision=highest,
        preferred_element_type=jnp.float32,
    )
    d_qkv_w, d_out_w = lax.psum((d_qkv_w, d_out_w), "dp")
    d_qkv_w = d_qkv_w.astype(jnp.float32)
    d_out_w = d_out_w.astype(jnp.float32)
    small = jnp.concatenate([d_attn_gain, d_ff_gain, d_rel.reshape(-1)])
    small = lax.psum(small, "dp")
    d_rel = small[2 * model_width :].reshape(BUCKETS, slots_here)
    weights = (
        query_weight,
        key_weight,
        value_weight,
        rel_bias,
        gate_weight,
        up_weight,
        out_weight,
        down_weight,
    )
    grads = (
        d_qkv_w[:, :lane_width],
        d_qkv_w[:, lane_width : 2 * lane_width],
        d_qkv_w[:, 2 * lane_width :],
        d_rel,
        d_gate_w,
        d_up_w,
        d_out_w,
        d_down_w,
    )
    split_rows = (False, False, False, False, False, False, True, True)
    whole_sums = []
    shared_sums = []
    weight_squares = []
    for grad, weight, rows_are_split in zip(grads, weights, split_rows):
        squares = grad * grad + 1e-30
        shared_axis = 0 if rows_are_split else 1
        shared_sums.append(jnp.sum(squares, axis=shared_axis))
        whole_sums.append(jnp.sum(squares, axis=1 - shared_axis))
        weight_squares.append(jnp.sum(weight * weight))
    parts = shared_sums + [small[: 2 * model_width], jnp.stack(weight_squares)]
    sums = lax.psum(jnp.concatenate(parts), "mp")
    split = []
    offset = 0
    for part in parts:
        split.append(sums[offset : offset + part.shape[0]])
        offset = offset + part.shape[0]
    gain_sums = split[len(weights)]
    weight_totals = split[len(weights) + 1]
    new_weights = []
    row_moments = []
    col_moments = []
    for position in range(len(weights)):
        grad = grads[position]
        weight = weights[position]
        rows_here, cols_here = grad.shape
        shared = split[position]
        if split_rows[position]:
            rows_here = rows_here * tensor_count
            row_moment = whole_sums[position] / cols_here
            col_moment = shared / rows_here
        else:
            cols_here = cols_here * tensor_count
            row_moment = shared / cols_here
            col_moment = whole_sums[position] / rows_here
        level = jnp.sum(shared) / (rows_here * cols_here)
        step_rate = step_scale * jnp.sqrt(weight_totals[position] / (rows_here * cols_here))
        row_factor = lax.rsqrt(row_moment / level) * step_rate
        col_factor = lax.rsqrt(col_moment)
        new_weights.append(weight - grad * row_factor[:, None] * col_factor[None, :])
        row_moments.append(row_moment)
        col_moments.append(col_moment)

    def gain_step(gain, grad):
        moment = grad * grad + 1e-30
        rate = step_scale * jnp.sqrt(jnp.mean(gain * gain))
        return gain - rate * grad * lax.rsqrt(jnp.mean(moment)), moment

    new_attn_gain, attn_gain_moment = gain_step(attn_gain, gain_sums[:model_width])
    new_ff_gain, ff_gain_moment = gain_step(ff_gain, gain_sums[model_width:])

    def matrix(position):
        return (new_weights[position], row_moments[position], col_moments[position])

    return (
        layer_out[None],
        input_grad[None],
        new_attn_gain,
        attn_gain_moment,
        *matrix(0),
        *matrix(1),
        *matrix(2),
        *matrix(6),
        *matrix(3),
        new_ff_gain,
        ff_gain_moment,
        *matrix(4),
        *matrix(5),
        *matrix(7),
    )


def gather_proj(proj_low):
    data_count = lax.axis_size("dp")
    rows = proj_low.shape[0] // data_count
    part = lax.dynamic_slice_in_dim(proj_low, lax.axis_index("dp") * rows, rows, 0)
    return lax.all_gather(part, ("mp", "dp"), axis=0, tiled=True)


def solution(mesh):
    return jax.shard_map(
        local,
        mesh=mesh,
        in_specs=(
            P("dp", "mp", None),
            P("dp", None),
            P(),
            P(),
            P(None, "mp"),
            P(None, "mp"),
            P(None, "mp"),
            P("mp", None),
            P(None, "mp"),
            P(),
            P(None, "mp"),
            P(None, "mp"),
            P("mp", None),
            P("dp", "mp", None),
        ),
        out_specs=(
            P("dp", "mp", None),
            P("dp", "mp", None),
            P(),
            P(),
            P(None, "mp"),
            P(),
            P("mp"),
            P(None, "mp"),
            P(),
            P("mp"),
            P(None, "mp"),
            P(),
            P("mp"),
            P("mp", None),
            P("mp"),
            P(),
            P(None, "mp"),
            P(),
            P("mp"),
            P(),
            P(),
            P(None, "mp"),
            P(),
            P("mp"),
            P(None, "mp"),
            P(),
            P("mp"),
            P("mp", None),
            P("mp"),
            P(),
        ),
        check_vma=False,
    )
```

time: 1020 us -> 742 us (0.73)
  local copies, waits for them, and re-layouts: 251 us -> 28.4 us
  waiting for transfers between devices: 534 us -> 441 us
  blocking collectives: 14 us -> 64.7 us
  Pallas kernels: 0 us -> 21.4 us
  other arithmetic: 96 us -> 77.4 us
  matrix products: 88.3 us -> 70.1 us
    unnamed x106 -> x90, local copies, waits for them, and re-layouts: 127 us -> 16.5 us
    reduce_scatter x2 -> x1, waiting for transfers between devices: 147 us -> 59.1 us  [local(): lax.psum_scatter(ff_terms.astype(jnp.bfloat16), 'mp', scatter_dimension=0...]
    all_gather x4, waiting for transfers between devices: 147 us -> 194 us  [the longest x1 61.6 us: local(): flat_norm = lax.all_gather(normed_local, 'mp', axis=0, tiled=True)]
    psum x2 -> x1, waiting for transfers between devices: 148 us -> 115 us  [local(): d_qkv_w, d_out_w = lax.psum((d_qkv_w, d_out_w), 'dp')]
    another operation x19 -> x0, local copies, waits for them, and re-layouts: 32.3 us -> none  [the longest x2 32.3 us: toeplitz(): tiled = jnp.tile(rolled, (1, seq_len))[:, :seq_len * (span - 1)]]
    reshape x2 -> x5, local copies, waits for them, and re-layouts: 33.2 us -> 1.32 us  [the longest x1 0.85 us: to_owners(): pieces = rows_of_slots.reshape(count, seq_len // count, lanes)]
    psum x1 -> x2, blocking collectives: 14 us -> 45 us  [the longest x1 25.2 us: local(): small = lax.psum(small, 'dp')]
    slice x7 -> x3, local copies, waits for them, and re-layouts: 26.1 us -> 3.47 us  [the longest x1 2.79 us: local(): d_gate_up_w[:, ff_width:].astype(jnp.bfloat16)]
  transfers between devices with their start and end apart: 10 -> 10, of which waited for: 9 -> 8; matrix products, arithmetic and copies ran while one was open for 33% -> 12% of each run, Pallas kernels for 0% -> 3%
where the time goes in v1:
time: 742 us; the launch traced here: 735 us
  waiting for transfers between devices  441 us (59%)
  other arithmetic  77.4 us (10%)
  matrix products  70.1 us (9%)
  blocking collectives  64.7 us (9%)
  local copies, waits for them, and re-layouts  28.4 us (4%)
  between operations  28.3 us (4%)
  Pallas kernels  21.4 us (3%)
    psum x1, waiting for transfers between devices, local(): d_qkv_w, d_out_w = lax.psum((d_qkv_w, d_out_w), 'dp')  115 us
    all_gather x1, waiting for transfers between devices, local(): flat_norm = lax.all_gather(normed_local, 'mp', axis=0, tiled=True)  61.6 us
    reduce_scatter x1, waiting for transfers between devices, local(): lax.psum_scatter(ff_terms.astype(jnp.bfloat16), 'mp', scatter_dimension=0...  59.1 us
    all_gather x1, waiting for transfers between devices, local(): flat_cot = lax.all_gather(cotangent, 'mp', axis=0, tiled=True)  49.5 us
    reduce_scatter x1, waiting for transfers between devices, local(): lax.psum_scatter(dn_ff_terms.astype(jnp.bfloat16), 'mp', scatter_dimensio...  48.3 us
    all_gather x1, waiting for transfers between devices, local(): flat_ff = lax.all_gather(normed_ff_local, 'mp', axis=0, tiled=True)  47.8 us
    all_gather x1, waiting for transfers between devices, gather_proj(): return lax.all_gather(part, ('mp', 'dp'), axis=0, tiled=True)  35.3 us
    dot_general x4, matrix products, product(): return jnp.dot(left_side, right_side, preferred_element_type=jnp.float32)  25.7 us
  transfers between devices with their start and end apart: 10, of which 8 were waited for; matrix products, arithmetic and copies ran while one was open for 12% of the time, Pallas kernels for 3%

profile of v1, /device:TPU:0, one launch (start us, length us, event | category | flops | bytes accessed | tf_op | source)
XLA Modules:
  0.0 735.2 jit_solution(14762369847605219498)
XLA Ops:
  8.7 2.3 fusion.31
  13.6 61.6 %all-gather.6.cloned.1.call-done = bf16[1024,1472]{0,1:T(8,128)(2,1)} async-done(((bf16[256,1472]{0,1:T(8,128)(2,1)}), bf16[1024,1472]{0,1:T(8,128)(2,1)}) %all-gather.6.cloned.1.call-update) | async-done | bytes 3014672 | tf_op jit(solution)/shard_map/all_gather | solution.py:254
  75.2 4.1 convolution_convert_fusion.7.qkv_ref
  79.3 9.9 %attend.1 = (bf16[1024,128]{1,0:T(8,128)(2,1)S(1)}, f32[2,1024,1024]{2,1,0:T(8,128)S(1)}) custom-call(bf16[1024,384]{1,0:T(8,128)(2,1)S(1)} %convolution_convert_fusion.7.qkv_ref, s32[1024,1]{1,0:T(8,128)S(1)} %copy.67.seg_col_ref, s32[1,1024]{1,0:T(1,128)S(1)} %copy-done.2, f32[2,2048]{1,0:T(2,128)S(1)} %convolution_bitcast_fusion.vec_ref), custom_call_target="tpu_custom_call" | custom-call | flops 1073741824 | bytes 8388608 | tf_op jit(solution)/shard_map/attend/pallas_call | solution.py:83
  89.2 3.2 copy-done
  93.3 3.4 all-to-all-start
  96.8 35.3 %all-gather.8.cloned.1.call-done = bf16[512,1472]{1,0:T(8,128)(2,1)} async-done(((bf16[16,1472]{1,0:T(8,128)(2,1)}), bf16[512,1472]{1,0:T(8,128)(2,1)}) %all-gather.8.cloned.1.call-update) | async-done | bytes 1507344 | tf_op jit(solution)/shard_map/all_gather | solution.py:410
  132.1 2.2 multiply_reduce_fusion.3
  136.3 11.8 %multiply_reduce_fusion.1 = (f32[]{:T(128)}, bf16[1472,896]{1,0:T(8,128)(2,1)}, bf16[1472,896]{1,0:T(8,128)(2,1)}, f32[]{:T(128)}) fusion(f32[1472,896]{1,0:T(8,128)} %param.25, f32[1472,896]{1,0:T(8,128)} %param.24), kind=kLoop, calls=%fused_computation.26 | loop fusion | flops 7913470 | bytes 15826952 | tf_op jit(solution)/shard_map/reduce_sum | solution.py:343
  148.1 47.8 %all-gather.10.cloned.1.call-done = bf16[1024,1472]{0,1:T(8,128)(2,1)} async-done(((bf16[256,1472]{0,1:T(8,128)(2,1)}), bf16[1024,1472]{0,1:T(8,128)(2,1)}) %all-gather.10.cloned.1.call-update) | async-done | bytes 3014672 | tf_op jit(solution)/shard_map/all_gather | solution.py:261
  196.0 11.5 %fusion.22 = f32[1024,1792]{1,0:T(8,128)} fusion(bf16[1024,1472]{0,1:T(8,128)(2,1)} %all-gather.10.cloned.1.call-done, bf16[1472,896]{1,0:T(8,128)(2,1)} %get-tuple-element.230, bf16[1472,896]{1,0:T(8,128)(2,1)} %get-tuple-element.272), kind=kOutput, calls=%fused_computation.43 | convolution fusion | flops 5412814848 | bytes 15630336 | tf_op jit(solution)/shard_map/dot_general | solution.py:28
  207.4 49.5 %all-gather.12.cloned.1.call-done = bf16[1,1024,1472]{1,2,0:T(8,128)(2,1)} async-done(((bf16[1,256,1472]{1,2,0:T(8,128)(2,1)}), bf16[1,1024,1472]{1,2,0:T(8,128)(2,1)}) %all-gather.12.cloned.1.call-update) | async-done | bytes 3014672 | tf_op jit(solution)/shard_map/all_gather | solution.py:262
  256.9 13.1 %fusion.21 = (bf16[1024,896]{1,0:T(8,128)(2,1)S(1)}, bf16[1024,896]{1,0:T(8,128)(2,1)S(1)}, bf16[1024,896]{1,0:T(8,128)(2,1)}) fusion(f32[1024,1792]{1,0:T(8,128)} %fusion.22, f32[896,1472]{0,1:T(8,128)} %param.26, bf16[1,1024,1472]{1,2,0:T(8,128)(2,1)} %all-gather.12.cloned.1.call-done), kind=kOutput, calls=%fused_computation.37 | convolution fusion | flops 2726305792 | bytes 21135360 | tf_op jit(solution)/shard_map/dot_general | solution.py:38
  271.9 7.0 convolution_convert_fusion.2
  279.1 8.0 %convolution_convert_fusion.3 = bf16[1024,1472]{0,1:T(8,128)(2,1)} fusion(bf16[1024,896]{1,0:T(8,128)(2,1)} %get-tuple-element.228, f32[896,1472]{0,1:T(8,128)} %param.26), kind=kOutput, calls=%fused_computation.30 | convolution fusion | flops 2703958016 | bytes 10125312 | tf_op jit(solution)/shard_map/dot_general | solution.py:28
  287.2 48.3 %reduce-scatter.9.cloned.1.call-done = bf16[256,1472]{0,1:T(8,128)(2,1)} async-done(((bf16[1024,1472]{0,1:T(8,128)(2,1)}), bf16[256,1472]{0,1:T(8,128)(2,1)}) %reduce-scatter.9.cloned.1.call-update) | async-done | bytes 753680 | tf_op jit(solution)/shard_map/reduce_scatter | solution.py:279
  335.4 1.8 fusion.33
  337.3 59.1 %reduce-scatter.7.cloned.1.call-done = bf16[256,1472]{0,1:T(8,128)(2,1)} async-done(((bf16[1024,1472]{0,1:T(8,128)(2,1)}), bf16[256,1472]{0,1:T(8,128)(2,1)}) %reduce-scatter.7.cloned.1.call-update) | async-done | bytes 753680 | tf_op jit(solution)/shard_map/reduce_scatter | solution.py:268
  396.4 3.2 fusion.35
  399.6 1.7 convolution_convert_fusion.5
  401.3 2.6 copy.78
  404.0 2.0 fusion.42
  406.1 19.7 %all_to_all.10 = bf16[4,256,128]{2,1,0:T(8,128)(2,1)S(1)} all-to-all(bf16[4,256,128]{2,1,0:T(8,128)(2,1)S(1)} %bitcast.81), channel_id=1, replica_groups=mesh['dp'=8,'mp'=4] {'mp'}, dimensions={0} | all-to-all | bytes 524288 | tf_op jit(solution)/shard_map/all_to_all | solution.py:203
  425.8 3.4 copy-done.1
  429.2 11.5 %attend_back.1 = (bf16[1024,384]{1,0:T(8,128)(2,1)S(1)}, f32[2,2048]{1,0:T(2,128)S(1)}) custom-call(bf16[1024,384]{1,0:T(8,128)(2,1)S(1)} %convolution_convert_fusion.7.qkv_ref, bf16[1024,128]{1,0:T(8,128)(2,1)S(1)} %bitcast.72, f32[2,1024,1024]{2,1,0:T(8,128)S(1)} %copy-done.1), custom_call_target="tpu_custom_call" | custom-call | flops 2147483648 | bytes 8388608 | tf_op jit(solution)/shard_map/attend_back/pallas_call | solution.py:160
  440.7 3.4 convolution_convert_fusion.1
  444.4 7.4 %convolution_convert_fusion.4 = bf16[896,1472]{0,1:T(8,128)(2,1)} fusion(bf16[1024,896]{1,0:T(8,128)(2,1)} %get-tuple-element.228, bf16[1,1024,1472]{1,2,0:T(8,128)(2,1)} %all-gather.12.cloned.1.call-done), kind=kOutput, calls=%fused_computation.41 | convolution fusion | flops 2702450688 | bytes 7487488 | tf_op jit(solution)/shard_map/dot_general | solution.py:32
  451.8 5.8 convolution_convert_fusion
  457.7 2.8 fusion.82
  460.7 2.8 convolution_convert_fusion.6
  463.5 1.9 copy.79
  469.3 1.9 multiply_reduce_fusion.7
  471.2 1.9 multiply_reduce_fusion.6
  474.8 4.6 multiply_reduce_fusion
  480.0 24.0 %reduce-scatter.11.cloned.1.call-done = bf16[256,1472]{0,1:T(8,128)(2,1)} async-done(((bf16[1024,1472]{0,1:T(8,128)(2,1)}), bf16[256,1472]{0,1:T(8,128)(2,1)}) %reduce-scatter.11.cloned.1.call-update) | async-done | bytes 753680 | tf_op jit(solution)/shard_map/reduce_scatter | solution.py:294
  504.1 2.0 fusion.34
  506.1 25.2 %psum.50 = f32[3008]{0:T(1024)S(1)} all-reduce(f32[3008]{0:T(1024)S(1)} %concatenate.20), channel_id=1, replica_groups=mesh['dp'=8,'mp'=4] {'dp'}, use_global_device_ids=true, to_apply=%region_14.15 | all-reduce | flops 3008 | bytes 24064 | tf_op jit(solution)/shard_map/psum | solution.py:312
  532.7 2.5 fusion.50
  535.1 114.5 %all-reduce.4.cloned.1.call-done = (bf16[1472,384]{1,0:T(8,128)(2,1)}, bf16[1472,896]{1,0:T(8,128)(2,1)}, bf16[1472,896]{1,0:T(8,128)(2,1)}, bf16[128,1472]{0,1:T(8,128)(2,1)}, bf16[896,1472]{0,1:T(8,128)(2,1)}) async-done(((bf16[1472,384]{1,0:T(8,128)(2,1)}, bf16[1472,896]{1,0:T(8,128)(2,1)}, bf16[1472,896]{1,0:T(8,128)(2,1)}, bf16[128,1472]{0,1:T(8,128)(2,1)}, bf16[896,1472]{0,1:T(8,128)(2,1)}), ...) | async-done | bytes 9420816 | tf_op jit(solution)/shard_map/psum | solution.py:308
  652.4 1.7 fusion.11
  654.1 1.7 fusion.6
  655.7 1.8 fusion.1
  658.2 6.0 concatenate.21
  664.2 19.8 %psum.55 = f32[13288]{0:T(1024)S(1)} all-reduce(f32[13288]{0:T(1024)S(1)} %concatenate.21), channel_id=1, replica_groups=mesh['dp'=8,'mp'=4] {'mp'}, use_global_device_ids=true, to_apply=%region_33.34 | all-reduce | flops 13288 | bytes 106304 | tf_op jit(solution)/shard_map/psum | solution.py:345
  708.1 6.6 fusion.14
  715.5 3.5 fusion.9
  720.7 3.1 fusion.4
  726.2 2.0 multiply_subtract_fusion
  (156 shorter events, 36.1 us)
Async XLA Ops:
  7.2 4.2 copy-start.11
  7.2 5.2 copy-start.2
  7.2 5.5 copy-start.30
  7.2 5.8 copy-start.31
  7.2 67.9 %all-gather.6.cloned.1.call-start = ((), (), s32[]{:S(2)}) async-start(), calls=%async_computation.6 | async-start | bytes 3768320 | tf_op jit(solution)/shard_map/all_gather | solution.py:254
  8.7 66.5 %copy-start.13 = (f32[1472,128]{1,0:T(8,128)S(1)}, f32[1472,128]{1,0:T(8,128)}, u32[]{:S(2)}) copy-start(f32[1472,128]{1,0:T(8,128)} %param.20) | copy-start | bytes 2260996
  11.1 121.0 %all-gather.8.cloned.1.call-start = ((), (), s32[]{:S(2)}) async-start(), calls=%async_computation.7 | async-start | bytes 1622016 | tf_op jit(solution)/shard_map/all_gather | solution.py:410
  13.1 62.1 %copy-start.25 = (pred[2047,32]{1,0:T(8,128)(4,1)}, pred[2047,32]{1,0:T(8,128)(4,1)S(1)}, u32[]{:S(2)}) copy-start(pred[2047,32]{1,0:T(8,128)(4,1)S(1)} %iota_compare_fusion) | copy-start | bytes 196516
  79.3 52.8 %copy-start.4 = (bf16[1,256,1472]{1,2,0:T(8,128)(2,1)S(1)}, bf16[1,256,1472]{1,2,0:T(8,128)(2,1)}, u32[]{:S(2)}) copy-start(bf16[1,256,1472]{1,2,0:T(8,128)(2,1)} %param.14) | copy-start | bytes 2260996
  89.2 3.2 copy-start
  92.4 41.9 %copy-start.27 = (f32[1472]{0:T(1024)S(1)}, f32[1472]{0:T(1024)}, u32[]{:S(2)}) copy-start(f32[1472]{0:T(1024)} %param.23) | copy-start | bytes 17668
  93.3 38.8 %all-to-all-start = ((bf16[4,256,128]{1,2,0:T(8,128)(2,1)}), bf16[4,256,128]{1,2,0:T(8,128)(2,1)S(1)}, u32[]{:S(2)}, u32[]{:S(2)}) async-start(bf16[4,256,128]{1,2,0:T(8,128)(2,1)} %copy.68), calls=%async_computation | async-start | bytes 524288 | tf_op jit(solution)/shard_map/all_to_all | solution.py:195
  96.7 99.3 %all-gather.10.cloned.1.call-start = ((), (), s32[]{:S(2)}) async-start(), calls=%async_computation.8 | async-start | bytes 3768320 | tf_op jit(solution)/shard_map/all_gather | solution.py:261
  134.3 201.2 %copy-start.3 = (f32[256,1472]{0,1:T(8,128)}, f32[256,1472]{0,1:T(8,128)S(1)}, u32[]{:S(2)}) copy-start(f32[256,1472]{0,1:T(8,128)S(1)} %get-tuple-element.271) | copy-start | bytes 4521988
  135.7 121.2 %all-gather.12.cloned.1.call-start = ((), (), s32[]{:S(2)}) async-start(), calls=%async_computation.12 | async-start | bytes 3768320 | tf_op jit(solution)/shard_map/all_gather | solution.py:262
  136.2 199.2 %reduce-scatter.9.cloned.1.call-start = ((), (), s32[]{:S(2)}) async-start(), calls=%async_computation.10 | async-start | bytes 3768320 | tf_op jit(solution)/shard_map/reduce_scatter | solution.py:279
  256.9 15.0 %copy-start.22 = (bf16[1472,896]{1,0:T(8,128)(2,1)S(1)}, bf16[1472,896]{1,0:T(8,128)(2,1)}, u32[]{:S(2)}) copy-start(bf16[1472,896]{1,0:T(8,128)(2,1)} %get-tuple-element.230) | copy-start | bytes 7913476
  256.9 15.0 %copy-start.23 = (bf16[1472,896]{1,0:T(8,128)(2,1)S(1)}, bf16[1472,896]{1,0:T(8,128)(2,1)}, u32[]{:S(2)}) copy-start(bf16[1472,896]{1,0:T(8,128)(2,1)} %get-tuple-element.272) | copy-start | bytes 7913476
  278.9 117.5 %reduce-scatter.7.cloned.1.call-start = ((), (), s32[]{:S(2)}) async-start(), calls=%async_computation.9 | async-start | bytes 3768320 | tf_op jit(solution)/shard_map/reduce_scatter | solution.py:268
  287.1 109.3 %copy-start.21 = (bf16[1,256,1472]{1,2,0:T(8,128)(2,1)S(1)}, bf16[1,256,1472]{1,2,0:T(8,128)(2,1)}, u32[]{:S(2)}) copy-start(bf16[1,256,1472]{1,2,0:T(8,128)(2,1)} %param.27) | copy-start | bytes 2260996
  287.1 176.3 %reduce-scatter.13.cloned.1.call-start = ((), (), s32[]{:S(2)}) async-start(), calls=%async_computation.13 | async-start | bytes 1966080
  403.9 100.1 %reduce-scatter.11.cloned.1.call-start = ((), (), s32[]{:S(2)}) async-start(), calls=%async_computation.11 | async-start | bytes 3768320 | tf_op jit(solution)/shard_map/reduce_scatter | solution.py:294
  425.8 3.4 copy-start.1
  429.2 11.5 %copy-start.14 = (f32[1472,128]{1,0:T(8,128)S(1)}, f32[1472,128]{1,0:T(8,128)}, u32[]{:S(2)}) copy-start(f32[1472,128]{1,0:T(8,128)} %param.20) | copy-start | bytes 2260996
  429.2 11.5 %copy-start.17 = (f32[1472,128]{1,0:T(8,128)S(1)}, f32[1472,128]{1,0:T(8,128)}, u32[]{:S(2)}) copy-start(f32[1472,128]{1,0:T(8,128)} %param.19) | copy-start | bytes 2260996
  429.2 11.5 %copy-start.19 = (f32[1472,128]{1,0:T(8,128)S(1)}, f32[1472,128]{1,0:T(8,128)}, u32[]{:S(2)}) copy-start(f32[1472,128]{1,0:T(8,128)} %param.18) | copy-start | bytes 2260996
  444.1 205.6 %all-reduce.4.cloned.1.call-start = ((), (), s32[]{:S(2)}) async-start(), calls=%async_computation.14 | async-start | bytes 18841600 | tf_op jit(solution)/shard_map/psum | solution.py:308
  444.4 7.4 %copy-start.34 = (bf16[1024,1472]{0,1:T(8,128)(2,1)S(1)}, bf16[1024,1472]{0,1:T(8,128)(2,1)}, u32[]{:S(2)}) copy-start(bf16[1024,1472]{0,1:T(8,128)(2,1)} %all-gather.10.cloned.1.call-done) | copy-start | bytes 9043972
  444.4 7.4 %copy-start.36 = (bf16[1024,896]{1,0:T(8,128)(2,1)S(1)}, bf16[1024,896]{1,0:T(8,128)(2,1)}, u32[]{:S(2)}) copy-start(bf16[1024,896]{1,0:T(8,128)(2,1)} %copy-done.35) | copy-start | bytes 5505028
  444.4 7.4 %copy-start.38 = (bf16[1024,896]{1,0:T(8,128)(2,1)S(1)}, bf16[1024,896]{1,0:T(8,128)(2,1)}, u32[]{:S(2)}) copy-start(bf16[1024,896]{1,0:T(8,128)(2,1)} %copy-done.37) | copy-start | bytes 5505028
  457.7 3.0 copy-start.33
  465.4 7.8 %copy-start.15 = (f32[1472,128]{1,0:T(8,128)S(1)}, f32[1472,128]{1,0:T(8,128)}, u32[]{:S(2)}) copy-start(f32[1472,128]{1,0:T(8,128)} %param.20) | copy-start | bytes 2260996
  465.4 8.5 %copy-start.12 = (f32[128,1472]{0,1:T(8,128)S(1)}, f32[128,1472]{0,1:T(8,128)}, u32[]{:S(2)}) copy-start(f32[128,1472]{0,1:T(8,128)} %param.21) | copy-start | bytes 2260996
  474.7 4.6 copy-start.26
  474.7 29.3 %copy-start.5 = (bf16[1,256,1472]{1,2,0:T(8,128)(2,1)S(1)}, bf16[1,256,1472]{1,2,0:T(8,128)(2,1)}, u32[]{:S(2)}) copy-start(bf16[1,256,1472]{1,2,0:T(8,128)(2,1)} %param.14) | copy-start | bytes 2260996
  652.4 3.3 copy-start.6
  654.1 3.4 copy-start.24
  654.1 45.9 %copy-start.29 = (f32[32,2]{1,0:T(8,128)S(1)}, f32[32,2]{1,0:T(8,128)}, u32[]{:S(2)}) copy-start(f32[32,2]{1,0:T(8,128)} %copy.74) | copy-start | bytes 772
  708.1 7.3 slice-start
  708.1 7.3 slice-start.1
  708.1 7.3 copy-start.9
  715.4 3.5 slice-start.2
  715.4 4.3 slice-start.3
  715.4 5.2 copy-start.7
  720.7 3.2 copy-start.32
  720.7 5.5 copy-start.16
  720.7 5.5 copy-start.18
  720.7 5.5 copy-start.20
  (5 other events, 10.8 us)
Sparse Core Ops, SparseCore 0:
  11.2 63.9 all-gather.5
  78.6 53.4 all-gather.7
  135.8 60.1 all-gather.9
  197.4 59.4 all-gather.11
  279.0 56.4 reduce-scatter.8
  338.2 58.1 reduce-scatter.6
  404.1 39.5 reduce-scatter.12
  446.5 57.5 reduce-scatter.10
  510.1 139.5 all-reduce.3

commit v2 on v1

--- a/solution.py
+++ b/solution.py
@@ -186,6 +186,592 @@
         ),
         name="attend_back",
     )(qkv, grad, probs)
+
+
+class Butterfly:
+    def __init__(self, order, base):
+        self.order = order
+        self.me = lax.axis_index("dp")
+        self.line = lax.axis_index("mp")
+        self.base = base
+        self.offsets = []
+        total = 0
+        for s in range(len(order)):
+            self.offsets.append(total)
+            total += 1 << (len(order) - 1 - s)
+        self.count = total
+
+    def bit(self, b):
+        return (self.me // b) % 2
+
+    def partner(self, s):
+        b = self.order[s]
+        return (self.me + b * (1 - 2 * self.bit(b)), self.line)
+
+    def pieces(self, s):
+        b = self.order[s]
+        fixed = sum(k * self.bit(k) for k in self.order[:s])
+        free = self.order[s + 1 :]
+        found = []
+        for j in range(1 << len(free)):
+            rest = sum(k for i, k in enumerate(free) if (j >> i) & 1)
+            found.append((fixed + b * self.bit(b) + rest, fixed + b * (1 - self.bit(b)) + rest, j))
+        return found
+
+    def copy(self, src, dst, sems, slot, s):
+        return pltpu.make_async_remote_copy(
+            src_ref=src,
+            dst_ref=dst,
+            send_sem=sems[0].at[self.base + slot],
+            recv_sem=sems[1].at[self.base + slot],
+            device_id=self.partner(s),
+            device_id_type=pl.DeviceIdType.MESH,
+        )
+
+    def halve(self, s, source, landing, sems):
+        at = self.offsets[s]
+        return [
+            self.copy(source.at[theirs], landing.at[at + j], sems, at + j, s)
+            for _, theirs, j in self.pieces(s)
+        ]
+
+    def add(self, s, kept, landing, copies):
+        at = self.offsets[s]
+        for (mine, _, j), copy in zip(self.pieces(s), copies):
+            copy.wait_recv()
+            kept[mine] = (
+                kept[mine].astype(jnp.float32) + landing[at + j].astype(jnp.float32)
+            ).astype(jnp.bfloat16)
+
+    def double(self, s, whole, sems, first=None):
+        at = self.offsets[s]
+        return [
+            self.copy(whole.at[mine] if first is None else first, whole.at[mine], sems, at + j, s)
+            for mine, _, j in self.pieces(s)
+        ]
+
+
+def orders(data_count):
+    bits = [1 << i for i in range(data_count.bit_length() - 1)]
+    return (bits, bits[:1] + bits[:0:-1])
+
+
+def greet(peers):
+    barrier = pltpu.get_barrier_semaphore()
+    for peer in peers:
+        pl.semaphore_signal(barrier, inc=1, device_id=peer, device_id_type=pl.DeviceIdType.MESH)
+    pl.semaphore_wait(barrier, len(peers))
+
+
+def sum_weights_kernel(data_count, count, layout, *refs):
+    n = len(layout)
+    sources, wholes = refs[:n], refs[n : 2 * n]
+    kept, landings = refs[2 * n : 3 * n], refs[3 * n : 4 * n]
+    cross, final, load_sem, keep_sem, down_send, down_recv, up_send, up_recv, cross_send, cross_recv = refs[
+        4 * n :
+    ]
+    me = lax.axis_index("dp")
+    place = lax.axis_index("mp")
+    ways = orders(data_count)
+    span = data_count - 1
+    flies = [Butterfly(ways[way], i * span) for i, (way, _) in enumerate(layout)]
+    stages = len(ways[0])
+    down = (down_send, down_recv)
+    up = (up_send, up_recv)
+    loads = []
+    for i, fly in enumerate(flies):
+        for mine, _, j in fly.pieces(0):
+            load = pltpu.make_async_copy(
+                sources[i].at[mine], kept[i].at[mine], load_sem.at[i * data_count + j]
+            )
+            load.start()
+            loads.append(load)
+    others = [(place + k) % count for k in range(1, count)]
+    greet([flies[0].partner(s) for s in range(stages)] + [(me, other) for other in others])
+
+    sent = []
+
+    def start(copies):
+        for copy in copies:
+            copy.start()
+        sent.extend(copies)
+        return copies
+
+    flights = [start(fly.halve(0, sources[i], landings[i], down)) for i, fly in enumerate(flies)]
+    for load in loads:
+        load.wait()
+    for s in range(stages):
+        for i, fly in enumerate(flies):
+            fly.add(s, kept[i], landings[i], flights[i])
+            if s + 1 < stages:
+                flights[i] = start(fly.halve(s + 1, kept[i], landings[i], down))
+                continue
+            if layout[i][1]:
+                crossing = []
+                for k, other in enumerate(others):
+                    crossing.append(
+                        pltpu.make_async_remote_copy(
+                            src_ref=kept[i].at[me, other],
+                            dst_ref=cross.at[count - 2 - k],
+                            send_sem=cross_send.at[k],
+                            recv_sem=cross_recv.at[count - 2 - k],
+                            device_id=(me, other),
+                            device_id_type=pl.DeviceIdType.MESH,
+                        )
+                    )
+                start(crossing)
+                total = kept[i][me, place].astype(jnp.float32)
+                for k in range(count - 1):
+                    pltpu.make_async_remote_copy(
+                        src_ref=cross.at[k],
+                        dst_ref=cross.at[k],
+                        send_sem=cross_send.at[k],
+                        recv_sem=cross_recv.at[k],
+                        device_id=(me, others[0]),
+                        device_id_type=pl.DeviceIdType.MESH,
+                    ).wait_recv()
+                    total = total + cross[k].astype(jnp.float32)
+                final[...] = total.astype(jnp.bfloat16)
+                mine = final
+            else:
+                mine = kept[i].at[me]
+            keep = pltpu.make_async_copy(mine, wholes[i].at[me], keep_sem.at[i])
+            keep.start()
+            flights[i] = (keep, start(fly.double(s, wholes[i], up, mine)))
+    keeps = [keep for keep, _ in flights]
+    flights = [copies for _, copies in flights]
+    for keep in keeps:
+        keep.wait()
+    for s in reversed(range(stages)):
+        for i, fly in enumerate(flies):
+            for copy in flights[i]:
+                copy.wait_recv()
+            if s > 0:
+                flights[i] = start(fly.double(s - 1, wholes[i], up))
+    for copy in sent:
+        copy.wait_send()
+
+
+def sum_weights(arrays, layout):
+    count = lax.axis_size("mp")
+    data_count = arrays[0].shape[0]
+    anywhere = pl.BlockSpec(memory_space=pl.ANY)
+    dma = pltpu.SemaphoreType.DMA
+    low = jnp.bfloat16
+    shapes = [a.shape[1:] for a in arrays]
+    kept_shapes = [(s[1:] if crosses else s) for s, (_, crosses) in zip(shapes, layout)]
+    crossing = [s for s, (_, crosses) in zip(kept_shapes, layout) if crosses][0]
+    span = data_count - 1
+    n = len(arrays)
+    moved = 4 * sum(a.size for a in arrays)
+    return pl.pallas_call(
+        functools.partial(sum_weights_kernel, data_count, count, layout),
+        out_shape=[jax.ShapeDtypeStruct((data_count, *s), low) for s in kept_shapes],
+        in_specs=[anywhere] * n,
+        out_specs=[anywhere] * n,
+        scratch_shapes=[pltpu.VMEM((data_count, *s), low) for s in shapes]
+        + [pltpu.VMEM((span, *s), low) for s in shapes]
+        + [
+            pltpu.VMEM((count - 1, *crossing), low),
+            pltpu.VMEM(crossing, low),
+            dma((n * data_count,)),
+            dma((n,)),
+            dma((n * span,)),
+            dma((n * span,)),
+            dma((n * span,)),
+            dma((n * span,)),
+            dma((count - 1,)),
+            dma((count - 1,)),
+        ],
+        compiler_params=pltpu.CompilerParams(
+            collective_id=2, has_side_effects=True, vmem_limit_bytes=48 << 20
+        ),
+        cost_estimate=pl.CostEstimate(flops=moved, bytes_accessed=moved, transcendentals=0),
+        name="sum_weights",
+    )(*arrays)
+
+
+def gather_proj_kernel(data_count, count, own_ref, all_ref, load_sem, cross_send, cross_recv, side_send, side_recv):
+    me = lax.axis_index("dp")
+    place = lax.axis_index("mp")
+    others = [(place + k) % count for k in range(1, count)]
+    peers = [(me + k) % data_count for k in range(1, data_count)]
+    load = pltpu.make_async_copy(own_ref, all_ref.at[place], load_sem)
+    load.start()
+    greet([(me, other) for other in others] + [(peer, place) for peer in peers])
+    sent = []
+    for k, other in enumerate(others):
+        copy = pltpu.make_async_remote_copy(
+            src_ref=own_ref.at[me],
+            dst_ref=all_ref.at[place, me],
+            send_sem=cross_send.at[k],
+            recv_sem=cross_recv.at[count - 2 - k],
+            device_id=(me, other),
+            device_id_type=pl.DeviceIdType.MESH,
+        )
+        copy.start()
+        sent.append(copy)
+    arrivals = []
+    for k, other in enumerate(others):
+        pltpu.make_async_remote_copy(
+            src_ref=own_ref.at[me],
+            dst_ref=all_ref.at[other, me],
+            send_sem=cross_send.at[k],
+            recv_sem=cross_recv.at[k],
+            device_id=(me, other),
+            device_id_type=pl.DeviceIdType.MESH,
+        ).wait_recv()
+        for j, peer in enumerate(peers):
+            slot = k * (data_count - 1)
+            copy = pltpu.make_async_remote_copy(
+                src_ref=all_ref.at[other, me],
+                dst_ref=all_ref.at[other, me],
+                send_sem=side_send.at[slot + j],
+                recv_sem=side_recv.at[slot + data_count - 2 - j],
+                device_id=(peer, place),
+                device_id_type=pl.DeviceIdType.MESH,
+            )
+            copy.start()
+            sent.append(copy)
+            arrivals.append(
+                pltpu.make_async_remote_copy(
+                    src_ref=all_ref.at[other, peer],
+                    dst_ref=all_ref.at[other, peer],
+                    send_sem=side_send.at[slot + j],
+                    recv_sem=side_recv.at[slot + j],
+                    device_id=(peer, place),
+                    device_id_type=pl.DeviceIdType.MESH,
+                )
+            )
+    for arrival in arrivals:
+        arrival.wait_recv()
+    for copy in sent:
+        copy.wait_send()
+    load.wait()
+
+
+def gather_proj(proj_low):
+    count = lax.axis_size("mp")
+    data_count = lax.axis_size("dp")
+    lanes, width = proj_low.shape
+    part = lanes // data_count
+    anywhere = pl.BlockSpec(memory_space=pl.ANY)
+    dma = pltpu.SemaphoreType.DMA
+    gathered = pl.pallas_call(
+        functools.partial(gather_proj_kernel, data_count, count),
+        out_shape=jax.ShapeDtypeStruct((count, data_count, part, width), proj_low.dtype),
+        in_specs=[anywhere],
+        out_specs=anywhere,
+        scratch_shapes=[
+            dma,
+            dma((count - 1,)),
+            dma((count - 1,)),
+            dma(((count - 1) * (data_count - 1),)),
+            dma(((count - 1) * (data_count - 1),)),
+        ],
+        compiler_params=pltpu.CompilerParams(collective_id=0, has_side_effects=True),
+        cost_estimate=pl.CostEstimate(flops=0, bytes_accessed=50 << 20, transcendentals=0),
+        name="gather_proj",
+    )(proj_low.reshape(data_count, part, width))
+    return gathered.reshape(count * lanes, width)
+
+
+def turn_order(count):
+    return [sorted(range(count), key=lambda b: (abs(b - place), b < place)) for place in range(count)]
+
+
+def look_up(table, row, column):
+    found = jnp.int32(0)
+    for r, entries in enumerate(table):
+        for c, entry in enumerate(entries):
+            found = jnp.where((row == r) & (column == c), jnp.int32(entry), found)
+    return found
+
+
+def feed_forward_kernel(
+    count,
+    parts,
+    normed_hbm,
+    cot_hbm,
+    gate_up_hbm,
+    down_hbm,
+    out_hbm,
+    dn_ref,
+    d_gate_hbm,
+    d_up_hbm,
+    d_down_hbm,
+    normed,
+    cot,
+    gate_up,
+    down,
+    hidden,
+    d_gate_up,
+    outgoing,
+    incoming,
+    stage,
+    d_wide,
+    d_tall,
+    load_sem,
+    stage_sem,
+    gather_send,
+    gather_recv,
+    sum_send,
+    sum_recv,
+):
+    place = lax.axis_index("mp")
+    row = lax.axis_index("dp")
+    block_len, width = dn_ref.shape
+    units = down.shape[0]
+    part_len = block_len // parts
+    last = count - 1
+    has_left = place > 0
+    has_right = place < last
+
+    loads = [
+        pltpu.make_async_copy(normed_hbm, normed.at[place], load_sem.at[0]),
+        pltpu.make_async_copy(gate_up_hbm, gate_up, load_sem.at[1]),
+        pltpu.make_async_copy(down_hbm, down, load_sem.at[2]),
+        pltpu.make_async_copy(cot_hbm, cot, load_sem.at[3]),
+    ]
+    for load in loads:
+        load.start()
+
+    barrier = pltpu.get_barrier_semaphore()
+    for side, there in ((-1, has_left), (1, has_right)):
+
+        @pl.when(there)
+        def _():
+            pl.semaphore_signal(
+                barrier, inc=1, device_id=(row, place + side), device_id_type=pl.DeviceIdType.MESH
+            )
+
+    pl.semaphore_wait(barrier, has_left.astype(jnp.int32) + has_right.astype(jnp.int32))
+
+    def pass_block(block, side, slot):
+        return pltpu.make_async_remote_copy(
+            src_ref=normed.at[block],
+            dst_ref=normed.at[block],
+            send_sem=gather_send.at[slot],
+            recv_sem=gather_recv.at[block],
+            device_id=(row, place + side),
+            device_id_type=pl.DeviceIdType.MESH,
+        )
+
+    def rows_of(part):
+        return pl.ds(pl.multiple_of(part * part_len, part_len), part_len)
+
+    def pass_sum(block, part, side, slot):
+        return pltpu.make_async_remote_copy(
+            src_ref=outgoing.at[block, rows_of(part)],
+            dst_ref=incoming.at[slot, rows_of(part)],
+            send_sem=sum_send.at[block, part],
+            recv_sem=sum_recv.at[slot, part],
+            device_id=(row, place + side),
+            device_id_type=pl.DeviceIdType.MESH,
+        )
+
+    def landing(block, side):
+        return jnp.where((side == -1) & (place + side == block), count, block)
+
+    loads[0].wait()
+    for side, there in ((-1, has_left), (1, has_right)):
+
+        @pl.when(there)
+        def _():
+            pass_block(place, side, count + (side + 1) // 2).start()
+
+    for load in loads[1:]:
+        load.wait()
+
+    def store_out(turn, block):
+        return pltpu.make_async_copy(stage.at[turn % 2], out_hbm.at[block], stage_sem.at[turn % 2])
+
+    table = turn_order(count)
+    root = 0.7978845608028654
+
+    def turn_body(turn, carry):
+        block = look_up(table, place, turn)
+        distance = jnp.abs(block - place)
+
+        @pl.when((distance > 0) & ((block > place) | (place + distance > last)))
+        def _():
+            for side in (1, -1):
+                other = place + side * distance
+
+                @pl.when((other >= 0) & (other <= last))
+                def _():
+                    pass_block(other, 0, other).wait_recv()
+
+                    @pl.when((place - side >= 0) & (place - side <= last))
+                    def _():
+                        pass_block(other, -side, other).start()
+
+        acts = product(normed[block], gate_up[...])
+        gate_act = acts[:, :units]
+        up_act = acts[:, units:]
+        squared = gate_act * gate_act
+        bend = jnp.tanh(root * gate_act * (1.0 + 0.044715 * squared))
+        half = 0.5 * (1.0 + bend)
+        gelu = gate_act * half
+        hidden[block] = (gelu * up_act).astype(jnp.bfloat16)
+        d_hidden = right_inner(cot[block], down[...])
+        slope = half + 0.5 * gate_act * (1.0 - bend * bend) * (root * (1.0 + 0.134145 * squared))
+        d_gate_up[block, :, :units] = (d_hidden * up_act * slope).astype(jnp.bfloat16)
+        d_gate_up[block, :, units:] = (d_hidden * gelu).astype(jnp.bfloat16)
+        term = right_inner(d_gate_up[block], gate_up[...])
+
+        @pl.when(block == place)
+        def _():
+            dn_ref[...] = term
+
+        @pl.when(block != place)
+        def _():
+            outgoing[block] = term.astype(jnp.bfloat16)
+
+        for side, is_end in ((1, place == 0), (-1, place == last)):
+
+            @pl.when(is_end & (block != place))
+            def _():
+                for part in range(parts):
+                    pass_sum(block, part, side, landing(block, side)).start()
+
+        @pl.when(turn >= 2)
+        def _():
+            store_out(turn, block).wait()
+
+        stage[turn % 2] = product(hidden[block], down[...]).astype(jnp.bfloat16)
+        store_out(turn, block).start()
+        return carry
+
+    lax.fori_loop(0, count, turn_body, 0)
+
+    def relay(key):
+        def relay_part(part, carry):
+            for side, block in ((1, key), (-1, last - key)):
+                through = (block > place) & has_left if side == 1 else (block < place) & has_right
+
+                @pl.when(through)
+                def _():
+                    pass_sum(block, part, side, block).wait_recv()
+                    rows = rows_of(part)
+                    outgoing[block, rows] = (
+                        outgoing[block, rows].astype(jnp.float32)
+                        + incoming[block, rows].astype(jnp.float32)
+                    ).astype(jnp.bfloat16)
+                    pass_sum(block, part, side, landing(block, side)).start()
+
+            return carry
+
+        lax.fori_loop(0, parts, relay_part, 0)
+
+    def flat(ref):
+        return ref[...].reshape(count * block_len, ref.shape[2])
+
+    d_wide[:, width:] = jnp.zeros((2, d_wide.shape[1] - width, units), jnp.bfloat16)
+    d_tall[...] = left_inner(flat(hidden), flat(cot)).astype(jnp.bfloat16)
+    save_down = pltpu.make_async_copy(d_tall, d_down_hbm, load_sem.at[2])
+    save_down.start()
+    for key in range(1, last):
+        relay(key)
+    d_wide[0, :width] = left_inner(
+        flat(normed), d_gate_up[:, :, :units].reshape(count * block_len, units)
+    ).astype(jnp.bfloat16)
+    save_gate = pltpu.make_async_copy(d_wide.at[0], d_gate_hbm, load_sem.at[0])
+    save_gate.start()
+    relay(last)
+    d_wide[1, :width] = left_inner(
+        flat(normed), d_gate_up[:, :, units:].reshape(count * block_len, units)
+    ).astype(jnp.bfloat16)
+    save_up = pltpu.make_async_copy(d_wide.at[1], d_up_hbm, load_sem.at[1])
+    save_up.start()
+
+    for side, there in ((1, has_left), (-1, has_right)):
+
+        @pl.when(there)
+        def _():
+            slot = place if side == 1 else count
+
+            def add_part(part, carry):
+                pass_sum(place, part, side, slot).wait_recv()
+                rows = rows_of(part)
+                dn_ref[rows] += incoming[slot, rows].astype(jnp.float32)
+                return carry
+
+            lax.fori_loop(0, parts, add_part, 0)
+
+    for side, there in ((-1, has_left), (1, has_right)):
+
+        @pl.when(there)
+        def _():
+            pass_block(place, side, count + (side + 1) // 2).wait_send()
+
+    for block in range(count):
+
+        @pl.when((block != place) & has_left & has_right)
+        def _():
+            pass_block(block, 1, block).wait_send()
+
+        @pl.when(block != place)
+        def _():
+            for part in range(parts):
+                pass_sum(block, part, 1, block).wait_send()
+
+    for turn in (count - 2, count - 1):
+        store_out(turn, 0).wait()
+    for save in (save_down, save_gate, save_up):
+        save.wait()
+
+
+def feed_forward(normed, cot_all, gate_up, down, padded):
+    count = lax.axis_size("mp")
+    block_len, width = normed.shape
+    units = down.shape[0]
+    parts = 4
+    low = jnp.bfloat16
+    anywhere = pl.BlockSpec(memory_space=pl.ANY)
+    dma = pltpu.SemaphoreType.DMA
+    tokens = count * block_len
+    out_terms, dn, d_gate, d_up, d_down = pl.pallas_call(
+        functools.partial(feed_forward_kernel, count, parts),
+        out_shape=[
+            jax.ShapeDtypeStruct((count, block_len, width), low),
+            jax.ShapeDtypeStruct((block_len, width), jnp.float32),
+            jax.ShapeDtypeStruct((padded, units), low),
+            jax.ShapeDtypeStruct((padded, units), low),
+            jax.ShapeDtypeStruct((units, width), low),
+        ],
+        in_specs=[anywhere] * 4,
+        out_specs=[anywhere, pl.BlockSpec(memory_space=pltpu.VMEM), anywhere, anywhere, anywhere],
+        scratch_shapes=[
+            pltpu.VMEM((count, block_len, width), low),
+            pltpu.VMEM((count, block_len, width), low),
+            pltpu.VMEM((width, 2 * units), low),
+            pltpu.VMEM((units, width), low),
+            pltpu.VMEM((count, block_len, units), low),
+            pltpu.VMEM((count, block_len, 2 * units), low),
+            pltpu.VMEM((count, block_len, width), low),
+            pltpu.VMEM((count + 1, block_len, width), low),
+            pltpu.VMEM((2, block_len, width), low),
+            pltpu.VMEM((2, padded, units), low),
+            pltpu.VMEM((units, width), low),
+            dma((4,)),
+            dma((2,)),
+            dma((count + 2,)),
+            dma((count,)),
+            dma((count, parts)),
+            dma((count + 1, parts)),
+        ],
+        compiler_params=pltpu.CompilerParams(
+            collective_id=1, has_side_effects=True, vmem_limit_bytes=60 << 20
+        ),
+        cost_estimate=pl.CostEstimate(
+            flops=18 * tokens * width * units,
+            bytes_accessed=12 * width * units + 6 * tokens * width,
+            transcendentals=tokens * units,
+        ),
+        name="feed_forward",
+    )(normed, cot_all.reshape(count, block_len, width), gate_up, down)
+    return out_terms.reshape(count * block_len, width), dn, d_gate, d_up, d_down
 
 
 def to_owners(rows_of_slots):
@@ -253,51 +839,57 @@
     normed_local = rms_norm(residual_in, attn_gain).astype(jnp.bfloat16)
     flat_norm = lax.all_gather(normed_local, "mp", axis=0, tiled=True)
     proj_all = gather_proj(proj_low)
+    flat_norm, late_cot, proj_all, qkv_low, gate_up_low, down_low, vector = lax.optimization_barrier(
+        (flat_norm, cotangent, proj_all, qkv_low, gate_up_low, down_low, vector)
+    )
+    flat_cot = lax.all_gather(late_cot, "mp", axis=0, tiled=True)
     qkv = product(flat_norm, qkv_low).astype(jnp.bfloat16)
     attended, probs = attend(qkv, segment_ids.reshape(seq_len, 1), segment_ids, vector)
     own_attended = to_owners(attended)
     middle = residual_in + product(own_attended, proj_all)
     normed_ff_local = rms_norm(middle, ff_gain).astype(jnp.bfloat16)
-    flat_ff = lax.all_gather(normed_ff_local, "mp", axis=0, tiled=True)
-    flat_cot = lax.all_gather(cotangent, "mp", axis=0, tiled=True)
-    gate_up = product(flat_ff, gate_up_low)
-    gate_act = gate_up[:, :ff_width]
-    up_act = gate_up[:, ff_width:]
-    hidden = gated_gelu(gate_act, up_act).astype(jnp.bfloat16)
-    ff_terms = product(hidden, down_low)
-    ff_branch = lax.psum_scatter(
-        ff_terms.astype(jnp.bfloat16), "mp", scatter_dimension=0, tiled=True
-    ).astype(jnp.float32)
-    layer_out = (middle + ff_branch).astype(jnp.bfloat16)
-    d_hidden = right_inner(flat_cot, down_low)
-    gate_pull = jax.vjp(gated_gelu, gate_act, up_act)[1]
-    d_gate, d_up = gate_pull(d_hidden)
-    d_gate_up = jnp.concatenate([d_gate, d_up], axis=1).astype(jnp.bfloat16)
-    d_down_w = left_inner(hidden, flat_cot)
-    d_gate_up_w = left_inner(flat_ff, d_gate_up)
-    dn_ff_terms = right_inner(d_gate_up, gate_up_low)
-    dn_ff = lax.psum_scatter(
-        dn_ff_terms.astype(jnp.bfloat16), "mp", scatter_dimension=0, tiled=True
-    ).astype(jnp.float32)
-    d_gate_w = lax.psum(d_gate_up_w[:, :ff_width].astype(jnp.bfloat16), "dp").astype(jnp.float32)
-    d_up_w = lax.psum(d_gate_up_w[:, ff_width:].astype(jnp.bfloat16), "dp").astype(jnp.float32)
-    d_down_w = lax.psum(d_down_w.astype(jnp.bfloat16), "dp").astype(jnp.float32)
+    pad_to = 16 * data_count
+    padded = (model_width + pad_to - 1) // pad_to * pad_to
+    out_terms, dn_ff, d_gate_w, d_up_w, d_down_w = feed_forward(
+        normed_ff_local, flat_cot, gate_up_low, down_low, padded
+    )
     ff_norm_pull = jax.vjp(rms_norm, middle, ff_gain)[1]
     d_middle_norm, d_ff_gain = ff_norm_pull(dn_ff)
     d_middle = cotangent.astype(jnp.float32) + d_middle_norm
     d_attn_local = d_middle.astype(jnp.bfloat16)
     d_attended = to_slots(right_inner(d_attn_local, proj_all).astype(jnp.bfloat16))
+    flat_d_qkv, d_vector = attend_back(qkv, d_attended, probs)
+    dn_attn_terms = right_inner(flat_d_qkv, qkv_low).astype(jnp.bfloat16)
+    out_terms, dn_attn_terms = lax.optimization_barrier((out_terms, dn_attn_terms))
+    dn_attn = lax.psum_scatter(dn_attn_terms, "mp", scatter_dimension=0, tiled=True)
+    ff_branch = lax.psum_scatter(out_terms, "mp", scatter_dimension=0, tiled=True)
+    layer_out = (middle + ff_branch.astype(jnp.float32)).astype(jnp.bfloat16)
+    d_qkv_w = left_inner(flat_norm, flat_d_qkv).astype(jnp.bfloat16)
+    d_qkv_w = jnp.pad(d_qkv_w, ((0, padded - model_width), (0, 0)))
     d_out_w = left_inner(own_attended, d_attn_local).astype(jnp.bfloat16)
-    d_out_w = lax.psum_scatter(d_out_w, "mp", scatter_dimension=0, tiled=True)
-    flat_d_qkv, d_vector = attend_back(qkv, d_attended, probs)
-    dn_attn_terms = right_inner(flat_d_qkv, qkv_low)
-    dn_attn = lax.psum_scatter(
-        dn_attn_terms.astype(jnp.bfloat16), "mp", scatter_dimension=0, tiled=True
-    ).astype(jnp.float32)
+    d_out_w = d_out_w.reshape(tensor_count, data_count, -1, model_width).transpose(1, 0, 2, 3)
+    wide = (data_count, padded // data_count)
+    d_gate_w, d_up_w, d_down_w, d_qkv_w, d_out_w = sum_weights(
+        (
+            d_gate_w.reshape(*wide, ff_width),
+            d_up_w.reshape(*wide, ff_width),
+            d_down_w.reshape(data_count, ff_width // data_count, model_width),
+            d_qkv_w.reshape(*wide, 3 * lane_width),
+            d_out_w,
+        ),
+        ((0, False), (1, False), (0, False), (1, False), (1, True)),
+    )
+
+    def region(pieces):
+        flat = pieces.reshape(-1, pieces.shape[2])
+        return (flat[:model_width] if flat.shape[0] == padded else flat).astype(jnp.float32)
+
+    d_gate_w, d_up_w, d_down_w, d_qkv_w, d_out_w = (
+        region(pieces) for pieces in (d_gate_w, d_up_w, d_down_w, d_qkv_w, d_out_w)
+    )
     attn_norm_pull = jax.vjp(rms_norm, residual_in, attn_gain)[1]
-    d_input_norm, d_attn_gain = attn_norm_pull(dn_attn)
+    d_input_norm, d_attn_gain = attn_norm_pull(dn_attn.astype(jnp.float32))
     input_grad = (d_middle + d_input_norm).astype(jnp.bfloat16)
-    d_qkv_w = left_inner(flat_norm, flat_d_qkv).astype(jnp.bfloat16)
     d_rel = lax.dot_general(
         onehot,
         d_vector,
@@ -305,9 +897,6 @@
         precision=highest,
         preferred_element_type=jnp.float32,
     )
-    d_qkv_w, d_out_w = lax.psum((d_qkv_w, d_out_w), "dp")
-    d_qkv_w = d_qkv_w.astype(jnp.float32)
-    d_out_w = d_out_w.astype(jnp.float32)
     small = jnp.concatenate([d_attn_gain, d_ff_gain, d_rel.reshape(-1)])
     small = lax.psum(small, "dp")
     d_rel = small[2 * model_width :].reshape(BUCKETS, slots_here)
@@ -403,13 +992,6 @@
     )
 
 
-def gather_proj(proj_low):
-    data_count = lax.axis_size("dp")
-    rows = proj_low.shape[0] // data_count
-    part = lax.dynamic_slice_in_dim(proj_low, lax.axis_index("dp") * rows, rows, 0)
-    return lax.all_gather(part, ("mp", "dp"), axis=0, tiled=True)
-
-
 def solution(mesh):
     return jax.shard_map(
         local,

time: 742 us -> 543 us (0.73)
  waiting for transfers between devices: 441 us -> 49.6 us
  Pallas kernels: 21.4 us -> 262 us
  matrix products: 70.1 us -> 13.6 us
  local copies, waits for them, and re-layouts: 28.4 us -> 43.4 us
  other arithmetic: 77.4 us -> 65.1 us
  blocking collectives: 64.7 us -> 73.8 us
    pallas_call x0 -> x3, Pallas kernels: none -> 241 us  [the longest x1 113 us: feed_forward(): pl.pallas_call(functools.partial(feed_forward_kernel, count, parts), out_...]
    reduce_scatter x3 -> x2, waiting for transfers between devices: 131 us -> 0.01 us  [the longest x1 0.01 us: local(): lax.psum_scatter(dn_attn_terms, 'mp', scatter_dimension=0, tiled=True)]
    psum x1 -> x0, waiting for transfers between devices: 115 us -> none  [local(): d_qkv_w, d_out_w = lax.psum((d_qkv_w, d_out_w), 'dp')]
    all_gather x3 -> x1, waiting for transfers between devices: 133 us -> 29 us  [local(): flat_cot = lax.all_gather(late_cot, 'mp', axis=0, tiled=True)]
    all_gather x1, waiting for transfers between devices: 61.6 us -> 20.6 us  [local(): flat_norm = lax.all_gather(normed_local, 'mp', axis=0, tiled=True)]
    dot_general x4 -> x2, matrix products: 25.5 us -> 4.1 us  [right_inner(): lax.dot_general(left_side, right_side, (((1,), (1,)), ((), ())), preferre...]
    dot_general x4 -> x2, matrix products: 25.7 us -> 5.96 us  [product(): return jnp.dot(left_side, right_side, preferred_element_type=jnp.float32)]
    all_to_all x0 -> x1, blocking collectives: none -> 19.4 us  [to_owners(): pieces = lax.all_to_all(pieces, 'mp', split_axis=0, concat_axis=0)]
  transfers between devices with their start and end apart: 10 -> 4, of which waited for: 8 -> 2; matrix products, arithmetic and copies ran while one was open for 12% -> 15% of each run, Pallas kernels for 3% -> 26%
where the time goes in v2:
time: 543 us; the launch traced here: 536 us
  Pallas kernels  262 us (48%)
  blocking collectives  73.8 us (14%)
  other arithmetic  65.1 us (12%)
  waiting for transfers between devices  49.6 us (9%)
  local copies, waits for them, and re-layouts  43.4 us (8%)
  between operations  28.1 us (5%)
  matrix products  13.6 us (3%)
    pallas_call x1, Pallas kernels, feed_forward(): pl.pallas_call(functools.partial(feed_forward_kernel, count, parts), out_...  113 us
    pallas_call x1, Pallas kernels, sum_weights(): pl.pallas_call(functools.partial(sum_weights_kernel, data_count, count, l...  105 us
    all_gather x1, waiting for transfers between devices, local(): flat_cot = lax.all_gather(late_cot, 'mp', axis=0, tiled=True)  29 us
    unnamed x119, local copies, waits for them, and re-layouts  24.8 us
    pallas_call x1, Pallas kernels, gather_proj(): pl.pallas_call(functools.partial(gather_proj_kernel, data_count, count),...  23.4 us
    psum x1, blocking collectives, local(): sums = lax.psum(jnp.concatenate(parts), 'mp')  22.6 us
    psum x1, blocking collectives, local(): small = lax.psum(small, 'dp')  22.3 us
    all_gather x1, waiting for transfers between devices, local(): flat_norm = lax.all_gather(normed_local, 'mp', axis=0, tiled=True)  20.6 us
  transfers between devices with their start and end apart: 4, of which 2 were waited for; matrix products, arithmetic and copies ran while one was open for 15% of the time, Pallas kernels for 26%

profile of v2, /device:TPU:0, one launch (start us, length us, event | category | flops | bytes accessed | tf_op | source)
XLA Modules:
  0.0 535.9 jit_solution(17074221382807241423)
XLA Ops:
  7.3 1.5 copy.58
  9.0 1.1 fusion.15
  11.2 0.9 copy.60
  12.1 23.4 %gather_proj.1 = bf16[4,8,16,1472]{3,2,1,0:T(8,128)(2,1)} custom-call(bf16[8,16,1472]{2,1,0:T(8,128)(2,1)} %bitcast.108), custom_call_target="tpu_custom_call" | custom-call | bytes 52428800 | tf_op jit(solution)/shard_map/gather_proj/pallas_call | solution.py:460
  35.5 1.2 copy.59
  36.7 5.2 copy.61.down_hbm
  43.7 9.5 %multiply_reduce_fusion.1 = (f32[]{:T(128)}, bf16[1472,896]{1,0:T(8,128)(2,1)S(1)}, bf16[1472,896]{1,0:T(8,128)(2,1)S(1)}, f32[]{:T(128)}) fusion(f32[1472,896]{1,0:T(8,128)} %param.25, f32[1472,896]{1,0:T(8,128)} %param.24), kind=kLoop, calls=%fused_computation.18 | loop fusion | flops 7913470 | bytes 15826952 | tf_op jit(solution)/shard_map/reduce_sum | solution.py:932
  53.2 2.7 pad_maximum_fusion.gate_up_hbm
  56.0 20.6 %all-gather.3.cloned.1.call-done = bf16[1024,1472]{1,0:T(8,128)(2,1)} async-done(((bf16[256,1472]{1,0:T(8,128)(2,1)}), bf16[1024,1472]{1,0:T(8,128)(2,1)}) %all-gather.3.cloned.1.call-update) | async-done | bytes 3014672 | tf_op jit(solution)/shard_map/all_gather | solution.py:840
  76.9 3.7 convolution_convert_fusion.3.qkv_ref
  80.5 9.9 %attend.1 = (bf16[1024,128]{1,0:T(8,128)(2,1)S(1)}, f32[2,1024,1024]{2,1,0:T(8,128)S(1)}) custom-call(bf16[1024,384]{1,0:T(8,128)(2,1)S(1)} %convolution_convert_fusion.3.qkv_ref, s32[1024,1]{1,0:T(8,128)S(1)} %copy.62.seg_col_ref, s32[1,1024]{1,0:T(1,128)S(1)} %copy-done.2, f32[2,2048]{1,0:T(2,128)S(1)} %convolution_bitcast_fusion.vec_ref), custom_call_target="tpu_custom_call" | custom-call | flops 1073741824 | bytes 8388608 | tf_op jit(solution)/shard_map/attend/pallas_call | solution.py:83
  90.4 3.2 copy-done
  93.8 19.4 %all_to_all.10 = bf16[4,256,128]{1,2,0:T(8,128)(2,1)S(1)} all-to-all(bf16[4,256,128]{1,2,0:T(8,128)(2,1)S(1)} %copy.63), channel_id=1, replica_groups=mesh['dp'=8,'mp'=4] {'mp'}, dimensions={0} | all-to-all | bytes 524288 | tf_op jit(solution)/shard_map/all_to_all | solution.py:781
  113.2 2.3 multiply_reduce_fusion.5
  115.6 1.3 multiply_convert_fusion.normed_hbm
  116.8 29.0 %all-gather.5.cloned.1.call-done = bf16[1024,1472]{1,0:T(8,128)(2,1)} async-done(((bf16[256,1472]{1,0:T(8,128)(2,1)}), bf16[1024,1472]{1,0:T(8,128)(2,1)}) %all-gather.5.cloned.1.call-update) | async-done | bytes 3014672 | tf_op jit(solution)/shard_map/all_gather | solution.py:845
  145.8 112.7 %feed_forward.1 = (bf16[4,256,1472]{2,1,0:T(8,128)(2,1)}, f32[256,1472]{1,0:T(8,128)}, bf16[1536,896]{1,0:T(8,128)(2,1)}, bf16[1536,896]{1,0:T(8,128)(2,1)}, bf16[896,1472]{1,0:T(8,128)(2,1)}) custom-call(bf16[256,1472]{1,0:T(8,128)(2,1)} %multiply_convert_fusion.normed_hbm, bf16[4,256,1472]{2,1,0:T(8,128)(2,1)} %bitcast.111, ...), custom_call_target="tpu_custom_call" | custom-call | flops 24310185984 | bytes 24870912 | tf_op jit(solution)/shard_map/feed_forward/pallas_call | solution.py:734
  258.5 2.5 multiply_reduce_fusion.3
  261.5 0.9 copy-done.11
  263.2 9.5 %all_to_all.11 = bf16[4,256,128]{2,1,0:T(8,128)(2,1)S(1)} all-to-all(bf16[4,256,128]{2,1,0:T(8,128)(2,1)S(1)} %bitcast.109), channel_id=1, replica_groups=mesh['dp'=8,'mp'=4] {'mp'}, dimensions={0} | all-to-all | bytes 524288 | tf_op jit(solution)/shard_map/all_to_all | solution.py:789
  272.7 3.4 copy-done.1
  276.1 11.5 %attend_back.1 = (bf16[1024,384]{1,0:T(8,128)(2,1)S(1)}, f32[2,2048]{1,0:T(2,128)S(1)}) custom-call(bf16[1024,384]{1,0:T(8,128)(2,1)S(1)} %convolution_convert_fusion.3.qkv_ref, bf16[1024,128]{1,0:T(8,128)(2,1)S(1)} %bitcast.84, f32[2,1024,1024]{2,1,0:T(8,128)S(1)} %copy-done.1), custom_call_target="tpu_custom_call" | custom-call | flops 2147483648 | bytes 8388608 | tf_op jit(solution)/shard_map/attend_back/pallas_call | solution.py:160
  287.5 3.5 convolution_convert_fusion
  297.4 5.0 multiply_reduce_fusion
  303.0 1.6 copy.67
  304.6 1.7 copy.82
  307.0 1.8 convolution_convert_fusion.2
  308.8 0.9 copy-done.33
  310.6 104.8 %sum_weights.1 = (bf16[8,192,896]{2,1,0:T(8,128)(2,1)}, bf16[8,192,896]{2,1,0:T(8,128)(2,1)}, bf16[8,112,1472]{2,1,0:T(8,128)(2,1)}, bf16[8,192,384]{2,1,0:T(8,128)(2,1)S(1)}, bf16[8,16,1472]{2,1,0:T(8,128)(2,1)S(1)}) custom-call(bf16[8,192,896]{2,1,0:T(8,128)(2,1)} %bitcast.103, bf16[8,192,896]{2,1,0:T(8,128)(2,1)} %bitcast.104, ...), custom_call_target="tpu_custom_call" | custom-call | flops 21659648 | bytes 21659648 | tf_op jit(solution)/shard_map/sum_weights/pallas_call | solution.py:367
  415.4 3.1 fusion.10
  419.2 5.1 copy.72
  425.2 1.1 copy.70
  428.8 1.2 fusion.6
  430.6 1.2 fusion.1
  432.4 1.9 fusion.16
  434.4 22.3 %psum.14 = f32[3008]{0:T(1024)S(1)} all-reduce(f32[3008]{0:T(1024)S(1)} %concatenate.15), channel_id=1, replica_groups=mesh['dp'=8,'mp'=4] {'dp'}, use_global_device_ids=true, to_apply=%region_12.13 | all-reduce | flops 3008 | bytes 24064 | tf_op jit(solution)/shard_map/psum | solution.py:901
  456.9 5.3 concatenate.16
  462.2 22.6 %psum.15 = f32[13288]{0:T(1024)S(1)} all-reduce(f32[13288]{0:T(1024)S(1)} %concatenate.16), channel_id=1, replica_groups=mesh['dp'=8,'mp'=4] {'mp'}, use_global_device_ids=true, to_apply=%region_26.27 | all-reduce | flops 13288 | bytes 106304 | tf_op jit(solution)/shard_map/psum | solution.py:934
  486.1 1.3 fusion.43
  501.4 2.9 fusion.25
  504.3 2.3 copy.74
  506.5 1.3 fusion.24
  507.9 1.1 copy.73
  509.7 6.9 %fusion.9 = f32[1472,896]{1,0:T(8,128)} fusion(f32[1472,896]{1,0:T(8,128)} %param.25, f32[896]{0:T(1024)S(1)} %get-tuple-element.167, f32[1472]{0:T(1024)S(1)} %get-tuple-element.165, bf16[1536,896]{1,0:T(8,128)(2,1)} %bitcast.98), kind=kLoop, calls=%fused_computation.14 | loop fusion | flops 5275648 | bytes 13198592 | tf_op jit(solution)/shard_map/sub | solution.py:962
  516.7 3.5 fusion.4
  522.3 3.0 multiply_subtract_fusion
  525.3 1.1 multiply_subtract_fusion.1
  527.2 2.0 multiply_subtract_fusion.2
  (176 shorter events, 24.1 us)
Async XLA Ops:
  7.2 3.2 copy-start.27
  7.2 69.3 %all-gather.3.cloned.1.call-start = ((), (), s32[]{:S(2)}) async-start(), calls=%async_computation.4 | async-start | bytes 3932160 | tf_op jit(solution)/shard_map/all_gather | solution.py:840
  8.7 3.4 copy-start.5
  10.2 25.3 %copy-start.34 = (bf16[1,256,1472]{1,2,0:T(8,128)(2,1)S(1)}, bf16[1,256,1472]{1,2,0:T(8,128)(2,1)}, u32[]{:S(2)}) copy-start(bf16[1,256,1472]{1,2,0:T(8,128)(2,1)} %param.27) | copy-start | bytes 2260996
  10.2 135.6 %all-gather.5.cloned.1.call-start = ((), (), s32[]{:S(2)}) async-start(), calls=%async_computation.5 | async-start | bytes 3932160 | tf_op jit(solution)/shard_map/all_gather | solution.py:845
  36.7 5.2 copy-start.46
  36.7 6.2 %copy-start.47 = (f32[32,2]{0,1:T(2,128)S(1)}, f32[32,2]{0,1:T(2,128)}, u32[]{:S(2)}) copy-start(f32[32,2]{0,1:T(2,128)} %param.22) | copy-start | bytes 772
  36.7 6.8 %copy-start.16 = (f32[1472,128]{1,0:T(8,128)S(1)}, f32[1472,128]{1,0:T(8,128)}, u32[]{:S(2)}) copy-start(f32[1472,128]{1,0:T(8,128)} %param.20) | copy-start | bytes 2260996
  36.7 6.8 %copy-start.19 = (f32[1472,128]{1,0:T(8,128)S(1)}, f32[1472,128]{1,0:T(8,128)}, u32[]{:S(2)}) copy-start(f32[1472,128]{1,0:T(8,128)} %param.19) | copy-start | bytes 2260996
  36.7 6.8 %copy-start.22 = (f32[1472,128]{1,0:T(8,128)S(1)}, f32[1472,128]{1,0:T(8,128)}, u32[]{:S(2)}) copy-start(f32[1472,128]{1,0:T(8,128)} %param.18) | copy-start | bytes 2260996
  43.7 33.1 %copy-start.30 = (bf16[1472,384]{1,0:T(8,128)(2,1)}, bf16[1472,384]{1,0:T(8,128)(2,1)S(1)}, u32[]{:S(2)}) copy-start(bf16[1472,384]{1,0:T(8,128)(2,1)S(1)} %fusion.12) | copy-start | bytes 3391492
  53.2 23.4 %copy-start.2 = (s32[1,1024]{1,0:T(1,128)S(1)}, s32[1,1024]{1,0:T(1,128)}, u32[]{:S(2)}) copy-start(s32[1,1024]{1,0:T(1,128)} %seg_row_ref.1) | copy-start | bytes 12292
  76.6 355.8 %reduce-scatter.5.cloned.1.call-start = ((), (), s32[]{:S(2)}) async-start(), calls=%async_computation.7 | async-start | bytes 3932160 | tf_op jit(solution)/shard_map/reduce_scatter | solution.py:864
  90.4 3.2 copy-start
  93.8 21.7 %copy-start.35 = (f32[1472]{0:T(1024)S(1)}, f32[1472]{0:T(1024)}, u32[]{:S(2)}) copy-start(f32[1472]{0:T(1024)} %param.23) | copy-start | bytes 17668
  115.5 145.5 %copy-start.3 = (f32[256,1472]{1,0:T(8,128)}, f32[256,1472]{1,0:T(8,128)S(1)}, u32[]{:S(2)}) copy-start(f32[256,1472]{1,0:T(8,128)S(1)} %get-tuple-element.235) | copy-start | bytes 4521988
  262.5 10.2 %copy-start.7 = (f32[256,1472]{1,0:T(8,128)}, f32[256,1472]{1,0:T(8,128)S(1)}, u32[]{:S(2)}) copy-start(f32[256,1472]{1,0:T(8,128)S(1)} %fusion.17) | copy-start | bytes 4521988
  272.7 3.4 copy-start.1
  276.1 11.5 %copy-start.31 = (bf16[1472,384]{1,0:T(8,128)(2,1)S(1)}, bf16[1472,384]{1,0:T(8,128)(2,1)}, u32[]{:S(2)}) copy-start(bf16[1472,384]{1,0:T(8,128)(2,1)} %copy-done.30) | copy-start | bytes 3391492
  291.0 4.0 copy-start.23
  291.0 4.8 copy-start.20
  291.0 5.6 %copy-start.17 = (f32[1472,128]{1,0:T(8,128)S(1)}, f32[1472,128]{1,0:T(8,128)}, u32[]{:S(2)}) copy-start(f32[1472,128]{1,0:T(8,128)} %param.20) | copy-start | bytes 2260996
  291.0 215.5 %reduce-scatter.3.cloned.1.call-start = ((), (), s32[]{:S(2)}) async-start(), calls=%async_computation.6 | async-start | bytes 3932160 | tf_op jit(solution)/shard_map/reduce_scatter | solution.py:865
  297.4 5.0 copy-start.8
  426.2 2.6 copy-start.14
  426.4 4.2 copy-start.12
  428.8 3.5 copy-start.6
  428.8 3.5 copy-start.38
  428.8 3.5 copy-start.43
  430.0 4.3 copy-start.40
  430.6 68.0 %copy-start.39 = (f32[32,2]{1,0:T(8,128)S(1)}, f32[32,2]{1,0:T(8,128)}, u32[]{:S(2)}) copy-start(f32[32,2]{1,0:T(8,128)} %copy.71) | copy-start | bytes 772
  430.6 70.8 %copy-start.45 = (f32[256]{0:T(256)S(1)}, f32[256]{0:T(256)}, u32[]{:S(2)}) copy-start(f32[256]{0:T(256)} %copy-done.44) | copy-start | bytes 3076
  432.4 69.0 %copy-start.26 = (bf16[256,1472]{1,0:T(8,128)(2,1)S(1)}, bf16[256,1472]{1,0:T(8,128)(2,1)}, u32[]{:S(2)}) copy-start(bf16[256,1472]{1,0:T(8,128)(2,1)} %reduce-scatter.5.cloned.1.call-done) | copy-start | bytes 2260996
  501.4 5.2 copy-start.4
  509.7 6.9 %slice-start.2 = ((s8[5275648]{0:T(1024)(128)(4,1)}), s8[4194304]{0:T(1024)(128)(4,1)S(1)}, s32[]{:S(2)}) async-start(s8[5275648]{0:T(1024)(128)(4,1)} %bitcast.89), calls=%async_computation.10 | async-start | bytes 8388608
  509.7 6.9 %slice-start.3 = ((s8[5275648]{0:T(1024)(128)(4,1)}), s8[1081344]{0:T(1024)(128)(4,1)S(1)}, s32[]{:S(2)}) async-start(s8[5275648]{0:T(1024)(128)(4,1)} %bitcast.89), calls=%async_computation.11 | async-start | bytes 2162688
  509.7 6.9 %copy-start.13 = (bf16[8,192,896]{2,1,0:T(8,128)(2,1)S(1)}, bf16[8,192,896]{2,1,0:T(8,128)(2,1)}, u32[]{:S(2)}) copy-start(bf16[8,192,896]{2,1,0:T(8,128)(2,1)} %get-tuple-element.72) | copy-start | bytes 8257540
  509.7 11.2 %slice-start.4 = ((s8[5275648]{0:T(1024)(128)(4,1)}), s8[4194304]{0:T(1024)(128)(4,1)S(1)}, s32[]{:S(2)}) async-start(s8[5275648]{0:T(1024)(128)(4,1)} %bitcast.91), calls=%async_computation.12 | async-start | bytes 8388608
  516.6 5.0 slice-start
  516.7 4.3 copy-start.41
  516.7 5.2 slice-start.1
  516.7 5.5 %slice-start.5 = ((s8[5275648]{0:T(1024)(128)(4,1)}), s8[1081344]{0:T(1024)(128)(4,1)S(1)}, s32[]{:S(2)}) async-start(s8[5275648]{0:T(1024)(128)(4,1)} %bitcast.91), calls=%async_computation.13 | async-start | bytes 2162688
  522.2 3.1 copy-start.48
  522.2 3.1 copy-start.28
  522.2 3.1 copy-start.29
  522.2 4.2 copy-start.18
  522.3 4.2 copy-start.21
  522.3 4.2 copy-start.24
  (12 other events, 21.7 us)
Sparse Core Ops, SparseCore 0:
  10.3 66.1 all-gather.2
  78.1 67.6 all-gather.4
  291.2 61.2 reduce-scatter.4
  354.6 63.3 reduce-scatter.2

commit v3 on v2

v3 whole, which is shorter than its diff:
```python
import functools

import jax
import jax.numpy as jnp
from jax import lax
from jax.experimental import pallas as pl
from jax.experimental.pallas import tpu as pltpu
from jax.sharding import PartitionSpec as P

HD = 64
BUCKETS = 32
BLOCK = 128


highest = lax.Precision.HIGHEST
step_scale = 0.3


def rms_norm(values, gain):
    return values * lax.rsqrt(jnp.mean(values * values, axis=-1, keepdims=True) + 1e-06) * gain


def norm_back(values, gain, grad):
    scale = lax.rsqrt(jnp.mean(values * values, axis=-1, keepdims=True) + 1e-06)
    unit = values * scale
    pull = grad * gain
    return scale * (pull - unit * jnp.mean(pull * unit, axis=-1, keepdims=True))


def product(left_side, right_side):
    return jnp.dot(left_side, right_side, preferred_element_type=jnp.float32)


def left_inner(left_side, right_side):
    return lax.dot_general(
        left_side, right_side, (((0,), (0,)), ((), ())), preferred_element_type=jnp.float32
    )


def right_inner(left_side, right_side):
    return lax.dot_general(
        left_side, right_side, (((1,), (1,)), ((), ())), preferred_element_type=jnp.float32
    )


def slot_lanes(values, slot):
    lane = lax.broadcasted_iota(jnp.int32, values.shape, 1)
    return jnp.where((lane >= slot * HD) & (lane < (slot + 1) * HD), values, jnp.zeros_like(values))


def attend_kernel(seq_len, slots, qkv_ref, seg_col_ref, seg_row_ref, vec_ref, out_ref, probs_ref, tilt_ref):
    step = pl.program_id(0)
    steps = seq_len // BLOCK
    lanes = slots * HD

    @pl.when(step == 0)
    def _():
        for slot in range(slots):
            spread = jnp.broadcast_to(vec_ref[slot : slot + 1, :], (BLOCK, 2 * seq_len))
            tilt_ref[slot] = pltpu.roll(
                spread, 2 * seq_len - BLOCK + 1, 1, stride=1, stride_axis=0
            )

    same_doc = seg_col_ref[...] == seg_row_ref[...]
    rows = pl.ds(pl.multiple_of(step * BLOCK, BLOCK), BLOCK)
    window = pl.ds(pl.multiple_of((steps - 1 - step) * BLOCK, BLOCK), seq_len)
    queries = qkv_ref[rows, 0:lanes]
    keys = qkv_ref[:, lanes : 2 * lanes]
    values = qkv_ref[:, 2 * lanes : 3 * lanes]
    mixed = jnp.zeros((BLOCK, lanes), jnp.float32)
    for slot in range(slots):
        scores = right_inner(slot_lanes(queries, slot), keys) + tilt_ref[slot, :, window]
        scores = jnp.where(same_doc, scores, -1e30)
        peak = jnp.max(scores, axis=-1, keepdims=True)
        raised = jnp.exp(scores - peak)
        probs = raised * (1.0 / jnp.sum(raised, axis=-1, keepdims=True))
        probs_ref[slot] = probs
        mixed = mixed + slot_lanes(product(probs.astype(jnp.bfloat16), values), slot)
    out_ref[...] = mixed.astype(jnp.bfloat16)


def attend(qkv, seg_col, seg_row, vector):
    seq_len = qkv.shape[0]
    slots = vector.shape[0]
    lanes = slots * HD
    return pl.pallas_call(
        functools.partial(attend_kernel, seq_len, slots),
        grid=(seq_len // BLOCK,),
        in_specs=[
            pl.BlockSpec((seq_len, 3 * lanes), lambda i: (0, 0)),
            pl.BlockSpec((BLOCK, 1), lambda i: (i, 0)),
            pl.BlockSpec((1, seq_len), lambda i: (0, 0)),
            pl.BlockSpec((slots, 2 * seq_len), lambda i: (0, 0)),
        ],
        out_specs=[
            pl.BlockSpec((BLOCK, lanes), lambda i: (i, 0)),
            pl.BlockSpec((slots, BLOCK, seq_len), lambda i: (0, i, 0)),
        ],
        out_shape=[
            jax.ShapeDtypeStruct((seq_len, lanes), jnp.bfloat16),
            jax.ShapeDtypeStruct((slots, seq_len, seq_len), jnp.float32),
        ],
        scratch_shapes=[pltpu.VMEM((slots, BLOCK, 2 * seq_len), jnp.float32)],
        compiler_params=pltpu.CompilerParams(vmem_limit_bytes=58 << 20),
        cost_estimate=pl.CostEstimate(
            flops=8 * slots * seq_len * seq_len * HD,
            bytes_accessed=4 * slots * seq_len * seq_len,
            transcendentals=slots * seq_len * seq_len,
        ),
        name="attend",
    )(qkv, seg_col, seg_row, vector)


class Butterfly:
    def __init__(self, order, base):
        self.order = order
        self.me = lax.axis_index("dp")
        self.line = lax.axis_index("mp")
        self.base = base
        self.offsets = []
        total = 0
        for s in range(len(order)):
            self.offsets.append(total)
            total += 1 << (len(order) - 1 - s)

    def bit(self, b):
        return (self.me // b) % 2

    def partner(self, s):
        b = self.order[s]
        return (self.me + b * (1 - 2 * self.bit(b)), self.line)

    def width(self, s):
        return 1 << (len(self.order) - 1 - s)

    def piece(self, s, j, mine):
        b = self.order[s]
        found = sum(k * self.bit(k) for k in self.order[:s])
        found = found + b * (self.bit(b) if mine else 1 - self.bit(b))
        for i, k in enumerate(self.order[s + 1 :]):
            found = found + k * ((j // (1 << i)) % 2)
        return found

    def copy(self, src, dst, sems, slot, s):
        return pltpu.make_async_remote_copy(
            src_ref=src,
            dst_ref=dst,
            send_sem=sems[0].at[self.base + slot],
            recv_sem=sems[1].at[self.base + slot],
            device_id=self.partner(s),
            device_id_type=pl.DeviceIdType.MESH,
        )

    def halve(self, s, source, landing, sems):
        at = self.offsets[s]
        return [
            self.copy(source(self.piece(s, j, False)), landing.at[at + j], sems, at + j, s)
            for j in range(self.width(s))
        ]

    def add(self, s, kept, landing, copies):
        at = self.offsets[s]
        for j, copy in enumerate(copies):
            copy.wait_recv()
            mine = kept(self.piece(s, j, True))
            mine[...] = (mine[...].astype(jnp.float32) + landing[at + j].astype(jnp.float32)).astype(
                jnp.bfloat16
            )

    def double(self, s, whole, sems, first=None):
        at = self.offsets[s]
        copies = []
        for j in range(self.width(s)):
            view = whole(self.piece(s, j, True))
            copies.append(self.copy(view if first is None else first, view, sems, at + j, s))
        return copies


def orders(data_count):
    bits = [1 << i for i in range(data_count.bit_length() - 1)]
    return (bits, bits[:1] + bits[:0:-1])


def greet(peers):
    barrier = pltpu.get_barrier_semaphore()
    for peer in peers:
        pl.semaphore_signal(barrier, inc=1, device_id=peer, device_id_type=pl.DeviceIdType.MESH)
    pl.semaphore_wait(barrier, len(peers))


def row_pieces(ref, data_count, at=0, lanes=None):
    rows = ref.shape[0] // data_count
    columns = pl.ds(at, ref.shape[1] if lanes is None else lanes)
    return lambda q: ref.at[pl.ds(pl.multiple_of(q * rows, rows), rows), columns]


def total(values, axis):
    return jnp.sum(values, axis=axis, keepdims=True)


def sum_weights_kernel(data_count, count, model_width, parts, *refs):
    ff_hbm, qkv_hbm, out_hbm, qkv_low, gate_up_low, squares_ref = refs[:6]
    wholes, (shared_ref, own_ref, tall_ref) = refs[6:11], refs[11:14]
    kept, landings, full = refs[14:16], refs[16:18], refs[18:23]
    (
        cross,
        qkv_w,
        gate_up_w,
        tall,
        cols,
        gathered,
        load_sem,
        save_sem,
        down_send,
        down_recv,
        up_send,
        up_recv,
        cross_send,
        cross_recv,
        share_send,
        share_recv,
    ) = refs[23:]
    me = lax.axis_index("dp")
    place = lax.axis_index("mp")
    span = data_count - 1
    ways = orders(data_count)
    stages = len(ways[0])
    down, up = (down_send, down_recv), (up_send, up_recv)
    padded, units = full[0].shape
    lanes = full[4].shape[1]
    height = padded // data_count
    f32 = jnp.float32

    whole = [row_pieces(ref, data_count) for ref in full]
    saved = [row_pieces(wholes[i], data_count, at, wide) for i, at, wide, _ in parts]
    source = [row_pieces(ref, data_count) for ref in (qkv_hbm, out_hbm)]
    keep = [row_pieces(ref, data_count) for ref in kept]
    halvers = [Butterfly(ways[1 - i], i * span) for i in range(2)]
    doublers = [Butterfly(ways[way], k * span) for k, (_, _, _, way) in enumerate(parts)]
    views = [row_pieces(full[i], data_count, at, wide) for i, at, wide, _ in parts]

    loads = []

    def load(src, dst):
        copy = pltpu.make_async_copy(src, dst, load_sem.at[len(loads)])
        copy.start()
        loads.append(copy)

    first = doublers[0]
    for j in range(first.width(0)):
        q = first.piece(0, j, True)
        for i in range(3):
            load(row_pieces(ff_hbm.at[i], data_count)(q), whole[i](q))
    for i, fly in enumerate(halvers):
        for j in range(fly.width(0)):
            q = fly.piece(0, j, True)
            load(source[i](q), keep[i](q))
    load(qkv_low, qkv_w)
    load(gate_up_low, gate_up_w)
    others = [(place + k) % count for k in range(1, count)]
    greet([halvers[0].partner(s) for s in range(stages)] + [(me, other) for other in others])

    sent = []

    def start(copies):
        for copy in copies:
            copy.start()
        sent.extend(copies)
        return copies

    halves = [start(fly.halve(0, source[i], landings[i], down)) for i, fly in enumerate(halvers)]
    tall[...] = jnp.zeros_like(tall)
    cols[...] = jnp.zeros_like(cols)
    for copy in loads:
        copy.wait()

    doubles = {}

    def spread(s, arrays):
        for k, (i, _, _, _) in enumerate(parts):
            if i in arrays:
                doubles[k] = start(doublers[k].double(s, views[k], up))

    spread(0, (0, 1, 2))

    def note(k, q):
        i, start_lane, wide, _ = parts[k]
        rows = pl.ds(pl.multiple_of(q * height, height), height)
        grad = views[k](q)[...].astype(f32)
        if i == 3:
            at = lax.broadcasted_iota(jnp.int32, grad.shape, 0) + q * height
            grad = jnp.where(at < model_width, grad, 0.0)
        squares = grad * grad
        cols[i : i + 1, start_lane : start_lane + wide] += total(squares, 0)
        if i < 2:
            tall[rows, 3 + i : 4 + i] = total(squares, 1)
            weight = gate_up_w[rows, i * units : (i + 1) * units].astype(f32)
            tall[rows, 6:7] += total(grad * weight, 1)
        elif i == 3:
            for k in range(3):
                tall[rows, k : k + 1] = total(squares[:, k * lanes : (k + 1) * lanes], 1)
            tall[rows, 5:6] = total(grad * qkv_w[rows].astype(f32), 1)
        else:
            lane = 8 if i == 2 else 9
            tall[rows, lane : lane + 1] += total(squares, 1)

    saves = []

    def save(k, q, slot):
        copy = pltpu.make_async_copy(views[k](q), saved[k](q), save_sem.at[k * data_count + slot])
        copy.start()
        saves.append(copy)

    for s in range(stages):
        for i, fly in enumerate(halvers):
            fly.add(s, keep[i], landings[i], halves[i])
            if s + 1 < stages:
                halves[i] = start(fly.halve(s + 1, keep[i], landings[i], down))
    crossing = row_pieces(kept[1], data_count)(me)

    def lanes_of(other):
        return pl.ds(pl.multiple_of(other * lanes, lanes), lanes)

    start(
        [
            pltpu.make_async_remote_copy(
                src_ref=crossing.at[:, lanes_of(other)],
                dst_ref=cross.at[count - 2 - k],
                send_sem=cross_send.at[k],
                recv_sem=cross_recv.at[count - 2 - k],
                device_id=(me, other),
                device_id_type=pl.DeviceIdType.MESH,
            )
            for k, other in enumerate(others)
        ]
    )
    whole[3](me)[...] = keep[0](me)[...]
    spread(stages - 1, (3,))
    summed = crossing[:, lanes_of(place)].astype(f32)
    for k in range(count - 1):
        pltpu.make_async_remote_copy(
            src_ref=cross.at[k],
            dst_ref=cross.at[k],
            send_sem=cross_send.at[k],
            recv_sem=cross_recv.at[k],
            device_id=(me, others[0]),
            device_id_type=pl.DeviceIdType.MESH,
        ).wait_recv()
        summed = summed + cross[k].astype(f32)
    whole[4](me)[...] = summed.astype(jnp.bfloat16)
    spread(stages - 1, (4,))

    def note_pieces(k, s, mine):
        fly = doublers[k]
        for j in range(fly.width(s)):
            save(k, fly.piece(s, j, mine), j if mine else fly.width(s) + j)

        def note_piece(j, carry):
            note(k, fly.piece(s, j, mine))
            return carry

        lax.fori_loop(0, fly.width(s), note_piece, 0)

    early = [k for k, part in enumerate(parts) if part[0] < 3]
    late = [k for k, part in enumerate(parts) if part[0] >= 3]
    for k in early:
        note_pieces(k, 0, True)
    for k in late:
        note(k, me)
        save(k, me, 0)
    for k in early:
        for copy in doubles[k]:
            copy.wait_recv()
        note_pieces(k, 0, False)
    for s in reversed(range(stages)):
        for k in late:
            for copy in doubles[k]:
                copy.wait_recv()
            if s > 0:
                doubles[k] = start(doublers[k].double(s - 1, views[k], up))
        for k in late:
            note_pieces(k, s, False)

    slots_rel = full[3][model_width : model_width + BUCKETS, :128].astype(f32)
    tall[:BUCKETS, 7:8] = total(slots_rel * slots_rel, 1)
    share = gathered.at[place]
    share[...] = tall[...].T[0:16]
    share[10:11, :128] = squares_ref[...]
    shares = start(
        [
            pltpu.make_async_remote_copy(
                src_ref=share,
                dst_ref=share,
                send_sem=share_send.at[k],
                recv_sem=share_recv.at[place],
                device_id=(me, other),
                device_id_type=pl.DeviceIdType.MESH,
            )
            for k, other in enumerate(others)
        ]
    )
    own_ref[...] = jnp.zeros_like(own_ref)
    own_ref[:, : cols.shape[1]] = cols[...]
    for k, other in enumerate(others):
        pltpu.make_async_remote_copy(
            src_ref=gathered.at[other],
            dst_ref=gathered.at[other],
            send_sem=share_send.at[k],
            recv_sem=share_recv.at[other],
            device_id=(me, other),
            device_id_type=pl.DeviceIdType.MESH,
        ).wait_recv()
    summed = gathered[0]
    for k in range(1, count):
        summed = summed + gathered[k]
    shared_ref[...] = summed
    tall_ref[...] = jnp.concatenate([summed, jnp.zeros((112, padded), f32)], axis=0).T
    for copy in saves:
        copy.wait()
    for copy in sent:
        copy.wait_send()


def sum_weights(ff_grads, qkv, out, qkv_low, gate_up_low, squares, model_width):
    count = lax.axis_size("mp")
    data_count = lax.axis_size("dp")
    anywhere = pl.BlockSpec(memory_space=pl.ANY)
    near = pl.BlockSpec(memory_space=pltpu.VMEM)
    dma = pltpu.SemaphoreType.DMA
    low, f32 = jnp.bfloat16, jnp.float32
    span = data_count - 1
    units = ff_grads.shape[2]
    padded, wide = qkv.shape
    height = padded // data_count
    lanes = out.shape[1] // count
    full = [(padded, units)] * 3 + [(padded, wide), (padded, lanes)]
    parts = (*ff_parts(units), (3, 0, wide, 1), (4, 0, lanes, 0))
    n = len(parts)
    return pl.pallas_call(
        functools.partial(sum_weights_kernel, data_count, count, model_width, parts),
        out_shape=[jax.ShapeDtypeStruct(s, low) for s in full]
        + [
            jax.ShapeDtypeStruct((16, padded), f32),
            jax.ShapeDtypeStruct((8, padded), f32),
            jax.ShapeDtypeStruct((padded, 128), f32),
        ],
        in_specs=[anywhere] * 5 + [near],
        out_specs=[anywhere] * 5 + [near] * 3,
        scratch_shapes=[pltpu.VMEM(a.shape, low) for a in (qkv, out)]
        + [pltpu.VMEM((span, height, a.shape[1]), low) for a in (qkv, out)]
        + [pltpu.VMEM(s, low) for s in full]
        + [
            pltpu.VMEM((count - 1, height, lanes), low),
            pltpu.VMEM(qkv_low.shape, low),
            pltpu.VMEM(gate_up_low.shape, low),
            pltpu.VMEM((padded, 128), f32),
            pltpu.VMEM((8, (max(units, wide) + 127) // 128 * 128), f32),
            pltpu.VMEM((count, 16, padded), f32),
            dma((3 * data_count + 5,)),
            dma((n * data_count,)),
            dma((2 * span,)),
            dma((2 * span,)),
            dma((n * span,)),
            dma((n * span,)),
            dma((count - 1,)),
            dma((count - 1,)),
            dma((count - 1,)),
            dma((count,)),
        ],
        compiler_params=pltpu.CompilerParams(
            collective_id=2, has_side_effects=True, vmem_limit_bytes=56 << 20
        ),
        cost_estimate=pl.CostEstimate(
            flops=padded * units, bytes_accessed=200 << 20, transcendentals=0
        ),
        name="sum_weights",
    )(ff_grads, qkv, out, qkv_low, gate_up_low, squares)


def update_kernel(tensor_count, *refs):
    grads, rel_g = refs[:5], refs[5]
    weights, (rel_w, attn_w, ff_w) = refs[6:13], refs[13:16]
    shared_ref, own_ref, tall_ref = refs[16:19]
    news, rel_n = refs[19:26], refs[26]
    along, rel_r = refs[27:34], refs[34]
    across, rel_c = refs[35:42], refs[42]
    attn_n, attn_m, ff_n, ff_m = refs[43:47]
    first = pl.program_id(0) == 0
    f32 = jnp.float32
    width = attn_w.shape[1]
    lanes = weights[3].shape[1]
    slots = rel_w.shape[1]
    tiny = 1e-30

    def step_rate(lane, size):
        return step_scale * jnp.sqrt(shared_ref[10:11, lane : lane + 1] / size)

    qkv = grads[3][...].astype(f32)
    for k, (row, square, own, at) in enumerate(
        (
            (3, 4, 0, 0),
            (4, 5, 1, 0),
            (8, 7, 2, 0),
            (0, 0, 3, 0),
            (1, 1, 3, lanes),
            (2, 2, 3, 2 * lanes),
            (9, 6, 4, 0),
        )
    ):
        here = weights[k].shape[1]
        if own == 3:
            grad = qkv[:, at : at + lanes]
        else:
            grad = grads[own][...].astype(f32)
        cols = here * tensor_count
        size = width * cols
        level = total(shared_ref[row : row + 1, :width], 1) / size + tiny
        rate = step_rate(square, size)
        row_factor = lax.rsqrt((tall_ref[:, row : row + 1] / cols + tiny) / level) * rate
        col_moment = own_ref[own : own + 1, at : at + here] / width + tiny
        news[k][...] = weights[k][...] - grad * row_factor * lax.rsqrt(col_moment)

        @pl.when(first)
        def _():
            along[k][...] = (shared_ref[row : row + 1, :width] / cols + tiny).reshape(width)
            across[k][...] = col_moment.reshape(here)

    @pl.when(first)
    def _():
        rel = rel_g[:, :slots].astype(f32)
        cols = slots * tensor_count
        size = BUCKETS * cols
        row_sums = shared_ref[7:8, :BUCKETS]
        level = total(row_sums, 1) / size + tiny
        row_factor = lax.rsqrt((tall_ref[:BUCKETS, 7:8] / cols + tiny) / level) * step_rate(3, size)
        col_moment = total(rel * rel, 0) / BUCKETS + tiny
        rel_n[...] = rel_w[...] - rel * row_factor * lax.rsqrt(col_moment)
        rel_r[...] = row_sums / cols + tiny
        rel_c[...] = col_moment
        for gain, row, new, moment_out in ((attn_w, 5, attn_n, attn_m), (ff_w, 6, ff_n, ff_m)):
            value = gain[...]
            grad = shared_ref[row : row + 1, :width] / value
            moment = grad * grad + tiny
            rate = step_scale * jnp.sqrt(total(value * value, 1) / width)
            stepped = value - rate * grad * lax.rsqrt(total(moment, 1) / width)
            new[...] = stepped.reshape(width)
            moment_out[...] = moment.reshape(width)


def update(grads, weights, rel_w, attn_w, ff_w, shared, own, tall, chunks=8):
    tensor_count = lax.axis_size("mp")
    width = weights[0].shape[0]
    slots = rel_w.shape[1]
    f32 = jnp.float32

    def blocks(array):
        return pl.BlockSpec((width // chunks, array.shape[1]), lambda i: (i, 0))

    def fixed(rows, cols, at=0):
        return pl.BlockSpec((rows, cols), lambda i: (at, 0))

    def line(size):
        return pl.BlockSpec((size,), lambda i: (0,))

    matrices = [blocks(w) for w in weights]
    rel_spec = fixed(BUCKETS, slots)
    columns = [w.shape[1] for w in weights]
    return pl.pallas_call(
        functools.partial(update_kernel, tensor_count),
        grid=(chunks,),
        in_specs=[
            *[blocks(g) for g in grads],
            fixed(BUCKETS, grads[3].shape[1], width // BUCKETS),
            *matrices,
            rel_spec,
            fixed(1, width),
            fixed(1, width),
            fixed(*shared.shape),
            fixed(*own.shape),
            blocks(tall),
        ],
        out_specs=[*matrices, rel_spec]
        + [line(width)] * 7
        + [fixed(1, BUCKETS)]
        + [line(c) for c in columns]
        + [fixed(1, slots)]
        + [line(width)] * 4,
        out_shape=[jax.ShapeDtypeStruct(w.shape, f32) for w in weights]
        + [jax.ShapeDtypeStruct(rel_w.shape, f32)]
        + [jax.ShapeDtypeStruct((width,), f32)] * 7
        + [jax.ShapeDtypeStruct((1, BUCKETS), f32)]
        + [jax.ShapeDtypeStruct((c,), f32) for c in columns]
        + [jax.ShapeDtypeStruct((1, slots), f32)]
        + [jax.ShapeDtypeStruct((width,), f32)] * 4,
        compiler_params=pltpu.CompilerParams(vmem_limit_bytes=58 << 20),
        cost_estimate=pl.CostEstimate(
            flops=40 * width * columns[0], bytes_accessed=36 * width * columns[0], transcendentals=0
        ),
        name="update",
    )(
        *grads, grads[3], *weights, rel_w,
        attn_w.reshape(1, width), ff_w.reshape(1, width), shared, own, tall,
    )


def gather_proj_kernel(data_count, count, own_ref, all_ref, load_sem, cross_send, cross_recv, side_send, side_recv):
    me = lax.axis_index("dp")
    place = lax.axis_index("mp")
    others = [(place + k) % count for k in range(1, count)]
    peers = [(me + k) % data_count for k in range(1, data_count)]
    load = pltpu.make_async_copy(own_ref, all_ref.at[place], load_sem)
    load.start()
    greet([(me, other) for other in others] + [(peer, place) for peer in peers])
    sent = []
    for k, other in enumerate(others):
        copy = pltpu.make_async_remote_copy(
            src_ref=own_ref.at[me],
            dst_ref=all_ref.at[place, me],
            send_sem=cross_send.at[k],
            recv_sem=cross_recv.at[count - 2 - k],
            device_id=(me, other),
            device_id_type=pl.DeviceIdType.MESH,
        )
        copy.start()
        sent.append(copy)
    arrivals = []
    for k, other in enumerate(others):
        pltpu.make_async_remote_copy(
            src_ref=own_ref.at[me],
            dst_ref=all_ref.at[other, me],
            send_sem=cross_send.at[k],
            recv_sem=cross_recv.at[k],
            device_id=(me, other),
            device_id_type=pl.DeviceIdType.MESH,
        ).wait_recv()
        for j, peer in enumerate(peers):
            slot = k * (data_count - 1)
            copy = pltpu.make_async_remote_copy(
                src_ref=all_ref.at[other, me],
                dst_ref=all_ref.at[other, me],
                send_sem=side_send.at[slot + j],
                recv_sem=side_recv.at[slot + data_count - 2 - j],
                device_id=(peer, place),
                device_id_type=pl.DeviceIdType.MESH,
            )
            copy.start()
            sent.append(copy)
            arrivals.append(
                pltpu.make_async_remote_copy(
                    src_ref=all_ref.at[other, peer],
                    dst_ref=all_ref.at[other, peer],
                    send_sem=side_send.at[slot + j],
                    recv_sem=side_recv.at[slot + j],
                    device_id=(peer, place),
                    device_id_type=pl.DeviceIdType.MESH,
                )
            )
    for arrival in arrivals:
        arrival.wait_recv()
    for copy in sent:
        copy.wait_send()
    load.wait()


def gather_proj(proj_low):
    count = lax.axis_size("mp")
    data_count = lax.axis_size("dp")
    lanes, width = proj_low.shape
    part = lanes // data_count
    anywhere = pl.BlockSpec(memory_space=pl.ANY)
    dma = pltpu.SemaphoreType.DMA
    gathered = pl.pallas_call(
        functools.partial(gather_proj_kernel, data_count, count),
        out_shape=jax.ShapeDtypeStruct((count, data_count, part, width), proj_low.dtype),
        in_specs=[anywhere],
        out_specs=anywhere,
        scratch_shapes=[
            dma,
            dma((count - 1,)),
            dma((count - 1,)),
            dma(((count - 1) * (data_count - 1),)),
            dma(((count - 1) * (data_count - 1),)),
        ],
        compiler_params=pltpu.CompilerParams(collective_id=0, has_side_effects=True),
        cost_estimate=pl.CostEstimate(flops=0, bytes_accessed=50 << 20, transcendentals=0),
        name="gather_proj",
    )(proj_low.reshape(data_count, part, width))
    return gathered.reshape(count * lanes, width)


def turn_order(count):
    return [sorted(range(count), key=lambda b: (abs(b - place), b < place)) for place in range(count)]


def look_up(table, row, column):
    found = jnp.int32(0)
    for r, entries in enumerate(table):
        for c, entry in enumerate(entries):
            found = jnp.where((row == r) & (column == c), jnp.int32(entry), found)
    return found


def feed_forward_kernel(
    data_count,
    count,
    parts,
    normed_hbm,
    cot_hbm,
    gate_up_hbm,
    down_hbm,
    out_hbm,
    dn_ref,
    pieces_hbm,
    normed,
    cot,
    gate_up,
    down,
    hidden,
    d_gate_up,
    outgoing,
    incoming,
    stage,
    grads,
    land_whole,
    land_most,
    land_rest,
    load_sem,
    stage_sem,
    gather_send,
    gather_recv,
    sum_send,
    sum_recv,
    down_send,
    down_recv,
):
    place = lax.axis_index("mp")
    row = lax.axis_index("dp")
    block_len, width = dn_ref.shape
    units = down.shape[1]
    part_len = block_len // parts
    last = count - 1
    has_left = place > 0
    has_right = place < last

    loads = [
        pltpu.make_async_copy(normed_hbm, normed.at[place], load_sem.at[0]),
        pltpu.make_async_copy(gate_up_hbm.at[pl.ds(0, width)], gate_up, load_sem.at[1]),
        pltpu.make_async_copy(down_hbm, down, load_sem.at[2]),
        pltpu.make_async_copy(cot_hbm, cot, load_sem.at[3]),
    ]
    for load in loads:
        load.start()

    ways = orders(data_count)
    span = data_count - 1
    most = land_most.shape[2]
    shares = (
        (0, 0, units, 0, land_whole.at[0]),
        (1, 0, units, 1, land_whole.at[1]),
        (2, 0, most, 0, land_most),
        (2, most, units - most, 1, land_rest),
    )
    flies = [Butterfly(ways[way], k * span) for k, (_, _, _, way, _) in enumerate(shares)]
    stages = len(ways[0])
    sems = (down_send, down_recv)
    views = [row_pieces(grads.at[i], data_count, at, lanes) for i, at, lanes, _, _ in shares]

    barrier = pltpu.get_barrier_semaphore()
    for s in range(stages):
        pl.semaphore_signal(
            barrier, inc=1, device_id=flies[0].partner(s), device_id_type=pl.DeviceIdType.MESH
        )
    for side, there in ((-1, has_left), (1, has_right)):

        @pl.when(there)
        def _():
            pl.semaphore_signal(
                barrier, inc=1, device_id=(row, place + side), device_id_type=pl.DeviceIdType.MESH
            )

    pl.semaphore_wait(barrier, stages + has_left.astype(jnp.int32) + has_right.astype(jnp.int32))

    def pass_block(block, side, slot):
        return pltpu.make_async_remote_copy(
            src_ref=normed.at[block],
            dst_ref=normed.at[block],
            send_sem=gather_send.at[slot],
            recv_sem=gather_recv.at[block],
            device_id=(row, place + side),
            device_id_type=pl.DeviceIdType.MESH,
        )

    def rows_of(part):
        return pl.ds(pl.multiple_of(part * part_len, part_len), part_len)

    def pass_sum(block, part, side, slot):
        return pltpu.make_async_remote_copy(
            src_ref=outgoing.at[block, rows_of(part)],
            dst_ref=incoming.at[slot, rows_of(part)],
            send_sem=sum_send.at[block, part],
            recv_sem=sum_recv.at[slot, part],
            device_id=(row, place + side),
            device_id_type=pl.DeviceIdType.MESH,
        )

    def landing(block, side):
        return jnp.where((side == -1) & (place + side == block), count, block)

    loads[0].wait()
    for side, there in ((-1, has_left), (1, has_right)):

        @pl.when(there)
        def _():
            pass_block(place, side, count + (side + 1) // 2).start()

    for load in loads[1:]:
        load.wait()

    def store_out(turn, block):
        return pltpu.make_async_copy(stage.at[turn % 2], out_hbm.at[block], stage_sem.at[turn % 2])

    table = turn_order(count)
    root = 0.7978845608028654

    def turn_body(turn, carry):
        block = look_up(table, place, turn)
        distance = jnp.abs(block - place)

        @pl.when((distance > 0) & ((block > place) | (place + distance > last)))
        def _():
            for side in (1, -1):
                other = place + side * distance

                @pl.when((other >= 0) & (other <= last))
                def _():
                    pass_block(other, 0, other).wait_recv()

                    @pl.when((place - side >= 0) & (place - side <= last))
                    def _():
                        pass_block(other, -side, other).start()

        acts = product(normed[block], gate_up[...])
        gate_act = acts[:, :units]
        up_act = acts[:, units:]
        squared = gate_act * gate_act
        bend = jnp.tanh(root * gate_act * (1.0 + 0.044715 * squared))
        half = 0.5 * (1.0 + bend)
        gelu = gate_act * half
        hidden[block] = (gelu * up_act).astype(jnp.bfloat16)
        d_hidden = product(cot[block], down[...])
        slope = half + 0.5 * gate_act * (1.0 - bend * bend) * (root * (1.0 + 0.134145 * squared))
        d_gate_up[block, :, :units] = (d_hidden * up_act * slope).astype(jnp.bfloat16)
        d_gate_up[block, :, units:] = (d_hidden * gelu).astype(jnp.bfloat16)
        term = right_inner(d_gate_up[block], gate_up[...])

        @pl.when(block == place)
        def _():
            dn_ref[...] = term

        @pl.when(block != place)
        def _():
            outgoing[block] = term.astype(jnp.bfloat16)

        for side, is_end in ((1, place == 0), (-1, place == last)):

            @pl.when(is_end & (block != place))
            def _():
                for part in range(parts):
                    pass_sum(block, part, side, landing(block, side)).start()

        @pl.when(turn >= 2)
        def _():
            store_out(turn, block).wait()

        stage[turn % 2] = right_inner(hidden[block], down[...]).astype(jnp.bfloat16)
        store_out(turn, block).start()
        return carry

    lax.fori_loop(0, count, turn_body, 0)

    def relay(key):
        def relay_part(part, carry):
            for side, block in ((1, key), (-1, last - key)):
                through = (block > place) & has_left if side == 1 else (block < place) & has_right

                @pl.when(through)
                def _():
                    pass_sum(block, part, side, block).wait_recv()
                    rows = rows_of(part)
                    outgoing[block, rows] = (
                        outgoing[block, rows].astype(jnp.float32)
                        + incoming[block, rows].astype(jnp.float32)
                    ).astype(jnp.bfloat16)
                    pass_sum(block, part, side, landing(block, side)).start()

            return carry

        lax.fori_loop(0, parts, relay_part, 0)

    def flat(ref):
        return ref[...].reshape(count * block_len, ref.shape[2])

    sent = []

    def halve(k, s):
        copies = flies[k].halve(s, views[k], shares[k][4], sems)
        for copy in copies:
            copy.start()
        sent.extend(copies)
        return copies

    def add_halve(k, s, copies):
        flies[k].add(s, views[k], shares[k][4], copies)
        return halve(k, s + 1) if s + 1 < stages else None

    def weigh(i, left, right):
        grads[i, :width] = left_inner(left, right).astype(jnp.bfloat16)

    grads[:, width:] = jnp.zeros((3, grads.shape[1] - width, units), jnp.bfloat16)
    weigh(2, flat(cot), flat(hidden))
    flights = [None, None, halve(2, 0), halve(3, 0)]
    for key in range(1, last):
        relay(key)
    gate_side = d_gate_up[:, :, :units].reshape(count * block_len, units)
    weigh(0, flat(normed), gate_side)
    flights[0] = halve(0, 0)
    for k in (2, 3):
        flights[k] = add_halve(k, 0, flights[k])
    up_side = d_gate_up[:, :, units:].reshape(count * block_len, units)
    weigh(1, flat(normed), up_side)
    flights[1] = halve(1, 0)
    for k in (0, 1):
        flights[k] = add_halve(k, 0, flights[k])
    relay(last)
    for s in range(1, stages - 1):
        for k in (2, 3, 0, 1):
            flights[k] = add_halve(k, s, flights[k])

    for side, there in ((1, has_left), (-1, has_right)):

        @pl.when(there)
        def _():
            slot = place if side == 1 else count

            def add_part(part, carry):
                pass_sum(place, part, side, slot).wait_recv()
                rows = rows_of(part)
                dn_ref[rows] += incoming[slot, rows].astype(jnp.float32)
                return carry

            lax.fori_loop(0, parts, add_part, 0)

    for k in (2, 3, 0, 1):
        add_halve(k, stages - 1, flights[k])
    mine = pl.ds(pl.multiple_of(row * pieces_hbm.shape[1], pieces_hbm.shape[1]), pieces_hbm.shape[1])
    save = pltpu.make_async_copy(grads.at[:, mine], pieces_hbm, load_sem.at[0])
    save.start()
    for copy in sent:
        copy.wait_send()

    for side, there in ((-1, has_left), (1, has_right)):

        @pl.when(there)
        def _():
            pass_block(place, side, count + (side + 1) // 2).wait_send()

    for block in range(count):

        @pl.when((block != place) & has_left & has_right)
        def _():
            pass_block(block, 1, block).wait_send()

        @pl.when(block != place)
        def _():
            for part in range(parts):
                pass_sum(block, part, 1, block).wait_send()

    for turn in (count - 2, count - 1):
        store_out(turn, 0).wait()
    save.wait()


def feed_forward(normed, cot_all, gate_up, down):
    count = lax.axis_size("mp")
    data_count = lax.axis_size("dp")
    block_len, width = normed.shape
    units = down.shape[1]
    padded = gate_up.shape[0]
    parts = 2
    low = jnp.bfloat16
    anywhere = pl.BlockSpec(memory_space=pl.ANY)
    dma = pltpu.SemaphoreType.DMA
    tokens = count * block_len
    height = padded // data_count
    span = data_count - 1
    most = (units // 2 + 127) // 128 * 128
    out_terms, dn, pieces = pl.pallas_call(
        functools.partial(feed_forward_kernel, data_count, count, parts),
        out_shape=[
            jax.ShapeDtypeStruct((count, block_len, width), low),
            jax.ShapeDtypeStruct((block_len, width), jnp.float32),
            jax.ShapeDtypeStruct((3, height, units), low),
        ],
        in_specs=[anywhere] * 4,
        out_specs=[anywhere, pl.BlockSpec(memory_space=pltpu.VMEM), anywhere],
        scratch_shapes=[
            pltpu.VMEM((count, block_len, width), low),
            pltpu.VMEM((count, block_len, width), low),
            pltpu.VMEM((width, 2 * units), low),
            pltpu.VMEM((width, units), low),
            pltpu.VMEM((count, block_len, units), low),
            pltpu.VMEM((count, block_len, 2 * units), low),
            pltpu.VMEM((count, block_len, width), low),
            pltpu.VMEM((count + 1, block_len, width), low),
            pltpu.VMEM((2, block_len, width), low),
            pltpu.VMEM((3, padded, units), low),
            pltpu.VMEM((2, span, height, units), low),
            pltpu.VMEM((span, height, most), low),
            pltpu.VMEM((span, height, units - most), low),
            dma((4,)),
            dma((2,)),
            dma((count + 2,)),
            dma((count,)),
            dma((count, parts)),
            dma((count + 1, parts)),
            dma((4 * span,)),
            dma((4 * span,)),
        ],
        compiler_params=pltpu.CompilerParams(
            collective_id=1, has_side_effects=True, vmem_limit_bytes=60 << 20
        ),
        cost_estimate=pl.CostEstimate(
            flops=18 * tokens * width * units,
            bytes_accessed=12 * width * units + 6 * tokens * width,
            transcendentals=tokens * units,
        ),
        name="feed_forward",
    )(normed, cot_all.reshape(count, block_len, width), gate_up, down)
    return out_terms.reshape(tokens, width), dn, pieces


def ff_parts(units):
    most = (units // 2 + 127) // 128 * 128
    return ((0, 0, units, 0), (1, 0, units, 1), (2, 0, most, 0), (2, most, units - most, 1))


def attend_back_kernel(
    data_count,
    count,
    slots,
    dn_hbm,
    middle_hbm,
    cot_hbm,
    gain_ref,
    proj_hbm,
    own_hbm,
    qkv_hbm,
    probs_hbm,
    norm_hbm,
    qkv_low_hbm,
    onehot_hbm,
    ff_hbm,
    d_middle_hbm,
    terms_hbm,
    d_qkv_w_hbm,
    d_out_w_hbm,
    spread_hbm,
    dn,
    middle,
    cot,
    proj,
    own,
    qkv,
    probs,
    norm,
    qkv_low,
    onehot,
    d_own,
    grad,
    diag,
    dk,
    dv,
    d_qkv,
    terms,
    d_qkv_w,
    d_out_w,
    load_sem,
    probs_sem,
    cross_send,
    cross_recv,
    up_send,
    up_recv,
):
    place = lax.axis_index("mp")
    me = lax.axis_index("dp")
    block_len, width = dn.shape
    seq_len = qkv.shape[0]
    lanes = slots * HD
    padded = d_qkv_w.shape[0]
    steps = seq_len // BLOCK
    f32 = jnp.float32
    low = jnp.bfloat16

    loads = []

    def load(src, dst):
        copy = pltpu.make_async_copy(src, dst, load_sem.at[len(loads)])
        copy.start()
        loads.append(copy)

    load(dn_hbm, dn)
    load(middle_hbm, middle)
    load(cot_hbm, cot)
    load(proj_hbm, proj)
    load(own_hbm, own)
    load(qkv_hbm, qkv)
    load(norm_hbm, norm)
    load(qkv_low_hbm, qkv_low)
    load(onehot_hbm, onehot)
    height = padded // data_count
    mine = pl.ds(pl.multiple_of(me * height, height), height)
    load(ff_hbm, spread_hbm.at[:, mine])

    ways = orders(data_count)
    stages = len(ways[0])
    parts = ff_parts(spread_hbm.shape[2])
    span = data_count - 1
    flies = [Butterfly(ways[way], k * span) for k, (_, _, _, way) in enumerate(parts)]
    views = [row_pieces(spread_hbm.at[i], data_count, at, wide) for i, at, wide, _ in parts]
    others = [(place + k) % count for k in range(1, count)]
    greet([flies[0].partner(s) for s in range(1, stages)] + [(me, other) for other in others])
    sent = []

    def start(copies):
        for copy in copies:
            copy.start()
        sent.extend(copies)
        return copies

    flights = [
        start(
            fly.double(
                stages - 1, view, (up_send, up_recv), ff_hbm.at[i, :, pl.ds(at, wide)]
            )
        )
        for fly, view, (i, at, wide, _) in zip(flies, views, parts)
    ]

    table = turn_order(count)

    def fetch(t):
        per = block_len // BLOCK
        block = look_up(table, place, t // per) * per + t % per
        rows = pl.ds(pl.multiple_of(block * BLOCK, BLOCK), BLOCK)
        return block, pltpu.make_async_copy(
            probs_hbm.at[:, rows], probs.at[t % 2], probs_sem.at[t % 2]
        )

    fetch(0)[1].start()
    diag[...] = jnp.zeros_like(diag)
    dk[...] = jnp.zeros_like(dk)
    dv[...] = jnp.zeros_like(dv)
    for copy in loads[:3]:
        copy.wait()
    d_middle = cot[...].astype(f32) + norm_back(middle[...], gain_ref[...], dn[...])
    middle[...] = d_middle
    save_middle = pltpu.make_async_copy(middle, d_middle_hbm, load_sem.at[0])
    save_middle.start()
    cot[...] = d_middle.astype(low)
    loads[3].wait()
    d_all = right_inner(cot[...], proj[...]).astype(low)

    def own_rows(who):
        return pl.ds(pl.multiple_of(who * block_len, block_len), block_len)

    for k in range(count):
        d_own[k] = d_all[:, k * lanes : (k + 1) * lanes]
    start(
        [
            pltpu.make_async_remote_copy(
                src_ref=d_own.at[other],
                dst_ref=grad.at[own_rows(place)],
                send_sem=cross_send.at[k],
                recv_sem=cross_recv.at[place],
                device_id=(me, other),
                device_id_type=pl.DeviceIdType.MESH,
            )
            for k, other in enumerate(others)
        ]
    )
    grad[own_rows(place)] = d_own[place]
    loads[4].wait()
    d_out_w[width:] = jnp.zeros((padded - width, count * lanes), low)
    d_out_w[:width] = left_inner(cot[...], own[...]).astype(low)
    save_out = pltpu.make_async_copy(d_out_w, d_out_w_hbm, load_sem.at[1])
    save_out.start()
    loads[5].wait()

    def pass_on(s):
        for k, (fly, view) in enumerate(zip(flies, views)):
            for copy in flights[k]:
                copy.wait_recv()
            if s > 1:
                flights[k] = start(fly.double(s - 1, view, (up_send, up_recv)))

    def back_block(t, carry):
        per = block_len // BLOCK

        @pl.when((t > 0) & (t % per == 0))
        def _():
            who = look_up(table, place, t // per)
            pltpu.make_async_remote_copy(
                src_ref=d_own.at[0],
                dst_ref=grad.at[own_rows(who)],
                send_sem=cross_send.at[0],
                recv_sem=cross_recv.at[who],
                device_id=(me, who),
                device_id_type=pl.DeviceIdType.MESH,
            ).wait_recv()

        @pl.when(t + 1 < steps)
        def _():
            fetch(t + 1)[1].start()

        block, arrival = fetch(t)
        arrival.wait()
        rows = pl.ds(pl.multiple_of(block * BLOCK, BLOCK), BLOCK)
        window = pl.ds(pl.multiple_of((steps - 1 - block) * BLOCK, BLOCK), seq_len)
        queries = qkv[rows, 0:lanes]
        keys = qkv[:, lanes : 2 * lanes]
        values = qkv[:, 2 * lanes : 3 * lanes]
        d_query = jnp.zeros((BLOCK, lanes), f32)
        for slot in range(slots):
            weight = probs[t % 2, slot]
            slot_grad = slot_lanes(grad[rows], slot)
            d_probs = right_inner(slot_grad, values)
            delta = jnp.sum(weight * d_probs, axis=-1, keepdims=True)
            d_scores = (weight * (d_probs - delta)).astype(low)
            d_query = d_query + slot_lanes(product(d_scores, keys), slot)
            dk[...] += left_inner(slot_lanes(queries, slot), d_scores)
            dv[...] += left_inner(slot_grad, weight.astype(low))
            diag[slot, :, window] += d_scores.astype(f32)
        d_qkv[rows, 0:lanes] = d_query.astype(low)
        return carry

    loads[9].wait()
    pass_on(stages - 1)
    lax.fori_loop(0, steps, back_block, 0)
    for s in reversed(range(2, stages - 1)):
        pass_on(s)
    d_qkv[:, lanes : 2 * lanes] = dk[...].T.astype(low)
    d_qkv[:, 2 * lanes : 3 * lanes] = dv[...].T.astype(low)
    for copy in loads[6:9]:
        copy.wait()
    terms[...] = right_inner(d_qkv[...], qkv_low[:width]).astype(low)
    save_terms = pltpu.make_async_copy(terms, terms_hbm, load_sem.at[2])
    save_terms.start()
    d_qkv_w[:width] = left_inner(norm[...], d_qkv[...]).astype(low)
    d_qkv_w[width:] = jnp.zeros((padded - width, 3 * lanes), low)
    sums = []
    for slot in range(slots):
        level = diag[slot]
        rest = BLOCK // 2
        while rest >= 1:
            level = pltpu.roll(level[:rest], rest, 1) + level[rest:]
            rest //= 2
        sums.append(level)
    sums = jnp.concatenate(sums + [jnp.zeros((128 - slots, 2 * seq_len), f32)], axis=0)
    d_rel = lax.dot_general(
        onehot[...],
        sums,
        (((1,), (1,)), ((), ())),
        precision=highest,
        preferred_element_type=f32,
    )
    d_qkv_w[width : width + BUCKETS, :128] = d_rel.astype(low)
    save_qkv = pltpu.make_async_copy(d_qkv_w, d_qkv_w_hbm, load_sem.at[3])
    save_qkv.start()
    if stages > 1:
        pass_on(1)
    for copy in sent:
        copy.wait_send()
    for copy in (save_middle, save_out, save_terms, save_qkv):
        copy.wait()


def attend_back(dn, middle, cot, gain, proj_all, own, qkv, probs, norm, qkv_low, onehot, ff_pieces):
    count = lax.axis_size("mp")
    data_count = lax.axis_size("dp")
    seq_len = qkv.shape[0]
    slots = probs.shape[0]
    lanes = slots * HD
    block_len, width = dn.shape
    padded = qkv_low.shape[0]
    _, _, units = ff_pieces.shape
    far = pl.BlockSpec(memory_space=pltpu.HBM)
    near = pl.BlockSpec(memory_space=pltpu.VMEM)
    dma = pltpu.SemaphoreType.DMA
    low, f32 = jnp.bfloat16, jnp.float32
    span = data_count - 1
    scratch = [
        (dn.shape, f32),
        (middle.shape, f32),
        (cot.shape, low),
        (proj_all.shape, low),
        (own.shape, low),
        (qkv.shape, low),
        ((2, slots, BLOCK, seq_len), f32),
        (norm.shape, low),
        (qkv_low.shape, low),
        (onehot.shape, f32),
        ((count, block_len, lanes), low),
        ((seq_len, lanes), low),
        ((slots, BLOCK, 2 * seq_len), f32),
        ((lanes, seq_len), f32),
        ((lanes, seq_len), f32),
        (qkv.shape, low),
        ((seq_len, width), low),
        ((padded, 3 * lanes), low),
        ((padded, count * lanes), low),
    ]
    return pl.pallas_call(
        functools.partial(attend_back_kernel, data_count, count, slots),
        in_specs=[far] * 3 + [near] + [far] * 8,
        out_specs=[far] * 5,
        out_shape=[
            jax.ShapeDtypeStruct((block_len, width), f32),
            jax.ShapeDtypeStruct((seq_len, width), low),
            jax.ShapeDtypeStruct((padded, 3 * lanes), low),
            jax.ShapeDtypeStruct((padded, count * lanes), low),
            jax.ShapeDtypeStruct((3, padded, units), low),
        ],
        scratch_shapes=[pltpu.VMEM(shape, dtype) for shape, dtype in scratch]
        + [
            dma((10,)),
            dma((2,)),
            dma((count - 1,)),
            dma((count,)),
            dma((4 * span,)),
            dma((4 * span,)),
        ],
        compiler_params=pltpu.CompilerParams(
            collective_id=3, has_side_effects=True, vmem_limit_bytes=56 << 20
        ),
        cost_estimate=pl.CostEstimate(
            flops=16 * slots * seq_len * seq_len * HD, bytes_accessed=140 << 20, transcendentals=0
        ),
        name="attend_back",
    )(dn, middle, cot, gain, proj_all, own, qkv, probs, norm, qkv_low, onehot, ff_pieces)


def to_owners(rows_of_slots):
    count = lax.axis_size("mp")
    seq_len, lanes = rows_of_slots.shape
    pieces = rows_of_slots.reshape(count, seq_len // count, lanes)
    pieces = lax.all_to_all(pieces, "mp", split_axis=0, concat_axis=0)
    return pieces.transpose(1, 0, 2).reshape(seq_len // count, count * lanes)


def local(
    layer_in,
    segment_ids,
    bucket_table,
    attn_gain,
    query_weight,
    key_weight,
    value_weight,
    out_weight,
    rel_bias,
    ff_gain,
    gate_weight,
    up_weight,
    down_weight,
    cotangent,
):
    _, local_len, model_width = layer_in.shape
    seq_len = segment_ids.shape[1]
    lane_width = query_weight.shape[1]
    slots_here = lane_width // HD
    ff_width = gate_weight.shape[1]
    tensor_index = lax.axis_index("mp")
    tensor_count = lax.axis_size("mp")
    data_index = lax.axis_index("dp")
    data_count = lax.axis_size("dp")
    layer_in = layer_in[0]
    cotangent = cotangent[0]
    slot_ids = tensor_index * slots_here + jnp.arange(slots_here)
    slot_valid = ((slot_ids < 5) | (slot_ids == 6)).astype(jnp.float32)
    lane_mask = jnp.repeat(slot_valid, HD)
    qkv_low = (
        jnp.concatenate([query_weight, key_weight, value_weight], axis=1) * jnp.tile(lane_mask, 3)
    ).astype(jnp.bfloat16)
    proj_low = (out_weight * lane_mask[:, None]).astype(jnp.bfloat16)
    piece = 16 * data_count
    padded = (model_width + piece - 1) // piece * piece
    extra = padded - model_width
    gate_up_low = jnp.concatenate([gate_weight, up_weight], axis=1).astype(jnp.bfloat16)
    gate_up_low = jnp.pad(gate_up_low, ((0, extra), (0, 0)))
    squares = [
        jnp.sum(w * w)
        for w in (
            query_weight,
            key_weight,
            value_weight,
            rel_bias,
            gate_weight,
            up_weight,
            out_weight,
            down_weight,
        )
    ]
    squares = jnp.pad(jnp.stack(squares), (0, 120)).reshape(1, 128)
    down_turned = down_weight.T
    out_turned = out_weight.T
    down_low = down_turned.astype(jnp.bfloat16)
    onehot = (bucket_table[:, None] == jnp.arange(BUCKETS)[None, :]).astype(jnp.float32)
    onehot = jnp.pad(onehot, ((0, 1), (0, 0)))
    onehot_turned = onehot.T
    qkv_padded = jnp.pad(qkv_low, ((0, extra), (0, 0)))
    vector = lax.dot_general(
        rel_bias,
        onehot,
        (((0,), (1,)), ((), ())),
        precision=highest,
        preferred_element_type=jnp.float32,
    )
    residual_in = layer_in.astype(jnp.float32)
    normed_local = rms_norm(residual_in, attn_gain).astype(jnp.bfloat16)
    flat_norm = lax.all_gather(normed_local, "mp", axis=0, tiled=True)
    proj_all = gather_proj(proj_low)
    (
        flat_norm,
        late_cot,
        proj_all,
        qkv_low,
        gate_up_low,
        down_low,
        vector,
        squares,
        onehot_turned,
        qkv_padded,
    ) = lax.optimization_barrier(
        (
            flat_norm,
            cotangent,
            proj_all,
            qkv_low,
            gate_up_low,
            down_low,
            vector,
            squares,
            onehot_turned,
            qkv_padded,
        )
    )
    flat_cot = lax.all_gather(late_cot, "mp", axis=0, tiled=True)
    qkv = product(flat_norm, qkv_low).astype(jnp.bfloat16)
    attended, probs = attend(qkv, segment_ids.reshape(seq_len, 1), segment_ids, vector)
    own_attended = to_owners(attended)
    middle = residual_in + product(own_attended, proj_all)
    normed_ff_local = rms_norm(middle, ff_gain).astype(jnp.bfloat16)
    out_terms, dn_ff, ff_pieces = feed_forward(normed_ff_local, flat_cot, gate_up_low, down_low)
    d_middle, dn_attn_terms, d_qkv_w, d_out_w, ff_grads = attend_back(
        dn_ff,
        middle,
        cotangent,
        ff_gain.reshape(1, model_width),
        proj_all,
        own_attended,
        qkv,
        probs,
        flat_norm,
        qkv_padded,
        onehot_turned,
        ff_pieces,
    )
    ff_branch = lax.psum_scatter(out_terms, "mp", scatter_dimension=0, tiled=True)
    layer_out = (middle + ff_branch.astype(jnp.float32)).astype(jnp.bfloat16)
    dn_attn = lax.psum_scatter(dn_attn_terms, "mp", scatter_dimension=0, tiled=True)
    *grads, shared, own, tall = sum_weights(
        ff_grads, d_qkv_w, d_out_w, qkv_padded, gate_up_low, squares, model_width
    )
    weights = (
        gate_weight,
        up_weight,
        down_turned,
        query_weight,
        key_weight,
        value_weight,
        out_turned,
    )
    results = update(grads, weights, rel_bias, attn_gain, ff_gain, shared, own, tall)
    news, along, across = results[:8], results[8:16], results[16:24]
    new_attn_gain, attn_gain_moment, new_ff_gain, ff_gain_moment = results[24:]
    gate, up, down, query, key, value, out, rel = zip(news, along, across)
    rel = (rel[0], rel[1].reshape(BUCKETS), rel[2].reshape(slots_here))
    down = (down[0].T, down[2], down[1])
    out = (out[0].T, out[2], out[1])
    input_grad = d_middle + norm_back(residual_in, attn_gain, dn_attn.astype(jnp.float32))
    input_grad = input_grad.astype(jnp.bfloat16)
    return (
        layer_out[None],
        input_grad[None],
        new_attn_gain,
        attn_gain_moment,
        *query,
        *key,
        *value,
        *out,
        *rel,
        new_ff_gain,
        ff_gain_moment,
        *gate,
        *up,
        *down,
    )


def solution(mesh):
    return jax.shard_map(
        local,
        mesh=mesh,
        in_specs=(
            P("dp", "mp", None),
            P("dp", None),
            P(),
            P(),
            P(None, "mp"),
            P(None, "mp"),
            P(None, "mp"),
            P("mp", None),
            P(None, "mp"),
            P(),
            P(None, "mp"),
            P(None, "mp"),
            P("mp", None),
            P("dp", "mp", None),
        ),
        out_specs=(
            P("dp", "mp", None),
            P("dp", "mp", None),
            P(),
            P(),
            P(None, "mp"),
            P(),
            P("mp"),
            P(None, "mp"),
            P(),
            P("mp"),
            P(None, "mp"),
            P(),
            P("mp"),
            P("mp", None),
            P("mp"),
            P(),
            P(None, "mp"),
            P(),
            P("mp"),
            P(),
            P(),
            P(None, "mp"),
            P(),
            P("mp"),
            P(None, "mp"),
            P(),
            P("mp"),
            P("mp", None),
            P("mp"),
            P(),
        ),
        check_vma=False,
    )
```

time: 543 us -> 435 us (0.80)
  the two profiles are of different devices: /device:TPU:0 before, /device:TPU:11 now
where the time goes in v3:
time: 435 us; the launch traced here: 428 us
  Pallas kernels  305 us (70%)
  waiting for transfers between devices  39.6 us (9%)
  other arithmetic  25.2 us (6%)
  blocking collectives  19.1 us (4%)
  local copies, waits for them, and re-layouts  18.2 us (4%)
  between operations  14.5 us (3%)
  matrix products  6.31 us (1%)
    pallas_call x1, Pallas kernels, feed_forward(): pl.pallas_call(functools.partial(feed_forward_kernel, data_count, count,...  114 us
    pallas_call x1, Pallas kernels, sum_weights(): pl.pallas_call(functools.partial(sum_weights_kernel, data_count, count, m...  76.7 us
    pallas_call x1, Pallas kernels, attend_back(): pl.pallas_call(functools.partial(attend_back_kernel, data_count, count, s...  56.4 us
    all_gather x1, waiting for transfers between devices, local(): flat_cot = lax.all_gather(late_cot, 'mp', axis=0, tiled=True)  29.4 us
    pallas_call x1, Pallas kernels, gather_proj(): pl.pallas_call(functools.partial(gather_proj_kernel, data_count, count),...  24.2 us
    pallas_call x1, Pallas kernels, update(): pl.pallas_call(functools.partial(update_kernel, tensor_count), grid=(chun...  21.7 us
    all_to_all x1, blocking collectives, to_owners(): pieces = lax.all_to_all(pieces, 'mp', split_axis=0, concat_axis=0)  19.1 us
    pallas_call x1, Pallas kernels, attend(): pl.pallas_call(functools.partial(attend_kernel, seq_len, slots), grid=(se...  11.8 us
  transfers between devices with their start and end apart: 4, of which 2 were waited for; matrix products, arithmetic and copies ran while one was open for 10% of the time, Pallas kernels for 45%

profile of v3, /device:TPU:11, one launch (start us, length us, event | category | flops | bytes accessed | tf_op | source)
XLA Modules:
  0.0 427.8 jit_solution(538666540897024834)
XLA Ops:
  7.3 1.4 copy.63
  8.7 0.2 fusion.13
  8.9 1.1 fusion.7
  10.1 0.0 all-gather.5.cloned.1.call-start
  10.2 1.2 copy.64
  11.3 0.1 broadcast_in_dim.10
  11.4 0.1 mul.119
  11.5 0.8 multiply_reduce_fusion.4
  12.3 0.9 copy.65
  13.2 24.2 %gather_proj.1 = bf16[4,8,16,1472]{3,2,1,0:T(8,128)(2,1)} custom-call(bf16[8,16,1472]{2,1,0:T(8,128)(2,1)} %bitcast.66), custom_call_target="tpu_custom_call" | custom-call | bytes 52428800 | tf_op jit(solution)/shard_map/gather_proj/pallas_call | solution.py:672
  37.5 0.2 fusion.3
  37.7 1.1 pad.23.qkv_low_hbm.refs_3_
  38.8 0.3 copy-done.8
  39.1 0.6 multiply_reduce_fusion.8
  39.7 0.8 multiply_reduce_fusion.7
  40.5 0.8 multiply_reduce_fusion.6
  41.3 0.8 multiply_reduce_fusion.5
  42.1 3.4 multiply_reduce_fusion
  45.5 3.4 multiply_reduce_fusion.1
  48.9 5.3 %stack.35 = f32[8]{0:T(128)S(1)} concatenate(f32[1]{0:T(128)} %bitcast.8, f32[1]{0:T(128)} %bitcast.9, f32[1]{0:T(128)} %bitcast.10, f32[1]{0:T(128)} %bitcast.11, f32[1]{0:T(128)} %bitcast.12, f32[1]{0:T(128)} %bitcast.13, f32[1]{0:T(128)} %bitcast.14, f32[1]{0:T(128)} %bitcast.15), dimensions={0} | concatenate | bytes 64 | tf_op jit(solution)/shard_map/stack | solution.py:1412
  54.2 0.5 pad_bitcast_fusion.refs_5_
  54.7 0.8 convolution_bitcast_fusion.vec_ref
  55.5 0.7 convert_bitcast_fusion.onehot_hbm
  56.2 6.2 %fusion.2.gate_up_hbm.refs_4_ = bf16[1536,1792]{1,0:T(8,128)(2,1)} fusion(bf16[1472,896]{1,0:T(8,128)(2,1)S(1)} %get-tuple-element.235, bf16[1472,896]{1,0:T(8,128)(2,1)} %get-tuple-element.242), kind=kLoop, calls=%fused_computation.3 | loop fusion | flops 19267584 | bytes 10780672 | tf_op jit(solution)/shard_map/concatenate | solution.py:1397
  62.4 10.2 %all-gather.3.cloned.1.call-done.norm_hbm = bf16[1024,1472]{1,0:T(8,128)(2,1)} async-done(((bf16[256,1472]{1,0:T(8,128)(2,1)}), bf16[1024,1472]{1,0:T(8,128)(2,1)}) %all-gather.3.cloned.1.call-update) | async-done | bytes 3014672 | tf_op jit(solution)/shard_map/all_gather | solution.py:1429
  72.6 0.0 reduce-scatter.3.cloned.1.call-start
  72.6 1.0 copy.66.seg_col_ref
  73.7 4.9 %convolution_convert_fusion.qkv_ref.qkv_hbm = bf16[1024,384]{1,0:T(8,128)(2,1)} fusion(bf16[1024,1472]{1,0:T(8,128)(2,1)} %all-gather.3.cloned.1.call-done.norm_hbm, bf16[1472,384]{1,0:T(8,128)(2,1)} %copy-done.8), kind=kOutput, calls=%fused_computation.27 | convolution fusion | flops 1158021120 | bytes 4931584 | tf_op jit(solution)/shard_map/dot_general | solution.py:31
  78.5 11.8 %attend.1 = (bf16[1024,128]{1,0:T(8,128)(2,1)}, f32[2,1024,1024]{2,1,0:T(8,128)}) custom-call(bf16[1024,384]{1,0:T(8,128)(2,1)} %convolution_convert_fusion.qkv_ref.qkv_hbm, s32[1024,1]{1,0:T(8,128)} %copy.66.seg_col_ref, s32[1,1024]{1,0:T(1,128)} %seg_row_ref.1, f32[2,2048]{1,0:T(2,128)} %convolution_bitcast_fusion.vec_ref), custom_call_target="tpu_custom_call" | custom-call | flops 1073741824 | bytes 8388608 | tf_op jit(solution)/shard_map/attend/pallas_call | solution.py:86
  90.3 19.1 %all_to_all.5 = bf16[4,256,128]{2,1,0:T(8,128)(2,1)S(1)} all-to-all(bf16[4,256,128]{2,1,0:T(8,128)(2,1)} %bitcast.67), channel_id=1, replica_groups=mesh['dp'=8,'mp'=4] {'mp'}, dimensions={0} | all-to-all | bytes 524288 | tf_op jit(solution)/shard_map/all_to_all | solution.py:1356
  109.4 0.7 multiply_reduce_fusion.3
  110.1 1.3 multiply_convert_fusion.normed_hbm
  111.5 29.4 %all-gather.5.cloned.1.call-done = bf16[1024,1472]{1,0:T(8,128)(2,1)} async-done(((bf16[256,1472]{1,0:T(8,128)(2,1)}), bf16[1024,1472]{1,0:T(8,128)(2,1)}) %all-gather.5.cloned.1.call-update) | async-done | bytes 3014672 | tf_op jit(solution)/shard_map/all_gather | solution.py:1456
  140.9 113.8 %feed_forward.1 = (bf16[4,256,1472]{2,1,0:T(8,128)(2,1)}, f32[256,1472]{1,0:T(8,128)}, bf16[3,192,896]{2,1,0:T(8,128)(2,1)}) custom-call(bf16[256,1472]{1,0:T(8,128)(2,1)} %multiply_convert_fusion.normed_hbm, bf16[4,256,1472]{2,1,0:T(8,128)(2,1)} %bitcast.70, bf16[1536,1792]{1,0:T(8,128)(2,1)} %fusion.2.gate_up_hbm.refs_4_, ...), custom_call_target="tpu_custom_call" | custom-call | flops 24310185984 | bytes 24870912 | tf_op jit(solution)/shard_map/feed_forward/pallas_call | solution.py:997
  254.7 0.0 reduce-scatter.5.cloned.1.call-start
  254.8 0.6 broadcast_in_dim.24.gain_ref.refs_15_
  255.4 0.7 copy_bitcast_fusion.own_hbm
  256.1 56.4 %attend_back.1 = (f32[256,1472]{1,0:T(8,128)}, bf16[1024,1472]{1,0:T(8,128)(2,1)}, bf16[1536,384]{1,0:T(8,128)(2,1)}, bf16[1536,512]{1,0:T(8,128)(2,1)}, bf16[3,1536,896]{2,1,0:T(8,128)(2,1)}) custom-call(f32[256,1472]{1,0:T(8,128)} %get-tuple-element.95.dn_hbm, f32[256,1472]{1,0:T(8,128)} %copy-done, bf16[256,1472]{1,0:T(8,128)(2,1)} %bitcast.63, ...), custom_call_target="tpu_custom_call" | custom-call | flops 2147483648 | bytes 146800640 | tf_op jit(solution)/shard_map/attend_back/pallas_call | solution.py:1322
  312.6 0.7 copy.69.refs_13_
  313.3 0.6 broadcast_in_dim.26.refs_14_
  313.9 76.7 %sum_weights.1 = (bf16[1536,896]{1,0:T(8,128)(2,1)}, bf16[1536,896]{1,0:T(8,128)(2,1)}, bf16[1536,896]{1,0:T(8,128)(2,1)}, bf16[1536,384]{1,0:T(8,128)(2,1)}, bf...) custom-call(bf16[3,1536,896]{2,1,0:T(8,128)(2,1)} %get-tuple-element.102.refs_0_, ...), custom_call_target="tpu_custom_call" | custom-call | flops 1376256 | bytes 209715200 | tf_op jit(solution)/shard_map/sum_weights/pallas_call | solution.py:439
  390.6 21.7 %update.1 = (f32[1472,896]{1,0:T(8,128)}, f32[1472,896]{1,0:T(8,128)}, f32[1472,896]{1,0:T(8,128)}, f32[1472,128]{1,0:T(8,128)}, f32[1472,128]{1,0:T(8,128)}, /*...) custom-call(bf16[1536,896]{1,0:T(8,128)(2,1)} %get-tuple-element.106, ...), custom_call_target="tpu_custom_call" | custom-call | flops 52756480 | bytes 47480832 | tf_op jit(solution)/shard_map/update/pallas_call | solution.py:568
  412.3 1.4 copy.72
  413.7 1.3 fusion.14
  415.0 1.1 copy.70
  416.1 1.6 fusion.8
  417.8 1.9 fusion.15
  419.7 1.1 copy.71
  (51 shorter events, 0.3 us)
Async XLA Ops:
  7.2 1.7 copy-start.12
  7.2 65.3 %all-gather.3.cloned.1.call-start = ((), (), s32[]{:S(2)}) async-start(), calls=%async_computation.3 | async-start | bytes 3932160 | tf_op jit(solution)/shard_map/all_gather | solution.py:1429
  8.7 1.5 copy-start.11
  8.9 2.6 copy-start.10
  10.1 130.8 %all-gather.5.cloned.1.call-start = ((), (), s32[]{:S(2)}) async-start(), calls=%async_computation.4 | async-start | bytes 3932160 | tf_op jit(solution)/shard_map/all_gather | solution.py:1456
  12.3 25.2 %copy-start.5 = (f32[1472,128]{1,0:T(8,128)S(1)}, f32[1472,128]{1,0:T(8,128)}, u32[]{:S(2)}) copy-start(f32[1472,128]{1,0:T(8,128)} %refs_11_.1) | copy-start | bytes 2260996
  12.3 25.2 %copy-start.6 = (f32[1472,128]{1,0:T(8,128)S(1)}, f32[1472,128]{1,0:T(8,128)}, u32[]{:S(2)}) copy-start(f32[1472,128]{1,0:T(8,128)} %refs_10_.1) | copy-start | bytes 2260996
  12.3 25.2 %copy-start.7 = (f32[1472,128]{1,0:T(8,128)S(1)}, f32[1472,128]{1,0:T(8,128)}, u32[]{:S(2)}) copy-start(f32[1472,128]{1,0:T(8,128)} %refs_9_.1) | copy-start | bytes 2260996
  37.5 1.6 copy-start.16
  37.5 4.6 %copy-start.3 = (f32[896,1472]{0,1:T(8,128)S(1)}, f32[896,1472]{0,1:T(8,128)}, u32[]{:S(2)}) copy-start(f32[896,1472]{0,1:T(8,128)} %param.26) | copy-start | bytes 15826948
  37.7 1.4 copy-start.8
  37.7 7.8 %copy-start.2 = (f32[1472,896]{1,0:T(8,128)S(1)}, f32[1472,896]{1,0:T(8,128)}, u32[]{:S(2)}) copy-start(f32[1472,896]{1,0:T(8,128)} %refs_6_.1) | copy-start | bytes 15826948
  39.7 5.8 %slice-start = ((s8[5275648]{0:T(1024)(128)(4,1)}), s8[4194304]{0:T(1024)(128)(4,1)S(1)}, s32[]{:S(2)}) async-start(s8[5275648]{0:T(1024)(128)(4,1)} %bitcast.57), calls=%async_computation.7 | async-start | bytes 8388608
  42.1 3.4 slice-start.1
  45.5 9.2 %copy-start.14 = (s32[2047]{0:T(1024)S(1)}, s32[2047]{0:T(1024)}, u32[]{:S(2)}) copy-start(s32[2047]{0:T(1024)} %param.16) | copy-start | bytes 24568
  56.2 16.4 %copy-start.15 = (s32[1,1024]{1,0:T(1,128)S(1)}, s32[1,1024]{1,0:T(1,128)}, u32[]{:S(2)}) copy-start(s32[1,1024]{1,0:T(1,128)} %seg_row_ref.1) | copy-start | bytes 12292
  72.6 341.1 %reduce-scatter.3.cloned.1.call-start = ((), (), s32[]{:S(2)}) async-start(), calls=%async_computation.5 | async-start | bytes 3932160 | tf_op jit(solution)/shard_map/reduce_scatter | solution.py:1477
  78.5 30.9 %copy-start.4 = (bf16[4,8,16,1472]{3,2,1,0:T(8,128)(2,1)S(1)}, bf16[4,8,16,1472]{3,2,1,0:T(8,128)(2,1)}, u32[]{:S(2)}) copy-start(bf16[4,8,16,1472]{3,2,1,0:T(8,128)(2,1)} %gather_proj.1) | copy-start | bytes 4521988
  109.4 0.7 copy-start.13
  110.1 144.6 %copy-start = (f32[256,1472]{1,0:T(8,128)}, f32[256,1472]{1,0:T(8,128)S(1)}, u32[]{:S(2)}) copy-start(f32[256,1472]{1,0:T(8,128)S(1)} %get-tuple-element.241.middle_hbm) | copy-start | bytes 4521988
  254.7 161.4 %reduce-scatter.5.cloned.1.call-start = ((), (), s32[]{:S(2)}) async-start(), calls=%async_computation.6 | async-start | bytes 3932160 | tf_op jit(solution)/shard_map/reduce_scatter | solution.py:1479
  390.6 23.1 %copy-start.1 = (f32[256,1472]{1,0:T(8,128)S(1)}, f32[256,1472]{1,0:T(8,128)}, u32[]{:S(2)}) copy-start(f32[256,1472]{1,0:T(8,128)} %copy-done) | copy-start | bytes 4521988
  416.1 1.7 copy-start.9
Sparse Core Ops, SparseCore 0:
  10.2 62.2 all-gather.2
  74.1 66.6 all-gather.4
  254.9 65.8 reduce-scatter.2
  322.9 73.5 reduce-scatter.4

commit v4 on v3

--- a/solution.py
+++ b/solution.py
@@ -46,69 +46,6 @@
 def slot_lanes(values, slot):
     lane = lax.broadcasted_iota(jnp.int32, values.shape, 1)
     return jnp.where((lane >= slot * HD) & (lane < (slot + 1) * HD), values, jnp.zeros_like(values))
-
-
-def attend_kernel(seq_len, slots, qkv_ref, seg_col_ref, seg_row_ref, vec_ref, out_ref, probs_ref, tilt_ref):
-    step = pl.program_id(0)
-    steps = seq_len // BLOCK
-    lanes = slots * HD
-
-    @pl.when(step == 0)
-    def _():
-        for slot in range(slots):
-            spread = jnp.broadcast_to(vec_ref[slot : slot + 1, :], (BLOCK, 2 * seq_len))
-            tilt_ref[slot] = pltpu.roll(
-                spread, 2 * seq_len - BLOCK + 1, 1, stride=1, stride_axis=0
-            )
-
-    same_doc = seg_col_ref[...] == seg_row_ref[...]
-    rows = pl.ds(pl.multiple_of(step * BLOCK, BLOCK), BLOCK)
-    window = pl.ds(pl.multiple_of((steps - 1 - step) * BLOCK, BLOCK), seq_len)
-    queries = qkv_ref[rows, 0:lanes]
-    keys = qkv_ref[:, lanes : 2 * lanes]
-    values = qkv_ref[:, 2 * lanes : 3 * lanes]
-    mixed = jnp.zeros((BLOCK, lanes), jnp.float32)
-    for slot in range(slots):
-        scores = right_inner(slot_lanes(queries, slot), keys) + tilt_ref[slot, :, window]
-        scores = jnp.where(same_doc, scores, -1e30)
-        peak = jnp.max(scores, axis=-1, keepdims=True)
-        raised = jnp.exp(scores - peak)
-        probs = raised * (1.0 / jnp.sum(raised, axis=-1, keepdims=True))
-        probs_ref[slot] = probs
-        mixed = mixed + slot_lanes(product(probs.astype(jnp.bfloat16), values), slot)
-    out_ref[...] = mixed.astype(jnp.bfloat16)
-
-
-def attend(qkv, seg_col, seg_row, vector):
-    seq_len = qkv.shape[0]
-    slots = vector.shape[0]
-    lanes = slots * HD
-    return pl.pallas_call(
-        functools.partial(attend_kernel, seq_len, slots),
-        grid=(seq_len // BLOCK,),
-        in_specs=[
-            pl.BlockSpec((seq_len, 3 * lanes), lambda i: (0, 0)),
-            pl.BlockSpec((BLOCK, 1), lambda i: (i, 0)),
-            pl.BlockSpec((1, seq_len), lambda i: (0, 0)),
-            pl.BlockSpec((slots, 2 * seq_len), lambda i: (0, 0)),
-        ],
-        out_specs=[
-            pl.BlockSpec((BLOCK, lanes), lambda i: (i, 0)),
-            pl.BlockSpec((slots, BLOCK, seq_len), lambda i: (0, i, 0)),
-        ],
-        out_shape=[
-            jax.ShapeDtypeStruct((seq_len, lanes), jnp.bfloat16),
-            jax.ShapeDtypeStruct((slots, seq_len, seq_len), jnp.float32),
-        ],
-        scratch_shapes=[pltpu.VMEM((slots, BLOCK, 2 * seq_len), jnp.float32)],
-        compiler_params=pltpu.CompilerParams(vmem_limit_bytes=58 << 20),
-        cost_estimate=pl.CostEstimate(
-            flops=8 * slots * seq_len * seq_len * HD,
-            bytes_accessed=4 * slots * seq_len * seq_len,
-            transcendentals=slots * seq_len * seq_len,
-        ),
-        name="attend",
-    )(qkv, seg_col, seg_row, vector)
 
 
 class Butterfly:
@@ -601,91 +538,6 @@
         *grads, grads[3], *weights, rel_w,
         attn_w.reshape(1, width), ff_w.reshape(1, width), shared, own, tall,
     )
-
-
-def gather_proj_kernel(data_count, count, own_ref, all_ref, load_sem, cross_send, cross_recv, side_send, side_recv):
-    me = lax.axis_index("dp")
-    place = lax.axis_index("mp")
-    others = [(place + k) % count for k in range(1, count)]
-    peers = [(me + k) % data_count for k in range(1, data_count)]
-    load = pltpu.make_async_copy(own_ref, all_ref.at[place], load_sem)
-    load.start()
-    greet([(me, other) for other in others] + [(peer, place) for peer in peers])
-    sent = []
-    for k, other in enumerate(others):
-        copy = pltpu.make_async_remote_copy(
-            src_ref=own_ref.at[me],
-            dst_ref=all_ref.at[place, me],
-            send_sem=cross_send.at[k],
-            recv_sem=cross_recv.at[count - 2 - k],
-            device_id=(me, other),
-            device_id_type=pl.DeviceIdType.MESH,
-        )
-        copy.start()
-        sent.append(copy)
-    arrivals = []
-    for k, other in enumerate(others):
-        pltpu.make_async_remote_copy(
-            src_ref=own_ref.at[me],
-            dst_ref=all_ref.at[other, me],
-            send_sem=cross_send.at[k],
-            recv_sem=cross_recv.at[k],
-            device_id=(me, other),
-            device_id_type=pl.DeviceIdType.MESH,
-        ).wait_recv()
-        for j, peer in enumerate(peers):
-            slot = k * (data_count - 1)
-            copy = pltpu.make_async_remote_copy(
-                src_ref=all_ref.at[other, me],
-                dst_ref=all_ref.at[other, me],
-                send_sem=side_send.at[slot + j],
-                recv_sem=side_recv.at[slot + data_count - 2 - j],
-                device_id=(peer, place),
-                device_id_type=pl.DeviceIdType.MESH,
-            )
-            copy.start()
-            sent.append(copy)
-            arrivals.append(
-                pltpu.make_async_remote_copy(
-                    src_ref=all_ref.at[other, peer],
-                    dst_ref=all_ref.at[other, peer],
-                    send_sem=side_send.at[slot + j],
-                    recv_sem=side_recv.at[slot + j],
-                    device_id=(peer, place),
-                    device_id_type=pl.DeviceIdType.MESH,
-                )
-            )
-    for arrival in arrivals:
-        arrival.wait_recv()
-    for copy in sent:
-        copy.wait_send()
-    load.wait()
-
-
-def gather_proj(proj_low):
-    count = lax.axis_size("mp")
-    data_count = lax.axis_size("dp")
-    lanes, width = proj_low.shape
-    part = lanes // data_count
-    anywhere = pl.BlockSpec(memory_space=pl.ANY)
-    dma = pltpu.SemaphoreType.DMA
-    gathered = pl.pallas_call(
-        functools.partial(gather_proj_kernel, data_count, count),
-        out_shape=jax.ShapeDtypeStruct((count, data_count, part, width), proj_low.dtype),
-        in_specs=[anywhere],
-        out_specs=anywhere,
-        scratch_shapes=[
-            dma,
-            dma((count - 1,)),
-            dma((count - 1,)),
-            dma(((count - 1) * (data_count - 1),)),
-            dma(((count - 1) * (data_count - 1),)),
-        ],
-        compiler_params=pltpu.CompilerParams(collective_id=0, has_side_effects=True),
-        cost_estimate=pl.CostEstimate(flops=0, bytes_accessed=50 << 20, transcendentals=0),
-        name="gather_proj",
-    )(proj_low.reshape(data_count, part, width))
-    return gathered.reshape(count * lanes, width)
 
 
 def turn_order(count):
@@ -1058,7 +910,7 @@
     probs_hbm,
     norm_hbm,
     qkv_low_hbm,
-    onehot_hbm,
+    bucket_ref,
     ff_hbm,
     d_middle_hbm,
     terms_hbm,
@@ -1074,7 +926,6 @@
     probs,
     norm,
     qkv_low,
-    onehot,
     d_own,
     grad,
     diag,
@@ -1116,7 +967,6 @@
     load(qkv_hbm, qkv)
     load(norm_hbm, norm)
     load(qkv_low_hbm, qkv_low)
-    load(onehot_hbm, onehot)
     height = padded // data_count
     mine = pl.ds(pl.multiple_of(me * height, height), height)
     load(ff_hbm, spread_hbm.at[:, mine])
@@ -1162,13 +1012,13 @@
     dv[...] = jnp.zeros_like(dv)
     for copy in loads[:3]:
         copy.wait()
-    d_middle = cot[...].astype(f32) + norm_back(middle[...], gain_ref[...], dn[...])
+    d_middle = cot[...].astype(f32) + norm_back(middle[...], gain_ref[...].reshape(1, width), dn[...])
     middle[...] = d_middle
     save_middle = pltpu.make_async_copy(middle, d_middle_hbm, load_sem.at[0])
     save_middle.start()
     cot[...] = d_middle.astype(low)
     loads[3].wait()
-    d_all = right_inner(cot[...], proj[...]).astype(low)
+    d_all = product(cot[...], proj[:width]).astype(low)
 
     def own_rows(who):
         return pl.ds(pl.multiple_of(who * block_len, block_len), block_len)
@@ -1243,14 +1093,14 @@
         d_qkv[rows, 0:lanes] = d_query.astype(low)
         return carry
 
-    loads[9].wait()
+    loads[8].wait()
     pass_on(stages - 1)
     lax.fori_loop(0, steps, back_block, 0)
     for s in reversed(range(2, stages - 1)):
         pass_on(s)
     d_qkv[:, lanes : 2 * lanes] = dk[...].T.astype(low)
     d_qkv[:, 2 * lanes : 3 * lanes] = dv[...].T.astype(low)
-    for copy in loads[6:9]:
+    for copy in loads[6:8]:
         copy.wait()
     terms[...] = right_inner(d_qkv[...], qkv_low[:width]).astype(low)
     save_terms = pltpu.make_async_copy(terms, terms_hbm, load_sem.at[2])
@@ -1267,7 +1117,7 @@
         sums.append(level)
     sums = jnp.concatenate(sums + [jnp.zeros((128 - slots, 2 * seq_len), f32)], axis=0)
     d_rel = lax.dot_general(
-        onehot[...],
+        onehot_rows(bucket_ref[...]),
         sums,
         (((1,), (1,)), ((), ())),
         precision=highest,
@@ -1284,7 +1134,7 @@
         copy.wait()
 
 
-def attend_back(dn, middle, cot, gain, proj_all, own, qkv, probs, norm, qkv_low, onehot, ff_pieces):
+def attend_back(dn, middle, cot, gain, proj_all, own, qkv, probs, norm, qkv_low, bucket, ff_pieces):
     count = lax.axis_size("mp")
     data_count = lax.axis_size("dp")
     seq_len = qkv.shape[0]
@@ -1308,7 +1158,6 @@
         ((2, slots, BLOCK, seq_len), f32),
         (norm.shape, low),
         (qkv_low.shape, low),
-        (onehot.shape, f32),
         ((count, block_len, lanes), low),
         ((seq_len, lanes), low),
         ((slots, BLOCK, 2 * seq_len), f32),
@@ -1321,7 +1170,7 @@
     ]
     return pl.pallas_call(
         functools.partial(attend_back_kernel, data_count, count, slots),
-        in_specs=[far] * 3 + [near] + [far] * 8,
+        in_specs=[far] * 3 + [near] + [far] * 6 + [near, far],
         out_specs=[far] * 5,
         out_shape=[
             jax.ShapeDtypeStruct((block_len, width), f32),
@@ -1346,15 +1195,486 @@
             flops=16 * slots * seq_len * seq_len * HD, bytes_accessed=140 << 20, transcendentals=0
         ),
         name="attend_back",
-    )(dn, middle, cot, gain, proj_all, own, qkv, probs, norm, qkv_low, onehot, ff_pieces)
-
-
-def to_owners(rows_of_slots):
+    )(dn, middle, cot, gain, proj_all, own, qkv, probs, norm, qkv_low, bucket, ff_pieces)
+
+
+def onehot_rows(bucket):
+    rows = lax.broadcasted_iota(jnp.int32, (BUCKETS, bucket.shape[1]), 0)
+    return jnp.where(rows == bucket, 1.0, 0.0)
+
+
+def front_kernel(
+    data_count,
+    count,
+    slots,
+    x_hbm,
+    cot_hbm,
+    query_hbm,
+    key_hbm,
+    value_hbm,
+    out_hbm,
+    gate_hbm,
+    up_hbm,
+    down_hbm,
+    segments_ref,
+    bucket_ref,
+    rel_ref,
+    attn_gain_ref,
+    ff_gain_ref,
+    norm_far,
+    cot_far,
+    own_cot_far,
+    qkv_far,
+    probs_far,
+    own_far,
+    middle_far,
+    normed_far,
+    proj_far,
+    qkv_low_far,
+    gate_up_far,
+    down_far,
+    squares_ref,
+    x_in,
+    cot_in,
+    x,
+    norm,
+    cot,
+    thin,
+    wide,
+    gate_low,
+    up_low,
+    down_low,
+    blank,
+    proj,
+    qkv_low,
+    qkv,
+    tilt,
+    seg_col,
+    probs,
+    mixed,
+    own,
+    normed,
+    load_sem,
+    save_sem,
+    probs_sem,
+    norm_send,
+    norm_recv,
+    cot_send,
+    cot_recv,
+    cross_send,
+    cross_recv,
+    side_send,
+    side_recv,
+    mix_send,
+    mix_recv,
+):
+    place = lax.axis_index("mp")
+    me = lax.axis_index("dp")
+    last = count - 1
+    f32, low = jnp.float32, jnp.bfloat16
+    block_len, width = x.shape
+    seq_len = count * block_len
+    lanes = slots * HD
+    padded = proj.shape[0]
+    height = padded // data_count
+    units = gate_low.shape[1]
+    mesh_id = pl.DeviceIdType.MESH
+    others = [(place + k) % count for k in range(1, count)]
+    peers = [(me + k) % data_count for k in range(1, data_count)]
+
+    def load(k, from_ref, to_ref):
+        copy = pltpu.make_async_copy(from_ref, to_ref, load_sem.at[k])
+        copy.start()
+        return copy
+
+    load_x = load(0, x_hbm, x_in)
+    load_thin = [
+        load(1 + k, ref, thin.at[k])
+        for k, ref in enumerate((out_hbm, query_hbm, key_hbm, value_hbm))
+    ]
+    load_cot = load(5, cot_hbm, cot_in)
+    load_gate = load(6, gate_hbm, wide.at[0])
+    load_up = load(7, up_hbm, wide.at[1])
+    greet([(me, other) for other in others] + [(peer, place) for peer in peers])
+
+    saves = []
+
+    def save(from_ref, to_ref):
+        copy = pltpu.make_async_copy(from_ref, to_ref, save_sem.at[len(saves)])
+        copy.start()
+        saves.append(copy)
+
+    sent = []
+
+    def start(copy):
+        copy.start()
+        sent.append(copy)
+
+    def pass_block(buffer, sems, block, side, slot):
+        return pltpu.make_async_remote_copy(
+            src_ref=buffer.at[block],
+            dst_ref=buffer.at[block],
+            send_sem=sems[0].at[slot],
+            recv_sem=sems[1].at[block],
+            device_id=(me, place + side),
+            device_id_type=mesh_id,
+        )
+
+    def inside(block):
+        return (block >= 0) & (block <= last)
+
+    norm_sems = (norm_send, norm_recv)
+    cot_sems = (cot_send, cot_recv)
+
+    def take(buffer, sems, distance):
+        for side in (1, -1):
+            other = place + side * distance
+
+            @pl.when(inside(other))
+            def _():
+                pass_block(buffer, sems, other, side, other).wait_recv()
+
+                @pl.when(inside(place - side))
+                def _():
+                    pass_block(buffer, sems, other, -side, other).start()
+
+    def send_own(buffer, sems, side):
+        return pass_block(buffer, sems, place, side, count + (side + 1) // 2)
+
+    def cot_may_go(distance):
+        for side in (1, -1):
+            behind = place if side == 1 else last - place
+
+            @pl.when((behind == distance) & inside(place + side))
+            def _():
+                if distance == 0:
+                    send_own(norm, norm_sems, side).wait_send()
+                else:
+                    far_end = 0 if side == 1 else last
+                    pass_block(norm, norm_sems, far_end, side, far_end).wait_send()
+                send_own(cot, cot_sems, side).start()
+
+    between = inside(place - 1) & inside(place + 1)
+
+    load_x.wait()
+    x[...] = x_in[...].T.astype(f32)
+    norm[place] = rms_norm(x[...], attn_gain_ref[...].reshape(1, width)).astype(low)
+    for side in (1, -1):
+
+        @pl.when(inside(place + side))
+        def _():
+            send_own(norm, norm_sems, side).start()
+
+    load_cot.wait()
+    cot[place] = cot_in[...].T
+    save(cot.at[place], own_cot_far)
+
+    lane = lax.broadcasted_iota(jnp.int32, (1, lanes), 1)
+    slot_of = place * slots + lane // HD
+    lane_mask = jnp.where((slot_of < 5) | (slot_of == 6), 1.0, 0.0)
+    for copy in load_thin:
+        copy.wait()
+
+    def lanes_of(who):
+        return pl.ds(pl.multiple_of(who * lanes, lanes), lanes)
+
+    def rows_of(who):
+        return pl.ds(pl.multiple_of(who * height, height), height)
+
+    proj[width:, lanes_of(place)] = jnp.zeros((padded - width, lanes), low)
+    qkv_low[width:] = jnp.zeros((padded - width, 3 * lanes), low)
+    blank[...] = jnp.zeros_like(blank)
+    column = lax.broadcasted_iota(jnp.int32, (1, 128), 1)
+    squares = jnp.zeros((1, 128), f32)
+
+    def square_of(values, at):
+        return jnp.where(column == at, total(total(values * values, 1), 0), 0.0)
+
+    masked = (thin[0] * lane_mask).astype(low)
+    proj[:width, lanes_of(place)] = masked
+
+    def proj_copy(src, dst, sems, send_slot, recv_slot, device):
+        return pltpu.make_async_remote_copy(
+            src_ref=src,
+            dst_ref=dst,
+            send_sem=sems[0].at[send_slot],
+            recv_sem=sems[1].at[recv_slot],
+            device_id=device,
+            device_id_type=mesh_id,
+        )
+
+    cross, aside = (cross_send, cross_recv), (side_send, side_recv)
+    for k, other in enumerate(others):
+        view = proj.at[rows_of(me), lanes_of(place)]
+        start(proj_copy(view, view, cross, k, count - 2 - k, (me, other)))
+    for k in range(3):
+        qkv_low[:width, k * lanes : (k + 1) * lanes] = (thin[1 + k] * lane_mask).astype(low)
+        squares = squares + square_of(thin[1 + k], k)
+    squares = squares + square_of(thin[0], 6) + square_of(rel_ref[...], 3)
+    save(qkv_low, qkv_low_far)
+
+    onehot = onehot_rows(bucket_ref[...])
+    vector = lax.dot_general(
+        rel_ref[...],
+        onehot,
+        (((0,), (0,)), ((), ())),
+        precision=highest,
+        preferred_element_type=f32,
+    )
+    for slot in range(slots):
+        spread = jnp.broadcast_to(vector[slot : slot + 1, :], (BLOCK, 2 * seq_len))
+        tilt[slot] = pltpu.roll(spread, 2 * seq_len - BLOCK + 1, 1, stride=1, stride_axis=0)
+    seg_row = segments_ref[...].astype(f32)
+    seg_col[...] = jnp.broadcast_to(seg_row, (128, seq_len)).T
+
+    arrivals = []
+    for k, other in enumerate(others):
+        view = proj.at[rows_of(me), lanes_of(other)]
+        proj_copy(view, view, cross, k, k, (me, other)).wait_recv()
+        at = k * (data_count - 1)
+        for j, peer in enumerate(peers):
+            start(proj_copy(view, view, aside, at + j, at + data_count - 2 - j, (peer, place)))
+            come = proj.at[rows_of(peer), lanes_of(other)]
+            arrivals.append(proj_copy(come, come, aside, at + j, at + j, (peer, place)))
+
+    def own_rows(who):
+        return pl.ds(pl.multiple_of(who * block_len, block_len), block_len)
+
+    def project(block):
+        qkv[own_rows(block)] = product(norm[block], qkv_low[:width]).astype(low)
+
+    def project_at(distance):
+        for side in (1, -1):
+            other = place + side * distance
+
+            @pl.when(inside(other))
+            def _():
+                project(other)
+
+    project(place)
+    load_gate.wait()
+    gate_low[...] = wide[0].astype(low)
+    squares = squares + square_of(wide[0], 4)
+    load_down = load(6, down_hbm, wide.at[0])
+    rows_used = pl.ds(0, width)
+    save(gate_low, gate_up_far.at[rows_used, pl.ds(0, units)])
+    load_up.wait()
+    up_low[...] = wide[1].astype(low)
+    squares = squares + square_of(wide[1], 5)
+    save(up_low, gate_up_far.at[rows_used, pl.ds(units, units)])
+    save(blank, gate_up_far.at[pl.ds(width, padded - width)])
+    take(norm, norm_sems, 1)
+    cot_may_go(0)
+    project_at(1)
+    load_down.wait()
+    down_low[...] = wide[0].astype(low)
+    squares = squares + square_of(wide[0], 7)
+    save(down_low, down_far)
+    squares_ref[...] = squares
+    for distance in range(2, count):
+        take(norm, norm_sems, distance)
+        cot_may_go(distance - 1)
+        project_at(distance)
+    save(qkv, qkv_far)
+    save(norm, norm_far)
+
+    @pl.when(between)
+    def _():
+        take(cot, cot_sems, 1)
+
+    steps = seq_len // BLOCK
+    per = block_len // BLOCK
+    table = [order[::-1] for order in turn_order(count)]
+
+    def store_probs(t, block):
+        rows = pl.ds(pl.multiple_of(block * BLOCK, BLOCK), BLOCK)
+        return pltpu.make_async_copy(probs.at[t % 2], probs_far.at[:, rows], probs_sem.at[t % 2])
+
+    def mix_copy(owner):
+        return pltpu.make_async_remote_copy(
+            src_ref=mixed.at[own_rows(owner)],
+            dst_ref=own.at[:, lanes_of(place)],
+            send_sem=mix_send.at[owner],
+            recv_sem=mix_recv.at[place],
+            device_id=(me, owner),
+            device_id_type=mesh_id,
+        )
+
+    def attend_block(t, carry):
+        owner = look_up(table, place, t // per)
+        block = owner * per + t % per
+        rows = pl.ds(pl.multiple_of(block * BLOCK, BLOCK), BLOCK)
+        window = pl.ds(pl.multiple_of((steps - 1 - block) * BLOCK, BLOCK), seq_len)
+        same_doc = seg_col[rows, 0:1] == seg_row
+        queries = qkv[rows, 0:lanes]
+        keys = qkv[:, lanes : 2 * lanes]
+        values = qkv[:, 2 * lanes : 3 * lanes]
+        result = jnp.zeros((BLOCK, lanes), f32)
+
+        @pl.when(t >= 2)
+        def _():
+            store_probs(t, block).wait()
+
+        for slot in range(slots):
+            scores = right_inner(slot_lanes(queries, slot), keys) + tilt[slot, :, window]
+            scores = jnp.where(same_doc, scores, -1e30)
+            peak = jnp.max(scores, axis=-1, keepdims=True)
+            raised = jnp.exp(scores - peak)
+            weight = raised * (1.0 / jnp.sum(raised, axis=-1, keepdims=True))
+            probs[t % 2, slot] = weight
+            result = result + slot_lanes(product(weight.astype(low), values), slot)
+        store_probs(t, block).start()
+        mixed[rows] = result.astype(low)
+
+        @pl.when((t % per == per - 1) & (owner != place))
+        def _():
+            mix_copy(owner).start()
+
+        return carry
+
+    lax.fori_loop(0, steps, attend_block, 0)
+    own[:, lanes_of(place)] = mixed[own_rows(place)]
+
+    @pl.when(between)
+    def _():
+        for distance in range(2, count):
+            take(cot, cot_sems, distance)
+
+    for arrival in arrivals:
+        arrival.wait_recv()
+    save(proj, proj_far)
+    for k, other in enumerate(others):
+        pltpu.make_async_remote_copy(
+            src_ref=mixed.at[own_rows(other)],
+            dst_ref=own.at[:, lanes_of(other)],
+            send_sem=mix_send.at[other],
+            recv_sem=mix_recv.at[other],
+            device_id=(me, other),
+            device_id_type=mesh_id,
+        ).wait_recv()
+    save(own, own_far)
+    x[...] = x[...] + right_inner(own[...], proj[:width])
+    save(x, middle_far)
+    normed[...] = rms_norm(x[...], ff_gain_ref[...].reshape(1, width)).astype(low)
+    save(normed, normed_far)
+
+    @pl.when(jnp.logical_not(between))
+    def _():
+        for distance in range(1, count):
+            take(cot, cot_sems, distance)
+
+    save(cot, cot_far)
+    for t in (0, 1):
+        store_probs(t, 0).wait()
+    for copy in saves:
+        copy.wait()
+    for copy in sent:
+        copy.wait_send()
+    for k, other in enumerate(others):
+        mix_copy(other).wait_send()
+    for buffer, sems in ((norm, norm_sems), (cot, cot_sems)):
+        for side in (1, -1):
+            behind = place if side == 1 else last - place
+            unwaited = behind > 0 if buffer is norm else behind >= 0
+
+            @pl.when(unwaited & inside(place + side))
+            def _():
+                send_own(buffer, sems, side).wait_send()
+
+        for block in range(1, last) if buffer is norm else range(count):
+
+            @pl.when((block != place) & between)
+            def _():
+                pass_block(buffer, sems, block, 1, block).wait_send()
+
+
+def front(x, cot, weights, segments, bucket, rel_bias, attn_gain, ff_gain):
     count = lax.axis_size("mp")
-    seq_len, lanes = rows_of_slots.shape
-    pieces = rows_of_slots.reshape(count, seq_len // count, lanes)
-    pieces = lax.all_to_all(pieces, "mp", split_axis=0, concat_axis=0)
-    return pieces.transpose(1, 0, 2).reshape(seq_len // count, count * lanes)
+    data_count = lax.axis_size("dp")
+    query, key, value, out, gate, up, down = weights
+    width, block_len = x.shape
+    lanes = query.shape[1]
+    slots = lanes // HD
+    units = gate.shape[1]
+    seq_len = count * block_len
+    piece = 16 * data_count
+    padded = (width + piece - 1) // piece * piece
+    low, f32 = jnp.bfloat16, jnp.float32
+    far = pl.BlockSpec(memory_space=pltpu.HBM)
+    near = pl.BlockSpec(memory_space=pltpu.VMEM)
+    dma = pltpu.SemaphoreType.DMA
+    outs = [
+        ((count, block_len, width), low),
+        ((count, block_len, width), low),
+        ((block_len, width), low),
+        ((seq_len, 3 * lanes), low),
+        ((slots, seq_len, seq_len), f32),
+        ((block_len, count * lanes), low),
+        ((block_len, width), f32),
+        ((block_len, width), low),
+        ((padded, count * lanes), low),
+        ((padded, 3 * lanes), low),
+        ((padded, 2 * units), low),
+        ((width, units), low),
+        ((1, 128), f32),
+    ]
+    scratch = [
+        ((width, block_len), low),
+        ((width, block_len), low),
+        ((block_len, width), f32),
+        ((count, block_len, width), low),
+        ((count, block_len, width), low),
+        ((4, width, lanes), f32),
+        ((2, width, units), f32),
+        ((width, units), low),
+        ((width, units), low),
+        ((width, units), low),
+        ((padded - width, 2 * units), low),
+        ((padded, count * lanes), low),
+        ((padded, 3 * lanes), low),
+        ((seq_len, 3 * lanes), low),
+        ((slots, BLOCK, 2 * seq_len), f32),
+        ((seq_len, 128), f32),
+        ((2, slots, BLOCK, seq_len), f32),
+        ((seq_len, lanes), low),
+        ((block_len, count * lanes), low),
+        ((block_len, width), low),
+    ]
+    sides = (count - 1) * (data_count - 1)
+    return pl.pallas_call(
+        functools.partial(front_kernel, data_count, count, slots),
+        in_specs=[far] * 9 + [near] * 5,
+        out_specs=[far] * 12 + [near],
+        out_shape=[jax.ShapeDtypeStruct(shape, dtype) for shape, dtype in outs],
+        scratch_shapes=[pltpu.VMEM(shape, dtype) for shape, dtype in scratch]
+        + [
+            dma((8,)),
+            dma((16,)),
+            dma((2,)),
+            dma((count + 2,)),
+            dma((count,)),
+            dma((count + 2,)),
+            dma((count,)),
+            dma((count - 1,)),
+            dma((count - 1,)),
+            dma((sides,)),
+            dma((sides,)),
+            dma((count,)),
+            dma((count,)),
+        ],
+        compiler_params=pltpu.CompilerParams(
+            collective_id=0, has_side_effects=True, vmem_limit_bytes=60 << 20
+        ),
+        cost_estimate=pl.CostEstimate(
+            flops=8 * slots * seq_len * seq_len * HD,
+            bytes_accessed=300 << 20,
+            transcendentals=slots * seq_len * seq_len,
+        ),
+        name="front",
+    )(
+        x, cot, query, key, value, out, gate, up, down,
+        segments, bucket, rel_bias, attn_gain, ff_gain,
+    )
 
 
 def local(
@@ -1373,112 +1693,58 @@
     down_weight,
     cotangent,
 ):
-    _, local_len, model_width = layer_in.shape
-    seq_len = segment_ids.shape[1]
-    lane_width = query_weight.shape[1]
-    slots_here = lane_width // HD
-    ff_width = gate_weight.shape[1]
-    tensor_index = lax.axis_index("mp")
-    tensor_count = lax.axis_size("mp")
-    data_index = lax.axis_index("dp")
-    data_count = lax.axis_size("dp")
+    model_width = layer_in.shape[2]
+    slots_here = rel_bias.shape[1]
     layer_in = layer_in[0]
-    cotangent = cotangent[0]
-    slot_ids = tensor_index * slots_here + jnp.arange(slots_here)
-    slot_valid = ((slot_ids < 5) | (slot_ids == 6)).astype(jnp.float32)
-    lane_mask = jnp.repeat(slot_valid, HD)
-    qkv_low = (
-        jnp.concatenate([query_weight, key_weight, value_weight], axis=1) * jnp.tile(lane_mask, 3)
-    ).astype(jnp.bfloat16)
-    proj_low = (out_weight * lane_mask[:, None]).astype(jnp.bfloat16)
-    piece = 16 * data_count
-    padded = (model_width + piece - 1) // piece * piece
-    extra = padded - model_width
-    gate_up_low = jnp.concatenate([gate_weight, up_weight], axis=1).astype(jnp.bfloat16)
-    gate_up_low = jnp.pad(gate_up_low, ((0, extra), (0, 0)))
-    squares = [
-        jnp.sum(w * w)
-        for w in (
-            query_weight,
-            key_weight,
-            value_weight,
-            rel_bias,
-            gate_weight,
-            up_weight,
-            out_weight,
-            down_weight,
-        )
-    ]
-    squares = jnp.pad(jnp.stack(squares), (0, 120)).reshape(1, 128)
     down_turned = down_weight.T
     out_turned = out_weight.T
-    down_low = down_turned.astype(jnp.bfloat16)
-    onehot = (bucket_table[:, None] == jnp.arange(BUCKETS)[None, :]).astype(jnp.float32)
-    onehot = jnp.pad(onehot, ((0, 1), (0, 0)))
-    onehot_turned = onehot.T
-    qkv_padded = jnp.pad(qkv_low, ((0, extra), (0, 0)))
-    vector = lax.dot_general(
-        rel_bias,
-        onehot,
-        (((0,), (1,)), ((), ())),
-        precision=highest,
-        preferred_element_type=jnp.float32,
-    )
-    residual_in = layer_in.astype(jnp.float32)
-    normed_local = rms_norm(residual_in, attn_gain).astype(jnp.bfloat16)
-    flat_norm = lax.all_gather(normed_local, "mp", axis=0, tiled=True)
-    proj_all = gather_proj(proj_low)
+    bucket = jnp.pad(bucket_table, (0, 1)).reshape(1, -1)
     (
         flat_norm,
-        late_cot,
+        flat_cot,
+        own_cot,
+        qkv,
+        probs,
+        own_attended,
+        middle,
+        normed_ff_local,
         proj_all,
         qkv_low,
         gate_up_low,
         down_low,
-        vector,
         squares,
-        onehot_turned,
-        qkv_padded,
-    ) = lax.optimization_barrier(
-        (
-            flat_norm,
-            cotangent,
-            proj_all,
-            qkv_low,
-            gate_up_low,
-            down_low,
-            vector,
-            squares,
-            onehot_turned,
-            qkv_padded,
-        )
+    ) = front(
+        layer_in.T,
+        cotangent[0].T,
+        (query_weight, key_weight, value_weight, out_turned, gate_weight, up_weight, down_turned),
+        segment_ids,
+        bucket,
+        rel_bias,
+        attn_gain,
+        ff_gain,
     )
-    flat_cot = lax.all_gather(late_cot, "mp", axis=0, tiled=True)
-    qkv = product(flat_norm, qkv_low).astype(jnp.bfloat16)
-    attended, probs = attend(qkv, segment_ids.reshape(seq_len, 1), segment_ids, vector)
-    own_attended = to_owners(attended)
-    middle = residual_in + product(own_attended, proj_all)
-    normed_ff_local = rms_norm(middle, ff_gain).astype(jnp.bfloat16)
+    flat_norm = flat_norm.reshape(-1, model_width)
+    residual_in = layer_in.astype(jnp.float32)
     out_terms, dn_ff, ff_pieces = feed_forward(normed_ff_local, flat_cot, gate_up_low, down_low)
     d_middle, dn_attn_terms, d_qkv_w, d_out_w, ff_grads = attend_back(
         dn_ff,
         middle,
-        cotangent,
-        ff_gain.reshape(1, model_width),
+        own_cot,
+        ff_gain,
         proj_all,
         own_attended,
         qkv,
         probs,
         flat_norm,
-        qkv_padded,
-        onehot_turned,
+        qkv_low,
+        bucket,
         ff_pieces,
     )
     ff_branch = lax.psum_scatter(out_terms, "mp", scatter_dimension=0, tiled=True)
     layer_out = (middle + ff_branch.astype(jnp.float32)).astype(jnp.bfloat16)
     dn_attn = lax.psum_scatter(dn_attn_terms, "mp", scatter_dimension=0, tiled=True)
     *grads, shared, own, tall = sum_weights(
-        ff_grads, d_qkv_w, d_out_w, qkv_padded, gate_up_low, squares, model_width
+        ff_grads, d_qkv_w, d_out_w, qkv_low, gate_up_low, squares, model_width
     )
     weights = (
         gate_weight,

time: 435 us -> 419 us (0.963)
  the two profiles are of different devices: /device:TPU:11 before, /device:TPU:9 now
where the time goes in v4:
time: 419 us; the launch traced here: 411 us
  Pallas kernels  382 us (91%)
  between operations  14.6 us (3%)
  local copies, waits for them, and re-layouts  8.86 us (2%)
  other arithmetic  5.12 us (1%)
    pallas_call x1, Pallas kernels, front(): pl.pallas_call(functools.partial(front_kernel, data_count, count, slots),...  118 us
    pallas_call x1, Pallas kernels, feed_forward(): pl.pallas_call(functools.partial(feed_forward_kernel, data_count, count,...  106 us
    pallas_call x1, Pallas kernels, sum_weights(): pl.pallas_call(functools.partial(sum_weights_kernel, data_count, count, m...  74.9 us
    pallas_call x1, Pallas kernels, attend_back(): pl.pallas_call(functools.partial(attend_back_kernel, data_count, count, s...  61.4 us
    pallas_call x1, Pallas kernels, update(): pl.pallas_call(functools.partial(update_kernel, tensor_count), grid=(chun...  21.6 us
  transfers between devices with their start and end apart: 2, of which 0 were waited for; matrix products, arithmetic and copies ran while one was open for 1% of the time, Pallas kernels for 38%

profile of v4, /device:TPU:9, one launch (start us, length us, event | category | flops | bytes accessed | tf_op | source)
XLA Modules:
  0.0 410.9 jit_solution(2290635731255474438)
XLA Ops:
  7.2 0.0 reduce-scatter.3.cloned.1.call-start
  7.2 1.4 copy.46.rel_ref.refs_13_
  8.6 1.3 pad.4
  9.9 117.9 %front.1 = (bf16[4,256,1472]{2,1,0:T(8,128)(2,1)}, bf16[4,256,1472]{2,1,0:T(8,128)(2,1)}, bf16[256,1472]{1,0:T(8,128)(2,1)}, bf16[1024,384]{1,0:T(8,128)(2,1)}, ...) custom-call(bf16[1472,256]{1,0:T(8,128)(2,1)} %bitcast.28, ...), custom_call_target="tpu_custom_call" | custom-call | flops 1073741824 | bytes 314572800 | tf_op jit(solution)/shard_map/front/pallas_call | solution.py:1644
  127.8 106.3 %feed_forward.1 = (bf16[4,256,1472]{2,1,0:T(8,128)(2,1)}, f32[256,1472]{1,0:T(8,128)}, bf16[3,192,896]{2,1,0:T(8,128)(2,1)}) custom-call(bf16[256,1472]{1,0:T(8,128)(2,1)} %get-tuple-element.88.normed_hbm, bf16[4,256,1472]{2,1,0:T(8,128)(2,1)} %get-tuple-element.89.cot_hbm, bf16[1536,1792]{1,0:T(8,128)(2,1)} %get-tuple-element.90.gate_up_hbm.refs_4_, ...), custom_call_target="tpu_custom_call" | custom-call | flops 24310185984 | bytes 24870912 | tf_op jit(solution)/shard_map/feed_forward/pallas_call | solution.py:849
  234.1 0.0 reduce-scatter.3.cloned.1.call-update
  234.1 0.0 reduce-scatter.5.cloned.1.call-start
  234.2 61.4 %attend_back.1 = (f32[256,1472]{1,0:T(8,128)}, bf16[1024,1472]{1,0:T(8,128)(2,1)}, bf16[1536,384]{1,0:T(8,128)(2,1)}, bf16[1536,512]{1,0:T(8,128)(2,1)}, bf16[3,1536,896]{2,1,0:T(8,128)(2,1)}) custom-call(f32[256,1472]{1,0:T(8,128)} %get-tuple-element.93.dn_hbm, f32[256,1472]{1,0:T(8,128)} %get-tuple-element.87.middle_hbm, ...), custom_call_target="tpu_custom_call" | custom-call | flops 2147483648 | bytes 146800640 | tf_op jit(solution)/shard_map/attend_back/pallas_call | solution.py:1171
  295.6 0.0 copy-start.2
  295.6 0.0 copy-start.3
  295.6 0.0 copy-start.4
  295.6 0.0 reduce-scatter.5.cloned.1.call-update
  295.6 1.1 copy-done.2
  296.7 0.3 copy.44
  297.0 0.0 copy-done.3
  297.0 0.6 broadcast_in_dim.13.refs_14_
  297.6 0.0 copy-done.4
  297.6 0.6 reshape.95.refs_15_
  298.2 74.9 %sum_weights.1 = (bf16[1536,896]{1,0:T(8,128)(2,1)}, bf16[1536,896]{1,0:T(8,128)(2,1)}, bf16[1536,896]{1,0:T(8,128)(2,1)}, bf16[1536,384]{1,0:T(8,128)(2,1)}, bf...) custom-call(bf16[3,1536,896]{2,1,0:T(8,128)(2,1)} %get-tuple-element.104.refs_0_, ...), custom_call_target="tpu_custom_call" | custom-call | flops 1376256 | bytes 209715200 | tf_op jit(solution)/shard_map/sum_weights/pallas_call | solution.py:376
  373.1 0.0 copy-start
  373.1 21.6 %update.1 = (f32[1472,896]{1,0:T(8,128)}, f32[1472,896]{1,0:T(8,128)}, f32[1472,896]{1,0:T(8,128)}, f32[1472,128]{1,0:T(8,128)}, f32[1472,128]{1,0:T(8,128)}, /*...) custom-call(bf16[1536,896]{1,0:T(8,128)(2,1)} %get-tuple-element.108, ...), custom_call_target="tpu_custom_call" | custom-call | flops 52756480 | bytes 47480832 | tf_op jit(solution)/shard_map/update/pallas_call | solution.py:505
  394.8 1.4 copy.50
  396.1 0.2 fusion.7
  396.4 0.0 reduce-scatter.3.cloned.1.call-done
  396.4 0.0 copy-done
  396.4 1.3 fusion.8
  397.7 1.1 copy.48
  398.9 0.0 reduce-scatter.5.cloned.1.call-done
  398.9 0.0 copy-start.1
  398.9 1.6 fusion.2
  400.5 0.0 copy-done.1
  400.5 1.9 fusion.9
  402.4 1.1 copy.49
  (2 shorter events, 0.0 us)
Async XLA Ops:
  7.2 389.2 %reduce-scatter.3.cloned.1.call-start = ((), (), s32[]{:S(2)}) async-start(), calls=%async_computation.2 | async-start | bytes 3932160 | tf_op jit(solution)/shard_map/reduce_scatter | solution.py:1743
  234.1 164.7 %reduce-scatter.5.cloned.1.call-start = ((), (), s32[]{:S(2)}) async-start(), calls=%async_computation.3 | async-start | bytes 3932160 | tf_op jit(solution)/shard_map/reduce_scatter | solution.py:1745
  295.6 1.1 copy-start.2
  295.6 1.4 copy-start.3
  295.6 2.0 copy-start.4
  373.1 23.3 %copy-start = (f32[256,1472]{1,0:T(8,128)S(1)}, f32[256,1472]{1,0:T(8,128)}, u32[]{:S(2)}) copy-start(f32[256,1472]{1,0:T(8,128)} %get-tuple-element.87.middle_hbm) | copy-start | bytes 4521988
  398.9 1.7 copy-start.1
Sparse Core Ops, SparseCore 0:
  234.2 68.1 reduce-scatter.2
  304.7 74.0 reduce-scatter.4
